TPU v7x, 128 devices: a whole 4x4x4 slice. The times are simulated.
128 devices in a mesh: grp: 8 (over y_hi, z), gene: 16 (over y_lo, x, core).
Axes of the slice: x: 4, y: 4 (y_hi: 2, y_lo: 2; y = y_hi * 2 + y_lo), z: 4, core: 2. Of those that a mesh axis runs over, the one named last changes fastest.
Arguments:
- counts: int32 [2048, 15360], P('grp', 'gene'), may hold values from 0 to 12
- panels: int32 [15360], P('gene'), may hold values from 0 to 63
- membership: int32 [8, 256], P('grp'), may hold values from 0 to 3, never falling along the last dimension, each value on 1 to 128 neighbouring positions
- w_proj: bfloat16 [15360, 6400], P('gene'), may hold values from -0.0234375 to 0.0234375
- w_qkv_within: bfloat16 [1600, 32, 150], P(None, 'gene'), may hold values from -0.15625 to 0.15625
- w_out_within: bfloat16 [32, 50, 1600], P('gene'), may hold values from -0.4375 to 0.4375
- w_qkv_cross: bfloat16 [1600, 32, 150], P(None, 'gene'), may hold values from -0.15625 to 0.15625
- w_out_cross: bfloat16 [32, 50, 1600], P('gene'), may hold values from -0.4375 to 0.4375
- w_mean: bfloat16 [1600, 15360], P(None, 'gene'), may hold values from -0.25 to 0.25
- w_disp: bfloat16 [1600, 64], replicated, may hold values from -0.25 to 0.25
Outputs:
- cell_loss: float32 [2048], P('grp')
- grad_mean: float32 [1600, 15360], P('grp', 'gene')
- grad_disp: float32 [1600, 64], replicated
Inputs may be any that keep to these rules, and one draw needn't show every extreme that they name: `membership`: group numbers never fall along a row; a group has at most 128 cells.
All inputs are finite; a program needn't handle non-finite values.
Results may differ from a plain program's by a relative error of at most 0.00055.
Values may be sent and summed in bfloat16 or wider, within the bound.
A program may use at most 128 MiB of HBM per device.

v0:
```python
import jax
import jax.numpy as jnp
from jax import lax
from jax.sharding import PartitionSpec as P

EPS = 1e-06
FLOOR = 0.3
TARGET = 10000.0
DISP_BASE = 0.5


def rms_rows(values):
    return values * lax.rsqrt(jnp.mean(values * values, axis=-1, keepdims=True) + EPS)


def head_norm(values):
    return values * lax.rsqrt(jnp.maximum(jnp.mean(values * values, axis=-1, keepdims=True), FLOOR))


def split_heads(qkv, heads):
    qkv = qkv.reshape(qkv.shape[0], heads, 3, -1)
    query = head_norm(qkv[:, :, 0]).astype(jnp.bfloat16)
    keys = head_norm(qkv[:, :, 1]).astype(jnp.bfloat16)
    values = qkv[:, :, 2].astype(jnp.bfloat16)
    return (query, keys, values)


def within_cells(query, keys, values, modules):
    rows, heads, width = query.shape
    cells = rows // modules
    q_all = query.reshape(cells, modules, heads, width)
    k_all = keys.reshape(cells, modules, heads, width)
    v_all = values.reshape(cells, modules, heads, width)
    scores = jnp.einsum(
        "cmhd,cnhd->chmn", q_all, k_all, preferred_element_type=jnp.float32
    ) * width ** (-0.5)
    weights = jnp.exp(scores)
    probs = (weights / jnp.sum(weights, axis=-1, keepdims=True)).astype(jnp.bfloat16)
    mixed = jnp.einsum("chmn,cnhd->cmhd", probs, v_all, preferred_element_type=jnp.float32)
    return mixed.astype(jnp.bfloat16).reshape(rows, heads * width)


def across_cells(query, keys, values, groups, modules):
    rows, heads, width = query.shape
    cells = rows // modules
    q_all = query.reshape(cells, modules, heads, width)
    k_all = keys.reshape(cells, modules, heads, width)
    v_all = values.reshape(cells, modules, heads, width)
    scores = jnp.einsum(
        "cmhd,nmhd->mhcn", q_all, k_all, preferred_element_type=jnp.float32
    ) * width ** (-0.5)
    same = groups[:, None] == groups[None, :]
    weights = jnp.where(same[None, None], jnp.exp(scores), 0.0)
    probs = (weights / jnp.sum(weights, axis=-1, keepdims=True)).astype(jnp.bfloat16)
    mixed = jnp.einsum("mhcn,nmhd->cmhd", probs, v_all, preferred_element_type=jnp.float32)
    return mixed.astype(jnp.bfloat16).reshape(rows, heads * width)


def nb_terms(observed, rate, theta):
    total = theta + rate
    log_total = jnp.log(total)
    nll = -(
        lax.lgamma(observed + theta)
        - lax.lgamma(theta)
        - lax.lgamma(observed + 1.0)
        + theta * (jnp.log(theta) - log_total)
        + observed * (jnp.log(rate) - log_total)
    )
    d_rate = (theta + observed) / total - observed / rate
    d_theta = -(
        lax.digamma(observed + theta)
        - lax.digamma(theta)
        + jnp.log(theta)
        + 1.0
        - log_total
        - (theta + observed) / total
    )
    return (nll, d_rate, d_theta)


def shards(
    counts,
    panels,
    membership,
    w_proj,
    w_qkv_within,
    w_out_within,
    w_qkv_cross,
    w_out_cross,
    w_mean,
    w_disp,
):
    cells, genes_here = counts.shape
    width = w_qkv_within.shape[0]
    heads_here = w_qkv_within.shape[1]
    modules = w_proj.shape[1] // width
    gene_count = lax.axis_size("gene")
    genes_all = genes_here * gene_count
    rows = cells * modules
    share = rows // gene_count
    cell_share = cells // gene_count
    first = lax.axis_index("gene") * share
    observed = counts.astype(jnp.float32)
    library = 1.0 + lax.psum(jnp.sum(observed, axis=1), "gene")
    scaled = jnp.log1p(observed * (TARGET / library)[:, None]).astype(jnp.bfloat16)
    partial_value = jnp.dot(scaled, w_proj, preferred_element_type=jnp.float32).reshape(rows, width)
    tokens = lax.psum(partial_value, "gene")
    normed = rms_rows(tokens).astype(jnp.bfloat16)
    resid = lax.dynamic_slice_in_dim(tokens, first, share, 0)
    flat_within = w_qkv_within.reshape(width, -1)
    query, keys, values = split_heads(
        jnp.dot(normed, flat_within, preferred_element_type=jnp.float32), heads_here
    )
    mixed = within_cells(query, keys, values, modules)
    out_within = w_out_within.reshape(-1, width)
    block = mixed
    resid = resid + lax.psum_scatter(
        jnp.dot(block, out_within, preferred_element_type=jnp.float32),
        "gene",
        scatter_dimension=0,
        tiled=True,
    )
    flat_cross = w_qkv_cross.reshape(width, -1)
    qkv_cross = jnp.dot(
        lax.all_gather(rms_rows(resid).astype(jnp.bfloat16), "gene", axis=0, tiled=True),
        flat_cross,
        preferred_element_type=jnp.float32,
    )
    query, keys, values = split_heads(qkv_cross, heads_here)
    mixed = across_cells(query, keys, values, membership[0], modules)
    out_cross = w_out_cross.reshape(-1, width)
    block = mixed
    resid = resid + lax.psum_scatter(
        jnp.dot(block, out_cross, preferred_element_type=jnp.float32),
        "gene",
        scatter_dimension=0,
        tiled=True,
    )
    pooled = jnp.mean(resid.reshape(cell_share, modules, width), axis=1)
    hidden = lax.all_gather(rms_rows(pooled).astype(jnp.bfloat16), "gene", axis=0, tiled=True)
    panel_count = w_disp.shape[1]
    logit = jnp.dot(hidden, w_mean, preferred_element_type=jnp.float32)
    disp = jnp.dot(hidden, w_disp, preferred_element_type=jnp.float32)
    onehot = (panels[None, :] == jnp.arange(panel_count, dtype=jnp.int32)[:, None]).astype(
        jnp.float32
    )
    theta = jnp.dot(DISP_BASE + jax.nn.softplus(disp), onehot, precision=lax.Precision.HIGHEST)
    rate_scale = (library / genes_all)[:, None]
    rate = rate_scale * jax.nn.softplus(logit)
    nll, d_rate, d_theta = nb_terms(observed, rate, theta)
    norm_scale = (cells * lax.axis_size("grp")) ** (-0.5)
    d_logit = d_rate * rate_scale * jax.nn.sigmoid(logit) * norm_scale
    d_panel = jnp.dot(d_theta, onehot.T, precision=lax.Precision.HIGHEST)
    cell_part = jnp.sum(nll, axis=1)
    hidden_f = hidden.astype(jnp.float32)
    dims = (((0,), (0,)), ((), ()))
    cell_total = lax.psum(cell_part, "gene")
    d_disp = d_panel * jax.nn.sigmoid(disp) * norm_scale
    local_disp = lax.dot_general(hidden_f, d_disp, dims, precision=lax.Precision.HIGHEST)
    grad_disp = lax.psum(local_disp, ("grp", "gene"))
    cell_loss = cell_total / genes_all
    block = hidden_f
    grad_mean = lax.psum_scatter(
        lax.dot_general(block, d_logit, dims, precision=lax.Precision.HIGHEST),
        "grp",
        scatter_dimension=0,
        tiled=True,
    )
    return (cell_loss, grad_mean, grad_disp)


def solution(mesh):
    return jax.shard_map(
        shards,
        mesh=mesh,
        in_specs=(
            P("grp", "gene"),
            P("gene"),
            P("grp", None),
            P("gene", None),
            P(None, "gene", None),
            P("gene", None, None),
            P(None, "gene", None),
            P("gene", None, None),
            P(None, "gene"),
            P(),
        ),
        out_specs=(P("grp"), P("grp", "gene"), P()),
        check_vma=False,
    )
```

profile of v0, /device:TPU:1, one launch (start us, length us, event | category | flops | bytes accessed | tf_op | source)
XLA Modules:
  0.0 771.5 jit_solution(6979199559063120325)
XLA Ops:
  7.2 1.5 convert_reduce_fusion
  8.7 28.0 %psum.28 = f32[256]{0:T(256)S(1)} all-reduce(f32[256]{0:T(256)S(1)} %convert_reduce_fusion), channel_id=1, replica_groups=mesh['grp'=8,'gene'=16] {'gene'}, use_global_device_ids=true, to_apply=%region_1.0 | all-reduce | flops 256 | bytes 2048 | tf_op jit(solution)/shard_map/psum | solution.py:104
  36.8 11.3 %fusion.168 = f32[256,6400]{1,0:T(8,128)} fusion(bf16[960,6400]{1,0:T(8,128)(2,1)} %param.13, s32[256,960]{0,1:T(8,128)} %param.10, f32[256]{0:T(256)S(1)} %get-tuple-element.14), kind=kOutput, calls=%fused_computation.191 | convolution fusion | flops 3146465280 | bytes 19825664 | tf_op jit(solution)/shard_map/dot_general | solution.py:106
  48.0 8.7 %reshape.175 = f32[1024,1600]{1,0:T(8,128)} reshape(f32[256,6400]{1,0:T(8,128)} %fusion.168) | data formatting | bytes 13107200 | tf_op jit(solution)/shard_map/reshape | solution.py:106
  56.7 7.6 copy.115
  64.6 2.3 copy.116
  66.8 2.6 reshape.176
  69.4 2.4 dot_general.55
  72.6 1.8 reshape.178
  74.5 128.4 %all-reduce.3.cloned.1.call-done = f32[1024,1600]{0,1:T(8,128)} async-done(((f32[1024,1600]{0,1:T(8,128)}), f32[1024,1600]{0,1:T(8,128)}) %all-reduce.3.cloned.1.call-update) | async-done | bytes 6553616 | tf_op jit(solution)/shard_map/psum | solution.py:107
  202.9 3.5 multiply_reduce_fusion
  207.6 2.7 fusion.3
  213.4 2.3 copy.118
  215.7 2.5 copy.119
  218.2 3.9 fusion.165
  222.1 1.5 copy.122
  225.9 1.9 fusion.7
  227.8 1.3 copy.125
  230.4 4.9 fusion.246
  235.4 70.0 %reduce-scatter.10.cloned.1.call-done = f32[64,1600]{1,0:T(8,128)} async-done(((f32[1024,1600]{1,0:T(8,128)}), f32[64,1600]{1,0:T(8,128)}) %reduce-scatter.10.cloned.1.call-update) | async-done | bytes 409616
  305.3 2.2 copy.147
  307.5 1.7 multiply_reduce_fusion.1
  310.9 1.9 copy.128
  313.1 2.3 copy.129
  315.3 2.6 reshape.179
  318.0 2.4 dot_general.61
  321.2 1.8 reshape.181
  323.1 28.5 %all-gather.2.cloned.1.call-done = bf16[1024,1600]{1,0:T(8,128)(2,1)} async-done(((bf16[64,1600]{1,0:T(8,128)(2,1)}), bf16[1024,1600]{1,0:T(8,128)(2,1)}) %all-gather.2.cloned.1.call-update) | async-done | bytes 3276816 | tf_op jit(solution)/shard_map/all_gather | solution.py:125
  351.6 3.7 fusion
  357.2 2.4 copy.131
  359.9 2.3 copy.132
  363.2 2.0 copy.130
  365.2 1.7 multiply_convert_fusion.2
  366.9 1.8 multiply_convert_fusion.1
  372.5 4.9 fusion.247
  377.5 68.0 %reduce-scatter.12.cloned.1.call-done = f32[64,1600]{1,0:T(8,128)} async-done(((f32[1024,1600]{1,0:T(8,128)}), f32[64,1600]{1,0:T(8,128)}) %reduce-scatter.12.cloned.1.call-update) | async-done | bytes 409616
  445.5 2.2 copy.149
  447.7 2.4 add.116
  450.1 2.2 copy.140
  452.2 1.9 reshape.182
  455.6 23.6 %all_gather.7 = bf16[256,1600]{1,0:T(8,128)(2,1)S(1)} all-gather(bf16[16,1600]{1,0:T(8,128)(2,1)S(1)} %multiply_convert_fusion.6), channel_id=1, replica_groups=mesh['grp'=8,'gene'=16] {'gene'}, dimensions={0}, use_global_device_ids=true | all-gather | bytes 870400 | tf_op jit(solution)/shard_map/all_gather | solution.py:140
  480.7 19.0 %add_reduce_fusion = (f32[256]{0:T(256)S(1)}, f32[256,960]{0,1:T(8,128)S(1)}) fusion(s32[256,960]{0,1:T(8,128)S(1)} %copy-done.5, f32[256,960]{0,1:T(8,128)S(1)} %fusion.249, f32[256]{0:T(256)S(1)} %get-tuple-element.13, s32[960]{0:T(1024)S(1)} %copy-done.12, f32[256,64]{0,1:T(8,128)S(1)} %fusion.248), kind=kOutput, calls=%fused_computation.136 | convolution fusion | flops 231927552 | bytes 3020544 | tf_op jit(solution)/shard_map/dot_general | solution.py:147
  499.8 15.5 %fusion.9 = f32[256,64]{0,1:T(8,128)S(1)} fusion(f32[256,960]{0,1:T(8,128)S(1)} %get-tuple-element.18, s32[256,960]{0,1:T(8,128)S(1)} %copy-done.5, f32[256,960]{0,1:T(8,128)S(1)} %fusion.249, f32[256]{0:T(256)S(1)} %get-tuple-element.13, s32[960]{0:T(1024)S(1)} %copy-done.12, f32[256,64]{0,1:T(8,128)S(1)} %fusion.248), kind=kOutput, calls=%fused_computation.26 | convolution fusion | flops 229928960 | bytes 3085056 | tf_op jit(solution)/shard_map/dot_general | solution.py:153
  516.7 8.4 %fusion.107 = f32[1600,960]{1,0:T(8,128)} fusion(bf16[256,1600]{1,0:T(8,128)(2,1)} %copy-done.3, f32[256,960]{0,1:T(8,128)} %copy-done.13, s32[256,960]{0,1:T(8,128)S(1)} %copy-done.6, f32[256,960]{0,1:T(8,128)S(1)} %get-tuple-element.18, f32[256]{0:T(256)S(1)} %get-tuple-element.13), kind=kOutput, calls=%fused_computation.126 | convolution fusion | flops 4723261440 | bytes 9913344 | tf_op jit(solution)/shard_map/dot_general | solution.py:164
  525.1 27.0 %psum.30 = f32[256]{0:T(256)S(1)} all-reduce(f32[256]{0:T(256)S(1)} %neg.22), channel_id=1, replica_groups=mesh['grp'=8,'gene'=16] {'gene'}, use_global_device_ids=true, to_apply=%region_16.17 | all-reduce | flops 256 | bytes 2048 | tf_op jit(solution)/shard_map/psum | solution.py:157
  552.7 107.5 %all-reduce.5.cloned.1.call-done = f32[1600,64]{0,1:T(8,128)} async-done(((f32[1600,64]{0,1:T(8,128)}), f32[1600,64]{0,1:T(8,128)}) %all-reduce.5.cloned.1.call-update) | async-done | bytes 409616 | tf_op jit(solution)/shard_map/psum | solution.py:160
  660.2 102.4 %reduce-scatter.8.cloned.1.call-done = f32[200,960]{1,0:T(8,128)} async-done(((f32[1600,960]{1,0:T(8,128)}), f32[200,960]{1,0:T(8,128)}) %reduce-scatter.8.cloned.1.call-update) | async-done | bytes 768016 | tf_op jit(solution)/shard_map/reduce_scatter | solution.py:163
  762.5 1.8 copy.168
  (76 shorter events, 23.6 us)
Async XLA Ops:
  7.2 472.1 %copy-start = (bf16[1600,960]{0,1:T(8,128)(2,1)S(1)}, bf16[1600,960]{0,1:T(8,128)(2,1)}, u32[]{:S(2)}) copy-start(bf16[1600,960]{0,1:T(8,128)(2,1)} %param.18) | copy-start | bytes 9216004
  7.2 195.7 %all-reduce.3.cloned.1.call-start = ((), (), s32[]{:S(2)}) async-start(), calls=%async_computation.3 | async-start | bytes 13107200 | tf_op jit(solution)/shard_map/psum | solution.py:107
  64.3 7.5 copy-start.8
  64.3 241.0 %reduce-scatter.10.cloned.1.call-start = ((), (), s32[]{:S(2)}) async-start(), calls=%async_computation.7 | async-start | bytes 7241728
  202.9 4.7 copy-start.2
  235.3 116.3 %all-gather.2.cloned.1.call-start = ((), (), s32[]{:S(2)}) async-start(), calls=%async_computation.4 | async-start | bytes 3620864 | tf_op jit(solution)/shard_map/all_gather | solution.py:125
  309.2 0.9 copy-start.4
  312.8 7.6 copy-start.9
  312.8 132.7 %reduce-scatter.12.cloned.1.call-start = ((), (), s32[]{:S(2)}) async-start(), calls=%async_computation.8 | async-start | bytes 7241728
  315.3 7.6 copy-start.11
  366.9 2.5 copy-start.7
  377.4 282.7 %all-reduce.5.cloned.1.call-start = ((), (), s32[]{:S(2)}) async-start(), calls=%async_computation.6 | async-start | bytes 851968 | tf_op jit(solution)/shard_map/psum | solution.py:160
  455.6 24.7 %copy-start.10 = (bf16[1600,64]{0,1:T(8,128)(2,1)S(1)}, bf16[1600,64]{0,1:T(8,128)(2,1)}, u32[]{:S(2)}) copy-start(bf16[1600,64]{0,1:T(8,128)(2,1)} %param.19) | copy-start | bytes 614404
  479.2 36.1 %copy-start.3 = (bf16[256,1600]{1,0:T(8,128)(2,1)}, bf16[256,1600]{1,0:T(8,128)(2,1)S(1)}, u32[]{:S(2)}) copy-start(bf16[256,1600]{1,0:T(8,128)(2,1)S(1)} %all_gather.7) | copy-start | bytes 2457604
  479.2 1.5 copy-start.5
  479.2 1.5 copy-start.12
  480.3 19.4 %copy-start.13 = (f32[256,960]{0,1:T(8,128)}, f32[256,960]{0,1:T(8,128)S(1)}, u32[]{:S(2)}) copy-start(f32[256,960]{0,1:T(8,128)S(1)} %fusion.249) | copy-start | bytes 2949124
  499.8 16.9 %copy-start.6 = (s32[256,960]{0,1:T(8,128)S(1)}, s32[256,960]{0,1:T(8,128)}, u32[]{:S(2)}) copy-start(s32[256,960]{0,1:T(8,128)} %param.10) | copy-start | bytes 2949124
  516.6 245.9 %reduce-scatter.8.cloned.1.call-start = ((), (), s32[]{:S(2)}) async-start(), calls=%async_computation.5 | async-start | bytes 7372800 | tf_op jit(solution)/shard_map/reduce_scatter | solution.py:163
  525.1 239.3 %copy-start.1 = (bf16[1600,960]{0,1:T(8,128)(2,1)S(1)}, bf16[1600,960]{0,1:T(8,128)(2,1)}, u32[]{:S(2)}) copy-start(bf16[1600,960]{0,1:T(8,128)(2,1)} %param.18) | copy-start | bytes 9216004
Sparse Core Ops, SparseCore 0:
  64.4 138.3 all-reduce.2
  235.4 69.8 reduce-scatter.9
  312.9 38.6 all-gather.1
  377.5 67.9 reduce-scatter.11
  516.7 143.3 all-reduce.4
  664.5 98.0 reduce-scatter.7
where the time goes:
time: 777 us; the launch traced here: 771 us
  waiting for transfers between devices  505 us (65%)
  matrix products  80.1 us (10%)
  blocking collectives  78.6 us (10%)
  local copies, waits for them, and re-layouts  74.6 us (10%)
  other arithmetic  17.9 us (2%)
  between operations  14.7 us (2%)
    unnamed x8, waiting for transfers between devices  138 us
    psum x1, waiting for transfers between devices, shards(): tokens = lax.psum(partial_value, 'gene')  128 us
    psum x1, waiting for transfers between devices, shards(): grad_disp = lax.psum(local_disp, ('grp', 'gene'))  108 us
    reduce_scatter x1, waiting for transfers between devices, shards(): lax.psum_scatter(lax.dot_general(block, d_logit, dims, precision=lax.Prec...  102 us
    all_gather x1, waiting for transfers between devices, shards(): lax.all_gather(rms_rows(resid).astype(jnp.bfloat16), 'gene', axis=0, tile...  28.5 us
    psum x1, blocking collectives, shards(): library = 1.0 + lax.psum(jnp.sum(observed, axis=1), 'gene')  28 us
    psum x1, blocking collectives, shards(): cell_total = lax.psum(cell_part, 'gene')  27 us
    all_gather x1, blocking collectives, shards(): lax.all_gather(rms_rows(pooled).astype(jnp.bfloat16), 'gene', axis=0, til...  23.6 us
  transfers between devices with their start and end apart: 6, of which 6 were waited for; matrix products, arithmetic and copies ran while one was open for 4% of the time, Pallas kernels for 0%

commit v1 on v0

v1 whole, which is shorter than its diff:
```python
import functools
import math

import jax
import jax.numpy as jnp
from jax import lax
from jax.experimental import pallas as pl
from jax.experimental.pallas import tpu as pltpu
from jax.sharding import PartitionSpec as P

EPS = 1e-06
FLOOR = 0.3
TARGET = 10000.0
DISP_BASE = 0.5
MESH = pl.DeviceIdType.MESH
F32 = jnp.float32
BF16 = jnp.bfloat16

NX = 4
NY = 2
NG = 16
NCHIP = 8
NR = 8
NZ = 4
NM = 4
ROWS = 16
LIMIT = 64 * 1024 * 1024 - 256 * 1024
DN_T = (((1,), (1,)), ((), ()))
DN_0 = (((0,), (0,)), ((), ()))


def remote(src, dst, send, recv, axis, to):
    return pltpu.make_async_remote_copy(
        src_ref=src, dst_ref=dst, send_sem=send, recv_sem=recv, device_id={axis: to}, device_id_type=MESH
    )


class Place:
    def __init__(self):
        self.g = lax.axis_index("gene")
        self.core = lax.rem(self.g, 2)
        self.x = lax.rem(self.g // 2, NX)
        self.y = self.g // (2 * NX)
        self.right = self.at(self.y, self.shift(1), self.core)
        self.left = self.at(self.y, self.shift(3), self.core)
        self.other_y = self.at(1 - self.y, self.x, self.core)
        self.other_core = self.at(self.y, self.x, 1 - self.core)

    def shift(self, by):
        return lax.rem(self.x + by, NX)

    def at(self, y, x, core):
        return (y * NX + x) * 2 + core

    def chip(self, y, x):
        return y * NX + x


def greet(axis_peers):
    barrier = pltpu.get_barrier_semaphore()
    for axis, to in axis_peers:
        pl.semaphore_signal(barrier, inc=1, device_id={axis: to}, device_id_type=MESH)
    pl.semaphore_wait(barrier, len(axis_peers))


def near(place):
    return [("gene", t) for t in (place.right, place.left, place.other_y, place.other_core)]


def everyone(place):
    return [("gene", lax.rem(place.g + k, NG)) for k in range(1, NG)]


def rms(values):
    return values * lax.rsqrt(jnp.mean(values * values, axis=-1, keepdims=True) + EPS)


class Scatter:
    @staticmethod
    def scratch(width):
        return [
            pltpu.VMEM((NM, NCHIP, 2, ROWS, width), BF16),
            pltpu.VMEM((NM, NCHIP, ROWS, width), BF16),
            pltpu.VMEM((NM, NCHIP, ROWS, width), BF16),
            pltpu.VMEM((NM, 3, ROWS, width), BF16),
            pltpu.VMEM((NM, 3, ROWS, width), BF16),
            pltpu.VMEM((NM, 2, ROWS, width), BF16),
            pltpu.VMEM((NM, ROWS, width), BF16),
            pltpu.VMEM((NM, ROWS, width), BF16),
            pltpu.VMEM((NM, ROWS, width), F32),
            pltpu.SemaphoreType.DMA((NM, 8)),
            pltpu.SemaphoreType.DMA((NM, 8)),
        ]

    COUNT = 11

    def __init__(self, place, refs):
        (self.part, self.pair, self.chip, self.from_left, self.from_right, self.relay,
         self.y_out, self.y_in, self.mine, self.send, self.recv) = refs
        p = self.place = place
        x, y = p.x, p.y
        ahead, behind, across = p.shift(1), p.shift(3), p.shift(2)
        self.copies = []
        for m in range(NM):
            def go(slot, src, dst, to):
                return remote(src, dst, self.send.at[m, slot], self.recv.at[m, slot], "gene", to)
            self.copies.append([
                go(0, self.part.at[m, :, 1 - p.core], self.pair.at[m], p.other_core),
                go(1, self.chip.at[m, p.chip(0, across)], self.from_left.at[m, 0], p.right),
                go(2, self.chip.at[m, p.chip(1, across)], self.from_right.at[m, 0], p.left),
                go(3, self.chip.at[m, p.chip(1, ahead)], self.from_left.at[m, 2], p.right),
                go(4, self.chip.at[m, p.chip(0, behind)], self.from_right.at[m, 2], p.left),
                go(5, self.relay.at[m, 0], self.from_left.at[m, 1], p.right),
                go(6, self.relay.at[m, 1], self.from_right.at[m, 1], p.left),
                go(7, self.y_out.at[m], self.y_in.at[m], p.other_y),
            ])

    def give(self, m):
        self.copies[m][0].start()

    def spread(self, m):
        self.copies[m][0].wait_recv()
        for q in range(NCHIP):
            self.chip[m, q] = (self.part[m, q, self.place.core].astype(F32) + self.pair[m, q].astype(F32)).astype(BF16)
        for k in (1, 2, 3, 4):
            self.copies[m][k].start()

    def forward(self, m):
        p = self.place
        self.copies[m][1].wait_recv()
        self.relay[m, 0] = (
            self.chip[m, p.chip(0, p.shift(1))].astype(F32) + self.from_left[m, 0].astype(F32)
        ).astype(BF16)
        self.copies[m][5].start()
        self.copies[m][2].wait_recv()
        self.relay[m, 1] = (
            self.chip[m, p.chip(1, p.shift(3))].astype(F32) + self.from_right[m, 0].astype(F32)
        ).astype(BF16)
        self.copies[m][6].start()

    def cross(self, m):
        p = self.place
        for k in (3, 4, 5, 6):
            self.copies[m][k].wait_recv()
        self.y_out[m] = (
            self.chip[m, p.chip(1 - p.y, p.x)].astype(F32)
            + self.from_left[m, 2 - p.y].astype(F32)
            + self.from_right[m, 1 + p.y].astype(F32)
        ).astype(BF16)
        self.copies[m][7].start()
        self.mine[m] = (
            self.chip[m, p.chip(p.y, p.x)].astype(F32)
            + self.from_left[m, 1 + p.y].astype(F32)
            + self.from_right[m, 2 - p.y].astype(F32)
        )

    def take(self, m):
        self.copies[m][7].wait_recv()
        return self.mine[m] + self.y_in[m].astype(F32)

    def drain(self):
        for row in self.copies:
            for copy in row:
                copy.wait_send()


def run_scatter(scatter, produce, consume):
    steps = [produce, scatter.spread, scatter.forward, scatter.cross, consume]
    for t in range(NM + len(steps) - 1):
        for lag, step in enumerate(steps):
            if 0 <= t - lag < NM:
                step(t - lag)


class Gather:
    SLOTS = 15

    def __init__(self, place, block, send, recv, index):
        p = place
        ahead, behind, across = p.shift(1), p.shift(3), p.shift(2)
        y, z, c, x = p.y, 1 - p.y, p.core, p.x

        def go(slot, owner, to):
            ref = block(owner)
            return remote(ref, ref, send.at[index, slot], recv.at[index, slot], "gene", to)

        own, paired = p.at(y, x, c), p.at(z, x, c)
        held = [own, paired, p.at(y, behind, c), p.at(y, ahead, c), p.at(z, behind, c), p.at(z, ahead, c),
                p.at(y, across, c), p.at(z, across, c)]
        self.copies = [
            go(0, own, p.other_y),
            go(1, own, p.right),
            go(2, own, p.left),
            go(3, paired, p.right),
            go(4, paired, p.left),
            go(5, held[2], p.right),
            go(6, held[5], p.left),
        ] + [go(7 + k, held[k], p.other_core) for k in range(8)]
        self.c = self.copies

    def start(self):
        for k in (1, 2, 0, 7):
            self.c[k].start()

    def second(self):
        c = self.c
        c[1].wait_recv()
        c[5].start()
        c[9].start()
        c[0].wait_recv()
        c[3].start()
        c[4].start()
        c[8].start()
        c[2].wait_recv()
        c[10].start()

    def third(self):
        c = self.c
        c[4].wait_recv()
        c[6].start()
        c[12].start()
        c[3].wait_recv()
        c[11].start()

    def finish(self):
        c = self.c
        c[5].wait_recv()
        c[13].start()
        c[6].wait_recv()
        c[14].start()
        for k in range(7, 15):
            c[k].wait_recv()

    def drain(self):
        for copy in self.c:
            copy.wait_send()


def run_gather(gathers):
    for step in ("start", "second", "third", "finish", "drain"):
        for gather in gathers:
            getattr(gather, step)()


class Swap:
    def __init__(self, place, source, slots, send, recv, index):
        self.out, self.into = [], []
        for k in range(1, NG):
            to, frm = lax.rem(place.g + k, NG), lax.rem(place.g + NG - k, NG)
            self.out.append(remote(source(to), slots.at[place.g], send.at[index, k], recv.at[index, place.g], "gene", to))
            self.into.append(remote(source(frm), slots.at[frm], send.at[index, k], recv.at[index, frm], "gene", frm))

    def start(self):
        for copy in self.out:
            copy.start()

    def finish(self):
        for copy in self.into:
            copy.wait_recv()

    def drain(self):
        for copy in self.out:
            copy.wait_send()


def total_of(slots):
    total = slots[0]
    for k in range(1, NG):
        total = total + slots[k]
    return total


def encode_kernel(counts, w_hbm, normed, tokens, library, scaled, weights, tile, slots, w_sem, s_send, s_recv, a_send, a_recv, *refs):
    place = Place()
    width = tokens.shape[-1]
    wide = weights.shape[-1]
    greet(everyone(place))
    loads = [
        pltpu.make_async_copy(w_hbm.at[:, pl.ds((m * width) // 128 * 128, wide)], weights.at[m], w_sem.at[m])
        for m in range(NM)
    ]
    tile[...] = jnp.broadcast_to(jnp.sum(counts[...].astype(F32), axis=0, keepdims=True), tile.shape)
    swap = Swap(place, lambda t: tile, slots, s_send, s_recv, 0)
    swap.start()
    for load in loads:
        load.start()
    slots[place.g] = tile[...]
    swap.finish()
    total = 1.0 + total_of(slots)
    library[...] = total
    factor = TARGET / total[0:1]
    scaled[...] = jnp.log1p(counts[...].astype(F32) * factor).T.astype(BF16)
    scatter = Scatter(place, refs)
    gather = [
        Gather(place, lambda o, m=m: normed.at[m, pl.ds(pl.multiple_of(o * ROWS, ROWS), ROWS), :], a_send, a_recv, m)
        for m in range(NM)
    ]

    def produce(m):
        loads[m].wait()
        skip = (m * width) % 128
        out = jnp.dot(scaled[...], weights[m], preferred_element_type=F32)[:, skip:skip + width]
        scatter.part[m] = out.astype(BF16).reshape(NCHIP, 2, ROWS, width)
        scatter.give(m)

    def consume(m):
        value = scatter.take(m)
        tokens[m] = value
        normed[m, pl.ds(pl.multiple_of(place.g * ROWS, ROWS), ROWS), :] = rms(value).astype(BF16)
        gather[m].start()

    run_scatter(scatter, produce, consume)
    for step in ("second", "third", "finish", "drain"):
        for one in gather:
            getattr(one, step)()
    scatter.drain()
    swap.drain()


def half_sum(values):
    high = values.astype(BF16)
    low = (values - high.astype(F32)).astype(BF16)
    row = lax.broadcasted_iota(jnp.int32, (256, 128), 0)
    col = lax.broadcasted_iota(jnp.int32, (256, 128), 1)
    ones = ((lax.rem(row, 128) // 64) == (col // 64)).astype(BF16)
    return jnp.dot(jnp.concatenate([high, low], axis=1), ones, preferred_element_type=F32)


def heads_of(normed, w_qkv, query, keys, values, head):
    for m in range(NM):
        qkv = lax.dot_general(normed[m], w_qkv[...], DN_T, preferred_element_type=F32)
        for at, ref in ((0, query), (1, keys)):
            part = qkv[:, at * 128:(at + 1) * 128]
            mean = half_sum(part * part) / head
            ref[m] = (part * lax.rsqrt(jnp.maximum(mean, FLOOR))).astype(BF16)
        values[m] = qkv[:, 256:384].astype(BF16)


def within_mix(m, query, keys, values, head):
    q = query[m].astype(F32)
    weights = [jnp.exp(half_sum(q * keys[n].astype(F32)) * head ** (-0.5)) for n in range(NM)]
    total = weights[0] + weights[1] + weights[2] + weights[3]
    mixed = None
    for n in range(NM):
        term = (weights[n] / total).astype(BF16).astype(F32) * values[n].astype(F32)
        mixed = term if mixed is None else mixed + term
    return mixed.astype(BF16)


def cross_mix(m, query, keys, values, same, head):
    lane = lax.broadcasted_iota(jnp.int32, query.shape[1:], 1) // 64
    out = []
    for h in range(2):
        q = jnp.where(lane == h, query[m].astype(F32), 0.0).astype(BF16)
        scores = lax.dot_general(q, keys[m], DN_T, preferred_element_type=F32) * head ** (-0.5)
        weights = jnp.where(same, jnp.exp(scores), 0.0)
        probs = (weights / jnp.sum(weights, axis=-1, keepdims=True)).astype(BF16)
        out.append(jnp.dot(probs, values[m], preferred_element_type=F32))
    return jnp.where(lane == 0, out[0], out[1]).astype(BF16)


def within_kernel(head, normed_in, tokens, w_qkv, w_out, normed, resid, query, keys, values, a_send, a_recv, *refs):
    place = Place()
    width = tokens.shape[-1]
    greet(near(place))
    scatter = Scatter(place, refs)
    gather = [
        Gather(place, lambda o, m=m: normed.at[m, pl.ds(pl.multiple_of(o * ROWS, ROWS), ROWS), :], a_send, a_recv, m)
        for m in range(NM)
    ]
    heads_of(normed_in, w_qkv, query, keys, values, head)

    def produce(m):
        mixed = within_mix(m, query, keys, values, head)
        out = jnp.dot(mixed, w_out[...], preferred_element_type=F32)
        scatter.part[m] = out.astype(BF16).reshape(NCHIP, 2, ROWS, width)
        scatter.give(m)

    def consume(m):
        value = tokens[m] + scatter.take(m)
        resid[m] = value
        normed[m, pl.ds(pl.multiple_of(place.g * ROWS, ROWS), ROWS), :] = rms(value).astype(BF16)
        gather[m].start()

    run_scatter(scatter, produce, consume)
    for step in ("second", "third", "finish", "drain"):
        for one in gather:
            getattr(one, step)()
    scatter.drain()


def cross_kernel(head, normed_in, resid, w_qkv, w_out, groups, hidden, query, keys, values, a_send, a_recv, *refs):
    place = Place()
    width = resid.shape[-1]
    cells = hidden.shape[0]
    greet(near(place))
    scatter = Scatter(place, refs)
    gather = Gather(
        place, lambda o: hidden.at[pl.ds(pl.multiple_of(o * ROWS, ROWS), ROWS), :], a_send, a_recv, 0
    )
    heads_of(normed_in, w_qkv, query, keys, values, head)
    row = jnp.broadcast_to(groups[...].astype(F32), (cells, cells))
    same = row == row.T
    pool = []

    def produce(m):
        mixed = cross_mix(m, query, keys, values, same, head)
        out = jnp.dot(mixed, w_out[...], preferred_element_type=F32)
        scatter.part[m] = out.astype(BF16).reshape(NCHIP, 2, ROWS, width)
        scatter.give(m)

    def consume(m):
        pool.append(resid[m] + scatter.take(m))

    run_scatter(scatter, produce, consume)
    pooled = (pool[0] + pool[1] + pool[2] + pool[3]) * (1.0 / NM)
    hidden[pl.ds(pl.multiple_of(place.g * ROWS, ROWS), ROWS), :] = rms(pooled).astype(BF16)
    run_gather([gather])
    scatter.drain()


class GroupGather:
    SLOTS = 7

    def __init__(self, r, block, send, recv, index):
        z, h = lax.rem(r, NZ), r // NZ
        up, down = lax.rem(z + 1, NZ), lax.rem(z + 3, NZ)
        k = 1 - h

        def at(a, b):
            return a * NZ + b

        def go(slot, owner, to):
            ref = block(owner)
            return remote(ref, ref, send.at[index, slot], recv.at[index, slot], "grp", to)

        self.c = [
            go(0, at(h, z), at(k, z)),
            go(1, at(h, z), at(h, up)),
            go(2, at(h, z), at(h, down)),
            go(3, at(k, z), at(h, up)),
            go(4, at(k, z), at(h, down)),
            go(5, at(h, down), at(h, up)),
            go(6, at(k, up), at(h, down)),
        ]

    def start(self):
        for k in (1, 2, 0):
            self.c[k].start()

    def second(self):
        c = self.c
        c[1].wait_recv()
        c[5].start()
        c[0].wait_recv()
        c[3].start()
        c[4].start()

    def third(self):
        self.c[4].wait_recv()
        self.c[6].start()

    def finish(self):
        for k in (2, 3, 5, 6):
            self.c[k].wait_recv()

    def drain(self):
        for copy in self.c:
            copy.wait_send()


def log_factorials(count):
    return [math.log(math.factorial(k)) for k in range(count)]


def terms(x, theta, logit, rate_scale, norm_scale, most):
    tail = jnp.exp(-jnp.abs(logit))
    soft = jnp.maximum(logit, 0.0) + jnp.log1p(tail)
    sigmoid = jnp.where(logit >= 0, 1.0, tail) / (1.0 + tail)
    rate = rate_scale * soft
    product = jnp.ones_like(theta)
    slope = jnp.zeros_like(theta)
    log_factorial = jnp.zeros_like(theta)
    table = log_factorials(most + 1)
    for k in range(most):
        on = x > k
        term = theta + float(k)
        slope = jnp.where(on, slope * term + product, slope)
        product = jnp.where(on, product * term, product)
        if k:
            log_factorial = jnp.where(on, table[k + 1], log_factorial)
    total = theta + rate
    log_total = jnp.log(total)
    log_theta = jnp.log(theta)
    ratio = (theta + x) / total
    nll = -(
        jnp.log(product) - log_factorial
        + theta * (log_theta - log_total)
        + x * (jnp.log(rate) - log_total)
    )
    d_logit = (ratio - x / rate) * rate_scale * sigmoid * norm_scale
    d_theta = -(slope / product + log_theta + 1.0 - log_total - ratio)
    return nll, d_logit, d_theta


def decode_kernel(
    genes_all, cells_all, panel_count,
    counts, panel_row, panel_col, library, hidden, w_mean, w_disp,
    cell_loss, grad_mean, grad_disp,
    tile, slots, back, piece, columns, field, panel_part, loss, gradient, disp_block,
    s_send, s_recv, h_send, h_recv, v_send, v_recv, f_send, f_recv, o_send, o_recv,
):
    place = Place()
    r = lax.axis_index("grp")
    genes, cells = counts.shape
    width = hidden.shape[1]
    share = width // NR
    parts = 4
    step = genes // parts
    norm_scale = cells_all ** (-0.5)
    greet(everyone(place) + [("grp", lax.rem(r + k, NR)) for k in range(1, NR)])

    own = hidden[pl.ds(pl.multiple_of(place.g * ROWS, ROWS), ROWS), :].astype(F32)
    piece[...] = jnp.zeros_like(piece)
    for k in range(NR):
        piece[k, :, 0:share] = own[:, k * share:(k + 1) * share].astype(BF16)
    rows = pl.ds(pl.multiple_of(place.g * ROWS, ROWS), ROWS)
    out, into = [], []
    for k in range(1, NR):
        to, frm = lax.rem(r + k, NR), lax.rem(r + NR - k, NR)
        out.append(remote(piece.at[to], columns.at[r, rows], h_send.at[k], h_recv.at[r], "grp", to))
        into.append(remote(piece.at[frm], columns.at[frm, rows], h_send.at[k], h_recv.at[frm], "grp", frm))
    for copy in out:
        copy.start()
    columns[r, rows] = piece[r]

    disp = lax.dot_general(w_disp[...], hidden[...], DN_T, preferred_element_type=F32)
    table = DISP_BASE + (jnp.maximum(disp, 0.0) + jnp.log1p(jnp.exp(-jnp.abs(disp))))
    high = table.astype(BF16)
    rest = table - high.astype(F32)
    middle = rest.astype(BF16)
    low = (rest - middle.astype(F32)).astype(BF16)
    tables = jnp.concatenate([high, middle, low], axis=0)
    rate_scale = library[0:1] / genes_all
    panel_part[...] = jnp.zeros_like(panel_part)
    loss[...] = jnp.zeros_like(loss)

    v_gather = Gather(
        place, lambda o: columns.at[:, pl.ds(pl.multiple_of(o * ROWS, ROWS), ROWS), :], v_send, v_recv, 0
    )
    field_gather = [
        GroupGather(r, lambda o, p=p: field.at[o, pl.ds(p * step, step), :], f_send, f_recv, p) for p in range(parts)
    ]
    field_gather.append(
        GroupGather(r, lambda o: field.at[o, pl.ds(genes, panel_count), :], f_send, f_recv, parts)
    )

    def decode(p):
        at = pl.ds(p * step, step)
        x = counts[at, :].astype(F32)
        logit = lax.dot_general(w_mean[at, :], hidden[...], DN_T, preferred_element_type=F32)
        lane = lax.broadcasted_iota(jnp.int32, (step, 3 * panel_count), 1)
        pick = (panel_col[at, :] == lax.rem(lane, panel_count)).astype(F32).astype(BF16)
        theta = jnp.dot(pick, tables, preferred_element_type=F32)
        nll, d_logit, d_theta = terms(x, theta, logit, rate_scale, norm_scale, 12)
        field[r, at, :] = d_logit.astype(BF16)
        field_gather[p].start()
        loss[...] += jnp.sum(nll, axis=0, keepdims=True)
        row = lax.broadcasted_iota(jnp.int32, (step, 128), 1)
        wanted = jnp.where(lax.rem(row, 8) < 4, (row // 8) * 4 + lax.rem(row, 8), -1)
        pick_t = (panel_col[at, :] == wanted).astype(F32).astype(BF16)
        upper = d_theta.astype(BF16)
        lower = (d_theta - upper.astype(F32)).astype(BF16)
        panel_part[...] += lax.dot_general(pick_t, upper, DN_0, preferred_element_type=F32) + lax.dot_general(
            pick_t, lower, DN_0, preferred_element_type=F32
        )

    decode(0)
    for copy in into:
        copy.wait_recv()
    v_gather.start()
    decode(1)
    v_gather.second()
    field_gather[0].second()
    decode(2)
    v_gather.third()
    field_gather[0].third()
    field_gather[1].second()
    decode(3)

    row = lax.broadcasted_iota(jnp.int32, (128, cells), 0)
    both = jnp.where(lax.rem(row, 8) == 4, loss[...], panel_part[...])
    tile[...] = both.reshape(NG, 8, cells)
    first = Swap(place, lambda t: tile.at[t], slots, s_send, s_recv, 0)
    first.start()
    slots[place.g] = tile[place.g]
    v_gather.finish()
    field_gather[1].third()
    field_gather[2].second()
    first.finish()
    summed = total_of(slots)
    cell_loss[...] = summed[4:5] / genes_all
    back[place.g] = summed
    second = Swap(place, lambda t: back.at[place.g], back, s_send, s_recv, 1)
    second.start()
    field_gather[2].third()
    field_gather[3].second()
    second.finish()
    d_panel = jnp.concatenate([back[k, 0:4] for k in range(NG)], axis=0)
    tail = jnp.exp(-jnp.abs(disp))
    d_disp = d_panel * (jnp.where(disp >= 0, 1.0, tail) / (1.0 + tail)) * norm_scale
    field[r, pl.ds(genes, panel_count), :] = d_disp.astype(BF16)
    field_gather[parts].start()
    field_gather[3].third()
    field_gather[parts].second()
    field_gather[parts].third()

    def contract(at, size):
        total = jnp.zeros((size, columns.shape[2]), F32)
        for k in range(NR):
            total = total + jnp.dot(field[k, pl.ds(at, size), :], columns[k], preferred_element_type=F32)
        return total

    field_gather[parts].finish()
    part = contract(genes, panel_count)
    disp_block[r] = part
    spread, arrive = [], []
    for k in range(1, NR):
        to, frm = lax.rem(r + k, NR), lax.rem(r + NR - k, NR)
        spread.append(remote(disp_block.at[r], disp_block.at[r], o_send.at[k], o_recv.at[r], "grp", to))
        arrive.append(remote(disp_block.at[frm], disp_block.at[frm], o_send.at[k], o_recv.at[frm], "grp", frm))
    for copy in spread:
        copy.start()
    for p in range(parts):
        field_gather[p].finish()
        gradient[pl.ds(p * step, step), :] = contract(p * step, step)
    grad_mean[...] = gradient[...].T[0:share]
    for copy in arrive:
        copy.wait_recv()
    for k in range(NR):
        grad_disp[:, k * share:(k + 1) * share] = disp_block[k, :, 0:share]
    for copy in out + spread:
        copy.wait_send()
    for one in [v_gather, first, second] + field_gather:
        one.drain()


def whole():
    return pl.BlockSpec(memory_space=pltpu.VMEM)


def params(number):
    return pltpu.CompilerParams(collective_id=number, has_side_effects=True, vmem_limit_bytes=LIMIT)


def head_weights(w_qkv):
    width, heads, three = w_qkv.shape
    turned = jnp.transpose(w_qkv, (2, 1, 0)).reshape(3, three // 3, heads, width)
    turned = jnp.transpose(turned, (0, 2, 1, 3))
    turned = jnp.pad(turned, ((0, 0), (0, 0), (0, 64 - three // 3), (0, 0)))
    return turned.reshape(3 * heads * 64, width)


def out_weights(w_out):
    heads, head, width = w_out.shape
    return jnp.pad(w_out, ((0, 0), (0, 64 - head), (0, 0))).reshape(heads * 64, width)


def shards(counts, panels, membership, w_proj, w_qkv_within, w_out_within, w_qkv_cross, w_out_cross, w_mean, w_disp):
    cells, genes = counts.shape
    width = w_qkv_within.shape[0]
    head = w_out_within.shape[1]
    genes_all = genes * NG
    cells_all = cells * NR
    panel_count = w_disp.shape[1]
    counts_t = counts.T
    scatter = Scatter.scratch(width)
    gather_sems = [pltpu.SemaphoreType.DMA((NM, Gather.SLOTS))] * 2
    swap_sems = [pltpu.SemaphoreType.DMA((2, NG))] * 2
    block = jax.ShapeDtypeStruct((NM, cells, width), BF16)
    mine = jax.ShapeDtypeStruct((NM, ROWS, width), F32)
    normed, tokens, library = pl.pallas_call(
        encode_kernel,
        name="encode",
        out_shape=(block, mine, jax.ShapeDtypeStruct((8, cells), F32)),
        in_specs=[whole(), pl.BlockSpec(memory_space=pl.ANY)],
        out_specs=(whole(), whole(), whole()),
        scratch_shapes=[
            pltpu.VMEM((cells, genes), BF16),
            pltpu.VMEM((NM, genes, 1664), BF16),
            pltpu.VMEM((8, cells), F32),
            pltpu.VMEM((NG, 8, cells), F32),
            pltpu.SemaphoreType.DMA((NM,)),
        ] + swap_sems + gather_sems + scatter,
        compiler_params=params(0),
    )(counts_t, w_proj)
    heads_scratch = [pltpu.VMEM((NM, cells, 128), BF16)] * 3
    normed, resid = pl.pallas_call(
        functools.partial(within_kernel, head),
        name="within",
        out_shape=(block, mine),
        in_specs=[whole()] * 4,
        out_specs=(whole(), whole()),
        scratch_shapes=heads_scratch + gather_sems + scatter,
        compiler_params=params(1),
    )(normed, tokens, head_weights(w_qkv_within), out_weights(w_out_within))
    hidden = pl.pallas_call(
        functools.partial(cross_kernel, head),
        name="cross",
        out_shape=jax.ShapeDtypeStruct((cells, width), BF16),
        in_specs=[whole()] * 5,
        out_specs=whole(),
        scratch_shapes=heads_scratch + gather_sems + scatter,
        compiler_params=params(2),
    )(normed, resid, head_weights(w_qkv_cross), out_weights(w_out_cross), membership)
    cell_loss, grad_mean, grad_disp = pl.pallas_call(
        functools.partial(decode_kernel, genes_all, cells_all, panel_count),
        name="decode",
        out_shape=(
            jax.ShapeDtypeStruct((1, cells), F32),
            jax.ShapeDtypeStruct((width // NR, genes), F32),
            jax.ShapeDtypeStruct((panel_count, width), F32),
        ),
        in_specs=[whole()] * 7,
        out_specs=(whole(), whole(), whole()),
        scratch_shapes=[
            pltpu.VMEM((NG, 8, cells), F32),
            pltpu.VMEM((NG, 8, cells), F32),
            pltpu.VMEM((NG, 8, cells), F32),
            pltpu.VMEM((NR, ROWS, 256), BF16),
            pltpu.VMEM((NR, cells, 256), BF16),
            pltpu.VMEM((NR, genes + panel_count, cells), BF16),
            pltpu.VMEM((128, cells), F32),
            pltpu.VMEM((1, cells), F32),
            pltpu.VMEM((genes, 256), F32),
            pltpu.VMEM((NR, panel_count, 256), F32),
        ] + swap_sems + [
            pltpu.SemaphoreType.DMA((NR,)),
            pltpu.SemaphoreType.DMA((NR,)),
            pltpu.SemaphoreType.DMA((1, Gather.SLOTS)),
            pltpu.SemaphoreType.DMA((1, Gather.SLOTS)),
            pltpu.SemaphoreType.DMA((5, GroupGather.SLOTS)),
            pltpu.SemaphoreType.DMA((5, GroupGather.SLOTS)),
            pltpu.SemaphoreType.DMA((NR,)),
            pltpu.SemaphoreType.DMA((NR,)),
        ],
        compiler_params=params(3),
    )(counts_t, panels[None, :], panels[:, None], library, hidden, w_mean.T, w_disp.T)
    return cell_loss[0], grad_mean, grad_disp.T


def solution(mesh):
    return jax.shard_map(
        shards,
        mesh=mesh,
        in_specs=(
            P("grp", "gene"),
            P("gene"),
            P("grp", None),
            P("gene", None),
            P(None, "gene", None),
            P("gene", None, None),
            P(None, "gene", None),
            P("gene", None, None),
            P(None, "gene"),
            P(),
        ),
        out_specs=(P("grp"), P("grp", "gene"), P()),
        check_vma=False,
    )
```

time: 777 us -> 225 us (0.29)
  waiting for transfers between devices: 505 us -> 0 us
  Pallas kernels: 0 us -> 207 us
  matrix products: 80.1 us -> 0 us
  blocking collectives: 78.6 us -> 0 us
  local copies, waits for them, and re-layouts: 74.6 us -> 12.9 us
  other arithmetic: 17.9 us -> 0 us
  between operations: 14.7 us -> 0.7 us
    psum x2 -> x0, waiting for transfers between devices: 236 us -> none  [the longest x1 128 us: shards(): tokens = lax.psum(partial_value, 'gene')]
    pallas_call x0 -> x4, Pallas kernels: none -> 207 us  [the longest x1 60.8 us: shards(): pl.pallas_call(functools.partial(decode_kernel, genes_all, cells_all, pan...]
    unnamed x8 -> x0, waiting for transfers between devices: 138 us -> none
    reduce_scatter x1 -> x0, waiting for transfers between devices: 102 us -> none  [shards(): lax.psum_scatter(lax.dot_general(block, d_logit, dims, precision=lax.Prec...]
    dot_general x13 -> x0, matrix products: 70.3 us -> none  [the longest x1 19 us: shards(): jnp.dot(DISP_BASE + jax.nn.softplus(disp), onehot, precision=lax.Precisio...]
    psum x2 -> x0, blocking collectives: 55 us -> none  [the longest x1 28 us: shards(): library = 1.0 + lax.psum(jnp.sum(observed, axis=1), 'gene')]
    all_gather x1 -> x0, waiting for transfers between devices: 28.5 us -> none  [shards(): lax.all_gather(rms_rows(resid).astype(jnp.bfloat16), 'gene', axis=0, tile...]
    reshape x9 -> x2, local copies, waits for them, and re-layouts: 29.7 us -> 2.74 us  [head_weights(): jnp.transpose(w_qkv, (2, 1, 0)).reshape(3, three // 3, heads, width)]
  transfers between devices with their start and end apart: 6 -> 0, of which waited for: 6 -> 0; matrix products, arithmetic and copies ran while one was open for 4% -> 0% of each run, Pallas kernels for 0% -> 0%
where the time goes in v1:
time: 225 us; the launch traced here: 221 us
  Pallas kernels  207 us (92%)
  local copies, waits for them, and re-layouts  12.9 us (6%)
    pallas_call x1, Pallas kernels, shards(): pl.pallas_call(functools.partial(decode_kernel, genes_all, cells_all, pan...  60.8 us
    pallas_call x1, Pallas kernels, shards(): pl.pallas_call(encode_kernel, name='encode', out_shape=(block, mine, jax....  55.2 us
    pallas_call x1, Pallas kernels, shards(): pl.pallas_call(functools.partial(within_kernel, head), name='within', out...  49.5 us
    pallas_call x1, Pallas kernels, shards(): pl.pallas_call(functools.partial(cross_kernel, head), name='cross', out_s...  41.9 us
    unnamed x11, local copies, waits for them, and re-layouts  5.24 us

profile of v1, /device:TPU:1, one launch (start us, length us, event | category | flops | bytes accessed | tf_op | source)
XLA Modules:
  0.0 221.0 jit_solution(2926563612522961677)
XLA Ops:
  0.6 55.2 %encode.1 = (bf16[4,256,1600]{2,1,0:T(8,128)(2,1)}, f32[4,16,1600]{2,1,0:T(8,128)}, f32[8,256]{1,0:T(8,128)}) custom-call(s32[960,256]{1,0:T(8,128)} %bitcast.27, bf16[960,6400]{1,0:T(8,128)(2,1)} %w_hbm.1), custom_call_target="tpu_custom_call" | custom-call | tf_op jit(solution)/shard_map/encode/pallas_call | solution.py:682
  55.8 0.0 copy-start
  55.8 1.4 copy.27
  57.2 1.2 pad.14
  58.4 0.0 copy-done
  58.4 0.8 pad.15.clone
  59.2 49.5 %within.1 = (bf16[4,256,1600]{2,1,0:T(8,128)(2,1)}, f32[4,16,1600]{2,1,0:T(8,128)}) custom-call(bf16[4,256,1600]{2,1,0:T(8,128)(2,1)} %get-tuple-element.12.normed_in, f32[4,16,1600]{2,1,0:T(8,128)} %get-tuple-element.13.tokens, bf16[384,1600]{1,0:T(8,128)(2,1)} %bitcast.23, bf16[128,1600]{1,0:T(8,128)(2,1)} %bitcast.30), custom_call_target="tpu_custom_call" | custom-call | tf_op jit(solution)/shard_map/within/pallas_call | solution.py:698
  108.7 0.0 copy-start.1
  108.7 1.4 copy.26
  110.1 1.2 pad.16
  111.3 0.0 copy-done.1
  111.3 0.8 pad.17.clone
  112.1 0.0 copy-start.2
  112.1 41.9 %cross.1.hidden = bf16[256,1600]{1,0:T(8,128)(2,1)} custom-call(bf16[4,256,1600]{2,1,0:T(8,128)(2,1)} %get-tuple-element.14.normed_in, f32[4,16,1600]{2,1,0:T(8,128)} %get-tuple-element.15.resid, bf16[384,1600]{1,0:T(8,128)(2,1)} %bitcast.24, bf16[128,1600]{1,0:T(8,128)(2,1)} %bitcast.31, s32[1,256]{1,0:T(1,128)} %groups.1), custom_call_target="tpu_custom_call" | custom-call | tf_op jit(solution)/shard_map/cross/pallas_call | solution.py:707
  154.0 0.0 copy-done.2
  154.0 1.0 copy.21.panel_col
  155.0 60.8 %decode.1 = (f32[1,256]{1,0:T(1,128)}, f32[200,960]{1,0:T(8,128)}, f32[64,1600]{1,0:T(8,128)}) custom-call(s32[960,256]{1,0:T(8,128)} %bitcast.28, s32[1,960]{1,0:T(1,128)} %bitcast.36, s32[960,1]{1,0:T(8,128)} %copy.21.panel_col, f32[8,256]{1,0:T(8,128)} %get-tuple-element.11.library, bf16[256,1600]{1,0:T(8,128)(2,1)} %cross.1.hidden, ...), custom_call_target="tpu_custom_call" | custom-call | tf_op jit(solution)/shard_map/decode/pallas_call | solution.py:716
  215.9 1.2 copy.31
  217.1 2.1 copy.32
  219.2 1.8 copy.33
  (2 shorter events, 0.1 us)
Async XLA Ops:
  55.8 2.6 %copy-start = (bf16[2,50,1600]{2,0,1:T(2,128)(2,1)S(1)}, bf16[2,50,1600]{2,0,1:T(2,128)(2,1)}, u32[]{:S(2)}) copy-start(bf16[2,50,1600]{2,0,1:T(2,128)(2,1)} %param.15) | copy-start | bytes 960004
  108.7 2.5 %copy-start.1 = (bf16[2,50,1600]{2,0,1:T(2,128)(2,1)S(1)}, bf16[2,50,1600]{2,0,1:T(2,128)(2,1)}, u32[]{:S(2)}) copy-start(bf16[2,50,1600]{2,0,1:T(2,128)(2,1)} %param.17) | copy-start | bytes 960004
  112.1 41.9 %copy-start.2 = (s32[960]{0:T(1024)S(1)}, s32[960]{0:T(1024)}, u32[]{:S(2)}) copy-start(s32[960]{0:T(1024)} %param.11) | copy-start | bytes 11524

commit v2 on v1

--- a/solution.py
+++ b/solution.py
@@ -236,10 +236,33 @@
             copy.wait_send()
 
 
-def run_gather(gathers):
-    for step in ("start", "second", "third", "finish", "drain"):
-        for gather in gathers:
-            getattr(gather, step)()
+class Direct:
+    def __init__(self, place, block, send, recv, index):
+        p = place
+        chip = p.chip(p.y, p.x)
+        own = block(p.g)
+        self.out, self.pair = [], []
+        for k in range(NCHIP):
+            to, frm = lax.rem(chip + k, NCHIP) * 2 + p.core, lax.rem(chip + NCHIP - k, NCHIP) * 2 + p.core
+            ref = block(frm)
+            if k:
+                self.out.append(remote(own, own, send.at[index, k], recv.at[index, k], "gene", to))
+            self.pair.append(remote(ref, ref, send.at[index, 7 + k if k else 0], recv.at[index, 7 + k if k else 0], "gene", p.other_core))
+
+    def start(self):
+        for copy in self.out + self.pair[:1]:
+            copy.start()
+
+    def finish(self):
+        for k in range(1, NCHIP):
+            self.out[k - 1].wait_recv()
+            self.pair[k].start()
+        for copy in self.pair:
+            copy.wait_recv()
+
+    def drain(self):
+        for copy in self.out + self.pair:
+            copy.wait_send()
 
 
 class Swap:
@@ -326,14 +349,13 @@
     return jnp.dot(jnp.concatenate([high, low], axis=1), ones, preferred_element_type=F32)
 
 
-def heads_of(normed, w_qkv, query, keys, values, head):
-    for m in range(NM):
-        qkv = lax.dot_general(normed[m], w_qkv[...], DN_T, preferred_element_type=F32)
-        for at, ref in ((0, query), (1, keys)):
-            part = qkv[:, at * 128:(at + 1) * 128]
-            mean = half_sum(part * part) / head
-            ref[m] = (part * lax.rsqrt(jnp.maximum(mean, FLOOR))).astype(BF16)
-        values[m] = qkv[:, 256:384].astype(BF16)
+def heads_of(m, normed, w_qkv, query, keys, values, head):
+    qkv = lax.dot_general(normed[m], w_qkv[...], DN_T, preferred_element_type=F32)
+    for at, ref in ((0, query), (1, keys)):
+        part = qkv[:, at * 128:(at + 1) * 128]
+        mean = half_sum(part * part) / head
+        ref[m] = (part * lax.rsqrt(jnp.maximum(mean, FLOOR))).astype(BF16)
+    values[m] = qkv[:, 256:384].astype(BF16)
 
 
 def within_mix(m, query, keys, values, head):
@@ -368,7 +390,8 @@
         Gather(place, lambda o, m=m: normed.at[m, pl.ds(pl.multiple_of(o * ROWS, ROWS), ROWS), :], a_send, a_recv, m)
         for m in range(NM)
     ]
-    heads_of(normed_in, w_qkv, query, keys, values, head)
+    for m in range(NM):
+        heads_of(m, normed_in, w_qkv, query, keys, values, head)
 
     def produce(m):
         mixed = within_mix(m, query, keys, values, head)
@@ -393,17 +416,17 @@
     place = Place()
     width = resid.shape[-1]
     cells = hidden.shape[0]
-    greet(near(place))
+    greet(everyone(place))
     scatter = Scatter(place, refs)
-    gather = Gather(
+    gather = Direct(
         place, lambda o: hidden.at[pl.ds(pl.multiple_of(o * ROWS, ROWS), ROWS), :], a_send, a_recv, 0
     )
-    heads_of(normed_in, w_qkv, query, keys, values, head)
     row = jnp.broadcast_to(groups[...].astype(F32), (cells, cells))
     same = row == row.T
     pool = []
 
     def produce(m):
+        heads_of(m, normed_in, w_qkv, query, keys, values, head)
         mixed = cross_mix(m, query, keys, values, same, head)
         out = jnp.dot(mixed, w_out[...], preferred_element_type=F32)
         scatter.part[m] = out.astype(BF16).reshape(NCHIP, 2, ROWS, width)
@@ -415,7 +438,9 @@
     run_scatter(scatter, produce, consume)
     pooled = (pool[0] + pool[1] + pool[2] + pool[3]) * (1.0 / NM)
     hidden[pl.ds(pl.multiple_of(place.g * ROWS, ROWS), ROWS), :] = rms(pooled).astype(BF16)
-    run_gather([gather])
+    gather.start()
+    gather.finish()
+    gather.drain()
     scatter.drain()
 
 
@@ -466,6 +491,27 @@
 
     def drain(self):
         for copy in self.c:
+            copy.wait_send()
+
+
+class GroupDirect:
+    def __init__(self, r, block, send, recv):
+        self.out, self.into = [], []
+        for k in range(1, NR):
+            to, frm = lax.rem(r + k, NR), lax.rem(r + NR - k, NR)
+            self.out.append(remote(block(r), block(r), send.at[k], recv.at[k], "grp", to))
+            self.into.append(remote(block(r), block(frm), send.at[k], recv.at[k], "grp", frm))
+
+    def start(self):
+        for copy in self.out:
+            copy.start()
+
+    def finish(self):
+        for copy in self.into:
+            copy.wait_recv()
+
+    def drain(self):
+        for copy in self.out:
             copy.wait_send()
 
 
@@ -506,9 +552,9 @@
 def decode_kernel(
     genes_all, cells_all, panel_count,
     counts, panel_row, panel_col, library, hidden, w_mean, w_disp,
-    cell_loss, grad_mean, grad_disp,
-    tile, slots, back, piece, columns, field, panel_part, loss, gradient, disp_block,
-    s_send, s_recv, h_send, h_recv, v_send, v_recv, f_send, f_recv, o_send, o_recv,
+    cell_loss, gradient, disp_block,
+    tile, slots, back, piece, columns, field, panel_part, loss,
+    s_send, s_recv, h_send, h_recv, v_send, v_recv, f_send, f_recv, d_send, d_recv, o_send, o_recv,
 ):
     place = Place()
     r = lax.axis_index("grp")
@@ -551,9 +597,8 @@
     field_gather = [
         GroupGather(r, lambda o, p=p: field.at[o, pl.ds(p * step, step), :], f_send, f_recv, p) for p in range(parts)
     ]
-    field_gather.append(
-        GroupGather(r, lambda o: field.at[o, pl.ds(genes, panel_count), :], f_send, f_recv, parts)
-    )
+    disp_gather = GroupDirect(r, lambda o: field.at[o, pl.ds(genes, panel_count), :], d_send, d_recv)
+    spread = GroupDirect(r, lambda o: disp_block.at[o], o_send, o_recv)
 
     def decode(p):
         at = pl.ds(p * step, step)
@@ -584,8 +629,6 @@
     field_gather[0].second()
     decode(2)
     v_gather.third()
-    field_gather[0].third()
-    field_gather[1].second()
     decode(3)
 
     row = lax.broadcasted_iota(jnp.int32, (128, cells), 0)
@@ -594,26 +637,25 @@
     first = Swap(place, lambda t: tile.at[t], slots, s_send, s_recv, 0)
     first.start()
     slots[place.g] = tile[place.g]
-    v_gather.finish()
-    field_gather[1].third()
-    field_gather[2].second()
+    field_gather[0].third()
+    field_gather[1].second()
     first.finish()
     summed = total_of(slots)
     cell_loss[...] = summed[4:5] / genes_all
     back[place.g] = summed
     second = Swap(place, lambda t: back.at[place.g], back, s_send, s_recv, 1)
     second.start()
-    field_gather[2].third()
-    field_gather[3].second()
+    v_gather.finish()
+    field_gather[1].third()
     second.finish()
     d_panel = jnp.concatenate([back[k, 0:4] for k in range(NG)], axis=0)
     tail = jnp.exp(-jnp.abs(disp))
     d_disp = d_panel * (jnp.where(disp >= 0, 1.0, tail) / (1.0 + tail)) * norm_scale
     field[r, pl.ds(genes, panel_count), :] = d_disp.astype(BF16)
-    field_gather[parts].start()
-    field_gather[3].third()
-    field_gather[parts].second()
-    field_gather[parts].third()
+    disp_gather.start()
+    field_gather[2].second()
+    field_gather[2].third()
+    field_gather[3].second()
 
     def contract(at, size):
         total = jnp.zeros((size, columns.shape[2]), F32)
@@ -621,28 +663,26 @@
             total = total + jnp.dot(field[k, pl.ds(at, size), :], columns[k], preferred_element_type=F32)
         return total
 
-    field_gather[parts].finish()
-    part = contract(genes, panel_count)
-    disp_block[r] = part
-    spread, arrive = [], []
-    for k in range(1, NR):
-        to, frm = lax.rem(r + k, NR), lax.rem(r + NR - k, NR)
-        spread.append(remote(disp_block.at[r], disp_block.at[r], o_send.at[k], o_recv.at[r], "grp", to))
-        arrive.append(remote(disp_block.at[frm], disp_block.at[frm], o_send.at[k], o_recv.at[frm], "grp", frm))
-    for copy in spread:
-        copy.start()
+    disp_gather.finish()
+    disp_block[r] = contract(genes, panel_count)
+    spread.start()
+    field_gather[3].third()
     for p in range(parts):
         field_gather[p].finish()
         gradient[pl.ds(p * step, step), :] = contract(p * step, step)
+    spread.finish()
+    for copy in out:
+        copy.wait_send()
+    for one in [v_gather, first, second, disp_gather, spread] + field_gather:
+        one.drain()
+
+
+def finish_kernel(gradient, disp_block, loss, cell_loss, grad_mean, grad_disp):
+    share = grad_mean.shape[0]
+    cell_loss[...] = loss[...]
     grad_mean[...] = gradient[...].T[0:share]
-    for copy in arrive:
-        copy.wait_recv()
     for k in range(NR):
         grad_disp[:, k * share:(k + 1) * share] = disp_block[k, :, 0:share]
-    for copy in out + spread:
-        copy.wait_send()
-    for one in [v_gather, first, second] + field_gather:
-        one.drain()
 
 
 def whole():
@@ -713,13 +753,13 @@
         scratch_shapes=heads_scratch + gather_sems + scatter,
         compiler_params=params(2),
     )(normed, resid, head_weights(w_qkv_cross), out_weights(w_out_cross), membership)
-    cell_loss, grad_mean, grad_disp = pl.pallas_call(
+    cell_loss, gradient, disp_block = pl.pallas_call(
         functools.partial(decode_kernel, genes_all, cells_all, panel_count),
         name="decode",
         out_shape=(
             jax.ShapeDtypeStruct((1, cells), F32),
-            jax.ShapeDtypeStruct((width // NR, genes), F32),
-            jax.ShapeDtypeStruct((panel_count, width), F32),
+            jax.ShapeDtypeStruct((genes, 256), F32),
+            jax.ShapeDtypeStruct((NR, panel_count, 256), F32),
         ),
         in_specs=[whole()] * 7,
         out_specs=(whole(), whole(), whole()),
@@ -732,20 +772,31 @@
             pltpu.VMEM((NR, genes + panel_count, cells), BF16),
             pltpu.VMEM((128, cells), F32),
             pltpu.VMEM((1, cells), F32),
-            pltpu.VMEM((genes, 256), F32),
-            pltpu.VMEM((NR, panel_count, 256), F32),
         ] + swap_sems + [
             pltpu.SemaphoreType.DMA((NR,)),
             pltpu.SemaphoreType.DMA((NR,)),
             pltpu.SemaphoreType.DMA((1, Gather.SLOTS)),
             pltpu.SemaphoreType.DMA((1, Gather.SLOTS)),
-            pltpu.SemaphoreType.DMA((5, GroupGather.SLOTS)),
-            pltpu.SemaphoreType.DMA((5, GroupGather.SLOTS)),
+            pltpu.SemaphoreType.DMA((4, GroupGather.SLOTS)),
+            pltpu.SemaphoreType.DMA((4, GroupGather.SLOTS)),
+            pltpu.SemaphoreType.DMA((NR,)),
+            pltpu.SemaphoreType.DMA((NR,)),
             pltpu.SemaphoreType.DMA((NR,)),
             pltpu.SemaphoreType.DMA((NR,)),
         ],
         compiler_params=params(3),
     )(counts_t, panels[None, :], panels[:, None], library, hidden, w_mean.T, w_disp.T)
+    cell_loss, grad_mean, grad_disp = pl.pallas_call(
+        finish_kernel,
+        name="finish",
+        out_shape=(
+            jax.ShapeDtypeStruct((1, cells), F32),
+            jax.ShapeDtypeStruct((width // NR, genes), F32),
+            jax.ShapeDtypeStruct((panel_count, width), F32),
+        ),
+        in_specs=[whole()] * 3,
+        out_specs=(whole(), whole(), whole()),
+    )(gradient, disp_block, cell_loss)
     return cell_loss[0], grad_mean, grad_disp.T
 
 

time: 225 us -> 213 us (0.947)
  local copies, waits for them, and re-layouts: 12.9 us -> 7.74 us
  Pallas kernels: 207 us -> 202 us
    pallas_call x1, Pallas kernels: 60.8 us -> 55.4 us  [shards(): pl.pallas_call(functools.partial(decode_kernel, genes_all, cells_all, pan...]
    unnamed x11 -> x8, local copies, waits for them, and re-layouts: 5.24 us -> 0.1 us
    pallas_call x1, Pallas kernels: 41.9 us -> 38.8 us  [shards(): pl.pallas_call(functools.partial(cross_kernel, head), name='cross', out_s...]
    pallas_call x0 -> x1, Pallas kernels: none -> 2.74 us  [shards(): pl.pallas_call(finish_kernel, name='finish', out_shape=(jax.ShapeDtypeStr...]
where the time goes in v2:
time: 213 us; the launch traced here: 210 us
  Pallas kernels  202 us (95%)
  local copies, waits for them, and re-layouts  7.74 us (4%)
    pallas_call x1, Pallas kernels, shards(): pl.pallas_call(functools.partial(decode_kernel, genes_all, cells_all, pan...  55.4 us
    pallas_call x1, Pallas kernels, shards(): pl.pallas_call(encode_kernel, name='encode', out_shape=(block, mine, jax....  55.2 us
    pallas_call x1, Pallas kernels, shards(): pl.pallas_call(functools.partial(within_kernel, head), name='within', out...  49.5 us
    pallas_call x1, Pallas kernels, shards(): pl.pallas_call(functools.partial(cross_kernel, head), name='cross', out_s...  38.8 us

profile of v2, /device:TPU:1, one launch (start us, length us, event | category | flops | bytes accessed | tf_op | source)
XLA Modules:
  0.0 210.2 jit_solution(3373722522731544639)
XLA Ops:
  0.6 55.2 %encode.1 = (bf16[4,256,1600]{2,1,0:T(8,128)(2,1)}, f32[4,16,1600]{2,1,0:T(8,128)}, f32[8,256]{1,0:T(8,128)}) custom-call(s32[960,256]{1,0:T(8,128)} %bitcast.27, bf16[960,6400]{1,0:T(8,128)(2,1)} %w_hbm.1), custom_call_target="tpu_custom_call" | custom-call | tf_op jit(solution)/shard_map/encode/pallas_call | solution.py:722
  55.8 0.0 copy-start
  55.9 1.4 copy.27
  57.2 1.2 pad.14
  58.4 0.0 copy-done
  58.4 0.8 pad.15.clone
  59.2 49.5 %within.1 = (bf16[4,256,1600]{2,1,0:T(8,128)(2,1)}, f32[4,16,1600]{2,1,0:T(8,128)}) custom-call(bf16[4,256,1600]{2,1,0:T(8,128)(2,1)} %get-tuple-element.15.normed_in, f32[4,16,1600]{2,1,0:T(8,128)} %get-tuple-element.16.tokens, bf16[384,1600]{1,0:T(8,128)(2,1)} %bitcast.23, bf16[128,1600]{1,0:T(8,128)(2,1)} %bitcast.30), custom_call_target="tpu_custom_call" | custom-call | tf_op jit(solution)/shard_map/within/pallas_call | solution.py:738
  108.7 0.0 copy-start.1
  108.7 1.4 copy.26
  110.1 1.2 pad.16
  111.3 0.0 copy-done.1
  111.3 0.8 pad.17.clone
  112.1 0.0 copy-start.2
  112.1 38.8 %cross.1.hidden = bf16[256,1600]{1,0:T(8,128)(2,1)} custom-call(bf16[4,256,1600]{2,1,0:T(8,128)(2,1)} %get-tuple-element.17.normed_in, f32[4,16,1600]{2,1,0:T(8,128)} %get-tuple-element.18.resid, bf16[384,1600]{1,0:T(8,128)(2,1)} %bitcast.24, bf16[128,1600]{1,0:T(8,128)(2,1)} %bitcast.31, s32[1,256]{1,0:T(1,128)} %groups.1), custom_call_target="tpu_custom_call" | custom-call | tf_op jit(solution)/shard_map/cross/pallas_call | solution.py:747
  151.0 0.0 copy-done.2
  151.0 1.0 copy.21.panel_col
  152.0 55.4 %decode.1 = (f32[1,256]{1,0:T(1,128)}, f32[960,256]{1,0:T(8,128)}, f32[8,64,256]{2,1,0:T(8,128)}) custom-call(s32[960,256]{1,0:T(8,128)} %bitcast.28, s32[1,960]{1,0:T(1,128)} %bitcast.35, s32[960,1]{1,0:T(8,128)} %copy.21.panel_col, f32[8,256]{1,0:T(8,128)} %get-tuple-element.14.library, bf16[256,1600]{1,0:T(8,128)(2,1)} %cross.1.hidden, ...), custom_call_target="tpu_custom_call" | custom-call | tf_op jit(solution)/shard_map/decode/pallas_call | solution.py:756
  207.4 2.7 %finish.1 = (f32[1,256]{1,0:T(1,128)}, f32[200,960]{1,0:T(8,128)}, f32[64,1600]{1,0:T(8,128)}) custom-call(f32[960,256]{1,0:T(8,128)} %get-tuple-element.19.gradient, f32[8,64,256]{2,1,0:T(8,128)} %get-tuple-element.20.disp_block, f32[1,256]{1,0:T(1,128)} %get-tuple-element.21.loss), custom_call_target="tpu_custom_call" | custom-call | tf_op jit(solution)/shard_map/finish/pallas_call | solution.py:789
  (2 shorter events, 0.1 us)
Async XLA Ops:
  55.8 2.6 %copy-start = (bf16[2,50,1600]{2,0,1:T(2,128)(2,1)S(1)}, bf16[2,50,1600]{2,0,1:T(2,128)(2,1)}, u32[]{:S(2)}) copy-start(bf16[2,50,1600]{2,0,1:T(2,128)(2,1)} %param.15) | copy-start | bytes 960004
  108.7 2.5 %copy-start.1 = (bf16[2,50,1600]{2,0,1:T(2,128)(2,1)S(1)}, bf16[2,50,1600]{2,0,1:T(2,128)(2,1)}, u32[]{:S(2)}) copy-start(bf16[2,50,1600]{2,0,1:T(2,128)(2,1)} %param.17) | copy-start | bytes 960004
  112.1 38.9 %copy-start.2 = (s32[960]{0:T(1024)S(1)}, s32[960]{0:T(1024)}, u32[]{:S(2)}) copy-start(s32[960]{0:T(1024)} %param.11) | copy-start | bytes 11524

commit v3 on v2

--- a/solution.py
+++ b/solution.py
@@ -63,10 +63,6 @@
     pl.semaphore_wait(barrier, len(axis_peers))
 
 
-def near(place):
-    return [("gene", t) for t in (place.right, place.left, place.other_y, place.other_core)]
-
-
 def everyone(place):
     return [("gene", lax.rem(place.g + k, NG)) for k in range(1, NG)]
 
@@ -79,8 +75,6 @@
     @staticmethod
     def scratch(width):
         return [
-            pltpu.VMEM((NM, NCHIP, 2, ROWS, width), BF16),
-            pltpu.VMEM((NM, NCHIP, ROWS, width), BF16),
             pltpu.VMEM((NM, NCHIP, ROWS, width), BF16),
             pltpu.VMEM((NM, 3, ROWS, width), BF16),
             pltpu.VMEM((NM, 3, ROWS, width), BF16),
@@ -88,66 +82,55 @@
             pltpu.VMEM((NM, ROWS, width), BF16),
             pltpu.VMEM((NM, ROWS, width), BF16),
             pltpu.VMEM((NM, ROWS, width), F32),
-            pltpu.SemaphoreType.DMA((NM, 8)),
-            pltpu.SemaphoreType.DMA((NM, 8)),
+            pltpu.SemaphoreType.DMA((NM, 7)),
+            pltpu.SemaphoreType.DMA((NM, 7)),
         ]
 
-    COUNT = 11
-
     def __init__(self, place, refs):
-        (self.part, self.pair, self.chip, self.from_left, self.from_right, self.relay,
-         self.y_out, self.y_in, self.mine, self.send, self.recv) = refs
+        (self.chip, self.from_left, self.from_right, self.relay, self.y_out, self.y_in, self.mine, send, recv) = refs
         p = self.place = place
-        x, y = p.x, p.y
         ahead, behind, across = p.shift(1), p.shift(3), p.shift(2)
         self.copies = []
         for m in range(NM):
             def go(slot, src, dst, to):
-                return remote(src, dst, self.send.at[m, slot], self.recv.at[m, slot], "gene", to)
+                return remote(src, dst, send.at[m, slot], recv.at[m, slot], "gene", to)
             self.copies.append([
-                go(0, self.part.at[m, :, 1 - p.core], self.pair.at[m], p.other_core),
-                go(1, self.chip.at[m, p.chip(0, across)], self.from_left.at[m, 0], p.right),
-                go(2, self.chip.at[m, p.chip(1, across)], self.from_right.at[m, 0], p.left),
-                go(3, self.chip.at[m, p.chip(1, ahead)], self.from_left.at[m, 2], p.right),
-                go(4, self.chip.at[m, p.chip(0, behind)], self.from_right.at[m, 2], p.left),
-                go(5, self.relay.at[m, 0], self.from_left.at[m, 1], p.right),
-                go(6, self.relay.at[m, 1], self.from_right.at[m, 1], p.left),
-                go(7, self.y_out.at[m], self.y_in.at[m], p.other_y),
+                go(0, self.chip.at[m, p.chip(0, across)], self.from_left.at[m, 0], p.right),
+                go(1, self.chip.at[m, p.chip(1, across)], self.from_right.at[m, 0], p.left),
+                go(2, self.chip.at[m, p.chip(1, ahead)], self.from_left.at[m, 2], p.right),
+                go(3, self.chip.at[m, p.chip(0, behind)], self.from_right.at[m, 2], p.left),
+                go(4, self.relay.at[m, 0], self.from_left.at[m, 1], p.right),
+                go(5, self.relay.at[m, 1], self.from_right.at[m, 1], p.left),
+                go(6, self.y_out.at[m], self.y_in.at[m], p.other_y),
             ])
 
-    def give(self, m):
-        self.copies[m][0].start()
-
     def spread(self, m):
-        self.copies[m][0].wait_recv()
-        for q in range(NCHIP):
-            self.chip[m, q] = (self.part[m, q, self.place.core].astype(F32) + self.pair[m, q].astype(F32)).astype(BF16)
-        for k in (1, 2, 3, 4):
+        for k in (0, 1, 2, 3):
             self.copies[m][k].start()
 
     def forward(self, m):
         p = self.place
-        self.copies[m][1].wait_recv()
+        self.copies[m][0].wait_recv()
         self.relay[m, 0] = (
             self.chip[m, p.chip(0, p.shift(1))].astype(F32) + self.from_left[m, 0].astype(F32)
         ).astype(BF16)
-        self.copies[m][5].start()
-        self.copies[m][2].wait_recv()
+        self.copies[m][4].start()
+        self.copies[m][1].wait_recv()
         self.relay[m, 1] = (
             self.chip[m, p.chip(1, p.shift(3))].astype(F32) + self.from_right[m, 0].astype(F32)
         ).astype(BF16)
-        self.copies[m][6].start()
+        self.copies[m][5].start()
 
     def cross(self, m):
         p = self.place
-        for k in (3, 4, 5, 6):
+        for k in (2, 3, 4, 5):
             self.copies[m][k].wait_recv()
         self.y_out[m] = (
             self.chip[m, p.chip(1 - p.y, p.x)].astype(F32)
             + self.from_left[m, 2 - p.y].astype(F32)
             + self.from_right[m, 1 + p.y].astype(F32)
         ).astype(BF16)
-        self.copies[m][7].start()
+        self.copies[m][6].start()
         self.mine[m] = (
             self.chip[m, p.chip(p.y, p.x)].astype(F32)
             + self.from_left[m, 1 + p.y].astype(F32)
@@ -155,7 +138,7 @@
         )
 
     def take(self, m):
-        self.copies[m][7].wait_recv()
+        self.copies[m][6].wait_recv()
         return self.mine[m] + self.y_in[m].astype(F32)
 
     def drain(self):
@@ -164,72 +147,55 @@
                 copy.wait_send()
 
 
-def run_scatter(scatter, produce, consume):
-    steps = [produce, scatter.spread, scatter.forward, scatter.cross, consume]
-    for t in range(NM + len(steps) - 1):
+def run_pipeline(steps, count=NM):
+    for t in range(count + len(steps) - 1):
         for lag, step in enumerate(steps):
-            if 0 <= t - lag < NM:
+            if 0 <= t - lag < count:
                 step(t - lag)
 
 
 class Gather:
-    SLOTS = 15
+    SLOTS = 7
 
     def __init__(self, place, block, send, recv, index):
         p = place
         ahead, behind, across = p.shift(1), p.shift(3), p.shift(2)
-        y, z, c, x = p.y, 1 - p.y, p.core, p.x
+        y, z, x = p.y, 1 - p.y, p.x
 
         def go(slot, owner, to):
             ref = block(owner)
             return remote(ref, ref, send.at[index, slot], recv.at[index, slot], "gene", to)
 
-        own, paired = p.at(y, x, c), p.at(z, x, c)
-        held = [own, paired, p.at(y, behind, c), p.at(y, ahead, c), p.at(z, behind, c), p.at(z, ahead, c),
-                p.at(y, across, c), p.at(z, across, c)]
-        self.copies = [
+        own, paired = p.chip(y, x), p.chip(z, x)
+        self.c = [
             go(0, own, p.other_y),
             go(1, own, p.right),
             go(2, own, p.left),
             go(3, paired, p.right),
             go(4, paired, p.left),
-            go(5, held[2], p.right),
-            go(6, held[5], p.left),
-        ] + [go(7 + k, held[k], p.other_core) for k in range(8)]
-        self.c = self.copies
+            go(5, p.chip(y, behind), p.right),
+            go(6, p.chip(z, ahead), p.left),
+        ]
 
     def start(self):
-        for k in (1, 2, 0, 7):
+        for k in (1, 2, 0):
             self.c[k].start()
 
     def second(self):
         c = self.c
         c[1].wait_recv()
         c[5].start()
-        c[9].start()
         c[0].wait_recv()
         c[3].start()
         c[4].start()
-        c[8].start()
-        c[2].wait_recv()
-        c[10].start()
 
     def third(self):
-        c = self.c
-        c[4].wait_recv()
-        c[6].start()
-        c[12].start()
-        c[3].wait_recv()
-        c[11].start()
+        self.c[4].wait_recv()
+        self.c[6].start()
 
     def finish(self):
-        c = self.c
-        c[5].wait_recv()
-        c[13].start()
-        c[6].wait_recv()
-        c[14].start()
-        for k in range(7, 15):
-            c[k].wait_recv()
+        for k in (2, 3, 5, 6):
+            self.c[k].wait_recv()
 
     def drain(self):
         for copy in self.c:
@@ -293,155 +259,259 @@
     return total
 
 
-def encode_kernel(counts, w_hbm, normed, tokens, library, scaled, weights, tile, slots, w_sem, s_send, s_recv, a_send, a_recv, *refs):
+def group_sum(values):
+    high = values.astype(BF16)
+    low = (values - high.astype(F32)).astype(BF16)
+    shape = (values.shape[1], values.shape[1])
+    row = lax.broadcasted_iota(jnp.int32, shape, 0) // 64
+    col = lax.broadcasted_iota(jnp.int32, shape, 1) // 64
+    ones = (row == col).astype(F32).astype(BF16)
+    return jnp.dot(high, ones, preferred_element_type=F32) + jnp.dot(low, ones, preferred_element_type=F32)
+
+
+def heads_of(rows, weights, head):
+    parts = [jnp.dot(rows, weights[k], preferred_element_type=F32) for k in range(3)]
+    for k in range(2):
+        mean = group_sum(parts[k] * parts[k]) / head
+        parts[k] = (parts[k] * lax.rsqrt(jnp.maximum(mean, FLOOR))).astype(BF16)
+    parts[2] = parts[2].astype(BF16)
+    return parts
+
+
+def turned(values, by):
+    if by == 0:
+        return values
+    row = lax.rem(lax.broadcasted_iota(jnp.int32, values.shape, 0), ROWS)
+    count = values.shape[0]
+    return jnp.where(row < by, pltpu.roll(values, count - ROWS + by, 0), pltpu.roll(values, by, 0))
+
+
+def within_mix(query, keys, values, head):
+    q, k, v = (part.astype(F32) for part in (query, keys, values))
+    count = q.shape[0]
+    scores = group_sum(jnp.concatenate([q * turned(k, 4 * d) for d in range(NM)], axis=0))
+    weights = [jnp.exp(scores[d * count:(d + 1) * count] * head ** (-0.5)) for d in range(NM)]
+    total = weights[0] + weights[1] + weights[2] + weights[3]
+    mixed = None
+    for d in range(NM):
+        term = (weights[d] / total).astype(BF16).astype(F32) * turned(v, 4 * d)
+        mixed = term if mixed is None else mixed + term
+    return mixed.astype(BF16)
+
+
+def cross_mix(query, keys, values, same, head):
+    lane = lax.broadcasted_iota(jnp.int32, query.shape, 1) // 64
+    q = query.astype(F32)
+    mixed = jnp.zeros(query.shape, F32)
+    for h in range(query.shape[1] // 64):
+        one = jnp.where(lane == h, q, 0.0).astype(BF16)
+        scores = lax.dot_general(one, keys, DN_T, preferred_element_type=F32) * head ** (-0.5)
+        weights = jnp.where(same, jnp.exp(scores), 0.0)
+        probs = (weights / jnp.sum(weights, axis=-1, keepdims=True)).astype(BF16)
+        mixed = jnp.where(lane == h, jnp.dot(probs, values, preferred_element_type=F32), mixed)
+    return mixed.astype(BF16)
+
+
+def encoder_scratch(width, genes, cells, head):
+    half = cells // 2
+    raw = [pltpu.VMEM((3, 2, head, width), BF16), pltpu.VMEM((2, head, width), BF16)]
+    layer = [
+        pltpu.VMEM((3, width, 256), BF16),
+        pltpu.VMEM((256, width), BF16),
+        pltpu.VMEM((NM, NCHIP, ROWS, width), BF16),
+    ]
+    return (
+        [
+            pltpu.VMEM((cells, genes), BF16),
+            pltpu.VMEM((NM, genes, 1664), BF16),
+            pltpu.VMEM((8, cells), F32),
+            pltpu.VMEM((NG, 8, cells), F32),
+            pltpu.VMEM((NM, NCHIP, 2, ROWS, width), BF16),
+            pltpu.VMEM((NM, NCHIP, ROWS, width), BF16),
+            pltpu.VMEM((128, width), F32),
+            pltpu.VMEM((NM, ROWS, width), F32),
+            pltpu.VMEM((NM, ROWS, width), F32),
+            pltpu.VMEM((NM, 2, 2, half, 256), BF16),
+            pltpu.VMEM((NM, half, 256), BF16),
+            pltpu.VMEM((cells, 128), F32),
+            pltpu.SemaphoreType.DMA((NM + 4,)),
+        ]
+        + raw * 2
+        + layer * 2
+        + [pltpu.SemaphoreType.DMA((1, NG))] * 2
+        + [pltpu.SemaphoreType.DMA((NM,))] * 2
+        + [pltpu.SemaphoreType.DMA((NM,))] * 2
+        + [pltpu.SemaphoreType.DMA((NM, NM))] * 2
+        + [pltpu.SemaphoreType.DMA((2 * NM, Gather.SLOTS))] * 2
+        + [pltpu.SemaphoreType.DMA((1, 16))] * 2
+        + Scatter.scratch(width) * 3
+    )
+
+
+def encoder_kernel(head, counts, groups, w_hbm, q1_hbm, q2_hbm, o1_hbm, o2_hbm, hidden, library, *refs):
+    (scaled, w_proj, tile, slots, halves, pair, padded, tokens, resid, kv, queries, spot, load_sem) = refs[:13]
+    raws, layers = refs[13:17], refs[17:23]
+    (s_send, s_recv, w_send, w_recv, p_send, p_recv, k_send, k_recv, a_send, a_recv, d_send, d_recv) = refs[23:35]
+    sums = refs[35:]
     place = Place()
-    width = tokens.shape[-1]
-    wide = weights.shape[-1]
+    width = resid.shape[-1]
+    wide = w_proj.shape[-1]
+    core, here = place.core, place.chip(place.y, place.x)
+    scatter = [Scatter(place, sums[9 * k:9 * k + 9]) for k in range(3)]
+    weights, outs, blocks = layers[0::3], layers[1::3], layers[2::3]
+
     greet(everyone(place))
-    loads = [
-        pltpu.make_async_copy(w_hbm.at[:, pl.ds((m * width) // 128 * 128, wide)], weights.at[m], w_sem.at[m])
-        for m in range(NM)
-    ]
     tile[...] = jnp.broadcast_to(jnp.sum(counts[...].astype(F32), axis=0, keepdims=True), tile.shape)
     swap = Swap(place, lambda t: tile, slots, s_send, s_recv, 0)
     swap.start()
-    for load in loads:
+    small = [
+        pltpu.make_async_copy(src, dst, load_sem.at[NM + k])
+        for k, (src, dst) in enumerate(zip((q1_hbm, o1_hbm, q2_hbm, o2_hbm), raws))
+    ]
+    loads = [
+        pltpu.make_async_copy(w_hbm.at[:, pl.ds((m * width) // 128 * 128, wide)], w_proj.at[m], load_sem.at[m])
+        for m in range(NM)
+    ]
+    for load in small[:2] + loads + small[2:]:
         load.start()
     slots[place.g] = tile[...]
+
+    lanes = pl.ds(pl.multiple_of(core * 128, 128), 128)
+    share = []
+    for k in range(2):
+        share.append([
+            remote(weights[k].at[:, :, lanes], weights[k].at[:, :, lanes], w_send.at[2 * k], w_recv.at[2 * k], "gene", place.other_core),
+            remote(outs[k].at[lanes, :], outs[k].at[lanes, :], w_send.at[2 * k + 1], w_recv.at[2 * k + 1], "gene", place.other_core),
+        ])
+
+    def prepare(k):
+        padded[...] = jnp.zeros_like(padded)
+        small[2 * k].wait()
+        for a in range(3):
+            for h in range(2):
+                padded[64 * h:64 * h + head, :] = raws[2 * k][a, h].astype(F32)
+            weights[k][a, :, lanes] = padded[...].T.astype(BF16)
+        share[k][0].start()
+        small[2 * k + 1].wait()
+        for h in range(2):
+            padded[64 * h:64 * h + head, :] = raws[2 * k + 1][h].astype(F32)
+        outs[k][lanes, :] = padded[...].astype(BF16)
+        share[k][1].start()
+
+    prepare(0)
     swap.finish()
     total = 1.0 + total_of(slots)
     library[...] = total
-    factor = TARGET / total[0:1]
-    scaled[...] = jnp.log1p(counts[...].astype(F32) * factor).T.astype(BF16)
-    scatter = Scatter(place, refs)
-    gather = [
-        Gather(place, lambda o, m=m: normed.at[m, pl.ds(pl.multiple_of(o * ROWS, ROWS), ROWS), :], a_send, a_recv, m)
+    scaled[...] = jnp.log1p(counts[...].astype(F32) * (TARGET / total[0:1])).T.astype(BF16)
+
+    pairs = [
+        remote(halves.at[m, :, 1 - core], pair.at[m], p_send.at[m], p_recv.at[m], "gene", place.other_core)
         for m in range(NM)
     ]
 
-    def produce(m):
+    def project(m):
         loads[m].wait()
         skip = (m * width) % 128
-        out = jnp.dot(scaled[...], weights[m], preferred_element_type=F32)[:, skip:skip + width]
-        scatter.part[m] = out.astype(BF16).reshape(NCHIP, 2, ROWS, width)
-        scatter.give(m)
-
-    def consume(m):
-        value = scatter.take(m)
-        tokens[m] = value
-        normed[m, pl.ds(pl.multiple_of(place.g * ROWS, ROWS), ROWS), :] = rms(value).astype(BF16)
-        gather[m].start()
-
-    run_scatter(scatter, produce, consume)
-    for step in ("second", "third", "finish", "drain"):
-        for one in gather:
-            getattr(one, step)()
-    scatter.drain()
-    swap.drain()
-
-
-def half_sum(values):
-    high = values.astype(BF16)
-    low = (values - high.astype(F32)).astype(BF16)
-    row = lax.broadcasted_iota(jnp.int32, (256, 128), 0)
-    col = lax.broadcasted_iota(jnp.int32, (256, 128), 1)
-    ones = ((lax.rem(row, 128) // 64) == (col // 64)).astype(BF16)
-    return jnp.dot(jnp.concatenate([high, low], axis=1), ones, preferred_element_type=F32)
-
-
-def heads_of(m, normed, w_qkv, query, keys, values, head):
-    qkv = lax.dot_general(normed[m], w_qkv[...], DN_T, preferred_element_type=F32)
-    for at, ref in ((0, query), (1, keys)):
-        part = qkv[:, at * 128:(at + 1) * 128]
-        mean = half_sum(part * part) / head
-        ref[m] = (part * lax.rsqrt(jnp.maximum(mean, FLOOR))).astype(BF16)
-    values[m] = qkv[:, 256:384].astype(BF16)
-
-
-def within_mix(m, query, keys, values, head):
-    q = query[m].astype(F32)
-    weights = [jnp.exp(half_sum(q * keys[n].astype(F32)) * head ** (-0.5)) for n in range(NM)]
-    total = weights[0] + weights[1] + weights[2] + weights[3]
-    mixed = None
-    for n in range(NM):
-        term = (weights[n] / total).astype(BF16).astype(F32) * values[n].astype(F32)
-        mixed = term if mixed is None else mixed + term
-    return mixed.astype(BF16)
-
-
-def cross_mix(m, query, keys, values, same, head):
-    lane = lax.broadcasted_iota(jnp.int32, query.shape[1:], 1) // 64
-    out = []
-    for h in range(2):
-        q = jnp.where(lane == h, query[m].astype(F32), 0.0).astype(BF16)
-        scores = lax.dot_general(q, keys[m], DN_T, preferred_element_type=F32) * head ** (-0.5)
-        weights = jnp.where(same, jnp.exp(scores), 0.0)
-        probs = (weights / jnp.sum(weights, axis=-1, keepdims=True)).astype(BF16)
-        out.append(jnp.dot(probs, values[m], preferred_element_type=F32))
-    return jnp.where(lane == 0, out[0], out[1]).astype(BF16)
-
-
-def within_kernel(head, normed_in, tokens, w_qkv, w_out, normed, resid, query, keys, values, a_send, a_recv, *refs):
-    place = Place()
-    width = tokens.shape[-1]
-    greet(near(place))
-    scatter = Scatter(place, refs)
-    gather = [
-        Gather(place, lambda o, m=m: normed.at[m, pl.ds(pl.multiple_of(o * ROWS, ROWS), ROWS), :], a_send, a_recv, m)
+        out = jnp.dot(scaled[...], w_proj[m], preferred_element_type=F32)[:, skip:skip + width]
+        halves[m] = out.astype(BF16).reshape(NCHIP, 2, ROWS, width)
+        pairs[m].start()
+
+    def join(m):
+        pairs[m].wait_recv()
+        for q in range(NCHIP):
+            scatter[0].chip[m, q] = (halves[m, q, core].astype(F32) + pair[m, q].astype(F32)).astype(BF16)
+        scatter[0].spread(m)
+
+    def keep(m):
+        scatter[0].mine[m] = scatter[0].take(m)
+
+    run_pipeline([project, join, scatter[0].forward, scatter[0].cross, keep])
+
+    gathers = [
+        [Gather(place, lambda q, k=k, m=m: blocks[k].at[m, q], a_send, a_recv, k * NM + m) for m in range(NM)]
+        for k in range(2)
+    ]
+    for s in range(NM):
+        for m in range(NM):
+            tokens[s, 4 * m:4 * m + 4, :] = scatter[0].mine[m, 4 * s:4 * s + 4, :]
+        blocks[0][s, here] = rms(tokens[s]).astype(BF16)
+        gathers[0][s].start()
+
+    prepare(1)
+    cells = 2 * kv.shape[3]
+    at = lax.broadcasted_iota(jnp.int32, (cells, cells), 1)
+    source = 32 * (lax.rem(at, 128) // ROWS) + ROWS * (at // 128) + lax.rem(at, ROWS)
+    order = (lax.broadcasted_iota(jnp.int32, (cells, cells), 0) == source).astype(F32).astype(BF16)
+    row = jnp.dot(
+        jnp.broadcast_to(groups[...].astype(F32), (128, cells)).astype(BF16), order, preferred_element_type=F32
+    )
+    spot[...] = row.T
+    same = jnp.broadcast_to(spot[lanes, 0:1], (128, cells)) == row
+    for copy in share[0]:
+        copy.wait_recv()
+
+    def within(s):
+        gathers[0][s].finish()
+        rows = blocks[0][s].reshape(NCHIP * ROWS, width)
+        mixed = within_mix(*heads_of(rows, weights[0], head), head)
+        out = jnp.dot(mixed, outs[0][...], preferred_element_type=F32)
+        scatter[1].chip[s] = out.astype(BF16).reshape(NCHIP, ROWS, width)
+        scatter[1].spread(s)
+
+    def add_within(s):
+        tokens[s] = tokens[s] + scatter[1].take(s)
+
+    run_pipeline([
+        lambda s: gathers[0][s].second(), lambda s: gathers[0][s].third(), within,
+        scatter[1].forward, scatter[1].cross, add_within,
+    ])
+
+    for m in range(NM):
+        for s in range(NM):
+            resid[m, 4 * s:4 * s + 4, :] = tokens[s, 4 * m:4 * m + 4, :]
+        blocks[1][m, here] = rms(resid[m]).astype(BF16)
+        gathers[1][m].start()
+    for copy in share[1]:
+        copy.wait_recv()
+    trade = [
+        remote(kv.at[m, core], kv.at[m, core], k_send.at[m, 0], k_recv.at[m, 0], "gene", place.other_core)
         for m in range(NM)
     ]
-    for m in range(NM):
-        heads_of(m, normed_in, w_qkv, query, keys, values, head)
-
-    def produce(m):
-        mixed = within_mix(m, query, keys, values, head)
-        out = jnp.dot(mixed, w_out[...], preferred_element_type=F32)
-        scatter.part[m] = out.astype(BF16).reshape(NCHIP, 2, ROWS, width)
-        scatter.give(m)
-
-    def consume(m):
-        value = tokens[m] + scatter.take(m)
-        resid[m] = value
-        normed[m, pl.ds(pl.multiple_of(place.g * ROWS, ROWS), ROWS), :] = rms(value).astype(BF16)
-        gather[m].start()
-
-    run_scatter(scatter, produce, consume)
-    for step in ("second", "third", "finish", "drain"):
-        for one in gather:
-            getattr(one, step)()
-    scatter.drain()
-
-
-def cross_kernel(head, normed_in, resid, w_qkv, w_out, groups, hidden, query, keys, values, a_send, a_recv, *refs):
-    place = Place()
-    width = resid.shape[-1]
-    cells = hidden.shape[0]
-    greet(everyone(place))
-    scatter = Scatter(place, refs)
-    gather = Direct(
-        place, lambda o: hidden.at[pl.ds(pl.multiple_of(o * ROWS, ROWS), ROWS), :], a_send, a_recv, 0
+
+    def look(m):
+        gathers[1][m].finish()
+        rows = blocks[1][m].reshape(NCHIP * ROWS, width)
+        queries[m], kv[m, core, 0], kv[m, core, 1] = heads_of(rows, weights[1], head)
+        trade[m].start()
+
+    def attend(m):
+        trade[m].wait_recv()
+        keys = jnp.concatenate([kv[m, 0, 0], kv[m, 1, 0]], axis=0)
+        values = jnp.concatenate([kv[m, 0, 1], kv[m, 1, 1]], axis=0)
+        mixed = cross_mix(queries[m], keys, values, same, head)
+        out = jnp.dot(mixed, outs[1][...], preferred_element_type=F32)
+        scatter[2].chip[m] = out.astype(BF16).reshape(NCHIP, ROWS, width)
+        scatter[2].spread(m)
+
+    def add_cross(m):
+        resid[m] = resid[m] + scatter[2].take(m)
+
+    run_pipeline([
+        lambda m: gathers[1][m].second(), lambda m: gathers[1][m].third(), look, attend,
+        scatter[2].forward, scatter[2].cross, add_cross,
+    ])
+
+    pooled = (resid[0] + resid[1] + resid[2] + resid[3]) * (1.0 / NM)
+    hidden[pl.ds(pl.multiple_of(place.g * ROWS, ROWS), ROWS), :] = rms(pooled).astype(BF16)
+    last = Direct(
+        place, lambda o: hidden.at[pl.ds(pl.multiple_of(o * ROWS, ROWS), ROWS), :], d_send, d_recv, 0
     )
-    row = jnp.broadcast_to(groups[...].astype(F32), (cells, cells))
-    same = row == row.T
-    pool = []
-
-    def produce(m):
-        heads_of(m, normed_in, w_qkv, query, keys, values, head)
-        mixed = cross_mix(m, query, keys, values, same, head)
-        out = jnp.dot(mixed, w_out[...], preferred_element_type=F32)
-        scatter.part[m] = out.astype(BF16).reshape(NCHIP, 2, ROWS, width)
-        scatter.give(m)
-
-    def consume(m):
-        pool.append(resid[m] + scatter.take(m))
-
-    run_scatter(scatter, produce, consume)
-    pooled = (pool[0] + pool[1] + pool[2] + pool[3]) * (1.0 / NM)
-    hidden[pl.ds(pl.multiple_of(place.g * ROWS, ROWS), ROWS), :] = rms(pooled).astype(BF16)
-    gather.start()
-    gather.finish()
-    gather.drain()
-    scatter.drain()
+    last.start()
+    last.finish()
+    for one in scatter + gathers[0] + gathers[1] + [swap, last]:
+        one.drain()
+    for copy in share[0] + share[1] + pairs + trade:
+        copy.wait_send()
 
 
 class GroupGather:
@@ -487,6 +557,55 @@
 
     def finish(self):
         for k in (2, 3, 5, 6):
+            self.c[k].wait_recv()
+
+    def drain(self):
+        for copy in self.c:
+            copy.wait_send()
+
+
+class GroupGatherZ:
+    def __init__(self, r, block, send, recv, index, upward):
+        z, h = lax.rem(r, NZ), r // NZ
+        up, down, across = lax.rem(z + 1, NZ), lax.rem(z + 3, NZ), lax.rem(z + 2, NZ)
+        k = 1 - h
+        self.upward = upward
+
+        def at(a, b):
+            return a * NZ + b
+
+        def go(slot, owner, to):
+            ref = block(owner)
+            return remote(ref, ref, send.at[index, slot], recv.at[index, slot], "grp", to)
+
+        self.c = [
+            go(0, at(h, z), at(h, up)),
+            go(1, at(h, z), at(h, down)),
+            go(2, at(h, down), at(h, up)) if upward else go(2, at(h, up), at(h, down)),
+            go(3, at(h, z), at(k, z)),
+            go(4, at(h, down), at(k, z)),
+            go(5, at(h, up), at(k, z)),
+            go(6, at(h, across), at(k, z)),
+        ]
+
+    def start(self):
+        for k in (0, 1, 3):
+            self.c[k].start()
+
+    def second(self):
+        c = self.c
+        for k in (0, 1):
+            c[k].wait_recv()
+            if self.upward == (k == 0):
+                c[2].start()
+            c[4 + k].start()
+
+    def third(self):
+        self.c[2].wait_recv()
+        self.c[6].start()
+
+    def finish(self):
+        for k in (3, 4, 5, 6):
             self.c[k].wait_recv()
 
     def drain(self):
@@ -591,12 +710,15 @@
     panel_part[...] = jnp.zeros_like(panel_part)
     loss[...] = jnp.zeros_like(loss)
 
-    v_gather = Gather(
+    v_gather = Direct(
         place, lambda o: columns.at[:, pl.ds(pl.multiple_of(o * ROWS, ROWS), ROWS), :], v_send, v_recv, 0
     )
-    field_gather = [
-        GroupGather(r, lambda o, p=p: field.at[o, pl.ds(p * step, step), :], f_send, f_recv, p) for p in range(parts)
-    ]
+    field_gather = []
+    for p in range(parts):
+        block = lambda o, p=p: field.at[o, pl.ds(p * step, step), :]
+        field_gather.append(
+            GroupGatherZ(r, block, f_send, f_recv, p, p == 1) if p % 2 else GroupGather(r, block, f_send, f_recv, p)
+        )
     disp_gather = GroupDirect(r, lambda o: field.at[o, pl.ds(genes, panel_count), :], d_send, d_recv)
     spread = GroupDirect(r, lambda o: disp_block.at[o], o_send, o_recv)
 
@@ -625,10 +747,10 @@
         copy.wait_recv()
     v_gather.start()
     decode(1)
-    v_gather.second()
     field_gather[0].second()
     decode(2)
-    v_gather.third()
+    field_gather[1].second()
+    field_gather[0].third()
     decode(3)
 
     row = lax.broadcasted_iota(jnp.int32, (128, cells), 0)
@@ -637,8 +759,8 @@
     first = Swap(place, lambda t: tile.at[t], slots, s_send, s_recv, 0)
     first.start()
     slots[place.g] = tile[place.g]
-    field_gather[0].third()
-    field_gather[1].second()
+    field_gather[2].second()
+    field_gather[1].third()
     first.finish()
     summed = total_of(slots)
     cell_loss[...] = summed[4:5] / genes_all
@@ -646,16 +768,15 @@
     second = Swap(place, lambda t: back.at[place.g], back, s_send, s_recv, 1)
     second.start()
     v_gather.finish()
-    field_gather[1].third()
+    field_gather[2].third()
+    field_gather[3].second()
     second.finish()
     d_panel = jnp.concatenate([back[k, 0:4] for k in range(NG)], axis=0)
     tail = jnp.exp(-jnp.abs(disp))
     d_disp = d_panel * (jnp.where(disp >= 0, 1.0, tail) / (1.0 + tail)) * norm_scale
     field[r, pl.ds(genes, panel_count), :] = d_disp.astype(BF16)
     disp_gather.start()
-    field_gather[2].second()
-    field_gather[2].third()
-    field_gather[3].second()
+    field_gather[3].third()
 
     def contract(at, size):
         total = jnp.zeros((size, columns.shape[2]), F32)
@@ -663,13 +784,17 @@
             total = total + jnp.dot(field[k, pl.ds(at, size), :], columns[k], preferred_element_type=F32)
         return total
 
+    def gradient_of(p):
+        field_gather[p].finish()
+        gradient[pl.ds(p * step, step), :] = contract(p * step, step)
+
+    gradient_of(0)
+    gradient_of(1)
     disp_gather.finish()
     disp_block[r] = contract(genes, panel_count)
     spread.start()
-    field_gather[3].third()
-    for p in range(parts):
-        field_gather[p].finish()
-        gradient[pl.ds(p * step, step), :] = contract(p * step, step)
+    gradient_of(2)
+    gradient_of(3)
     spread.finish()
     for copy in out:
         copy.wait_send()
@@ -695,15 +820,8 @@
 
 def head_weights(w_qkv):
     width, heads, three = w_qkv.shape
-    turned = jnp.transpose(w_qkv, (2, 1, 0)).reshape(3, three // 3, heads, width)
-    turned = jnp.transpose(turned, (0, 2, 1, 3))
-    turned = jnp.pad(turned, ((0, 0), (0, 0), (0, 64 - three // 3), (0, 0)))
-    return turned.reshape(3 * heads * 64, width)
-
-
-def out_weights(w_out):
-    heads, head, width = w_out.shape
-    return jnp.pad(w_out, ((0, 0), (0, 64 - head), (0, 0))).reshape(heads * 64, width)
+    turned_w = jnp.transpose(w_qkv, (2, 1, 0)).reshape(3, three // 3, heads, width)
+    return jnp.transpose(turned_w, (0, 2, 1, 3))
 
 
 def shards(counts, panels, membership, w_proj, w_qkv_within, w_out_within, w_qkv_cross, w_out_cross, w_mean, w_disp):
@@ -714,45 +832,16 @@
     cells_all = cells * NR
     panel_count = w_disp.shape[1]
     counts_t = counts.T
-    scatter = Scatter.scratch(width)
-    gather_sems = [pltpu.SemaphoreType.DMA((NM, Gather.SLOTS))] * 2
     swap_sems = [pltpu.SemaphoreType.DMA((2, NG))] * 2
-    block = jax.ShapeDtypeStruct((NM, cells, width), BF16)
-    mine = jax.ShapeDtypeStruct((NM, ROWS, width), F32)
-    normed, tokens, library = pl.pallas_call(
-        encode_kernel,
-        name="encode",
-        out_shape=(block, mine, jax.ShapeDtypeStruct((8, cells), F32)),
-        in_specs=[whole(), pl.BlockSpec(memory_space=pl.ANY)],
-        out_specs=(whole(), whole(), whole()),
-        scratch_shapes=[
-            pltpu.VMEM((cells, genes), BF16),
-            pltpu.VMEM((NM, genes, 1664), BF16),
-            pltpu.VMEM((8, cells), F32),
-            pltpu.VMEM((NG, 8, cells), F32),
-            pltpu.SemaphoreType.DMA((NM,)),
-        ] + swap_sems + gather_sems + scatter,
+    hidden, library = pl.pallas_call(
+        functools.partial(encoder_kernel, head),
+        name="encoder",
+        out_shape=(jax.ShapeDtypeStruct((cells, width), BF16), jax.ShapeDtypeStruct((8, cells), F32)),
+        in_specs=[whole()] * 2 + [pl.BlockSpec(memory_space=pl.ANY)] * 5,
+        out_specs=(whole(), whole()),
+        scratch_shapes=encoder_scratch(width, genes, cells, head),
         compiler_params=params(0),
-    )(counts_t, w_proj)
-    heads_scratch = [pltpu.VMEM((NM, cells, 128), BF16)] * 3
-    normed, resid = pl.pallas_call(
-        functools.partial(within_kernel, head),
-        name="within",
-        out_shape=(block, mine),
-        in_specs=[whole()] * 4,
-        out_specs=(whole(), whole()),
-        scratch_shapes=heads_scratch + gather_sems + scatter,
-        compiler_params=params(1),
-    )(normed, tokens, head_weights(w_qkv_within), out_weights(w_out_within))
-    hidden = pl.pallas_call(
-        functools.partial(cross_kernel, head),
-        name="cross",
-        out_shape=jax.ShapeDtypeStruct((cells, width), BF16),
-        in_specs=[whole()] * 5,
-        out_specs=whole(),
-        scratch_shapes=heads_scratch + gather_sems + scatter,
-        compiler_params=params(2),
-    )(normed, resid, head_weights(w_qkv_cross), out_weights(w_out_cross), membership)
+    )(counts_t, membership, w_proj, head_weights(w_qkv_within), head_weights(w_qkv_cross), w_out_within, w_out_cross)
     cell_loss, gradient, disp_block = pl.pallas_call(
         functools.partial(decode_kernel, genes_all, cells_all, panel_count),
         name="decode",
@@ -775,8 +864,8 @@
         ] + swap_sems + [
             pltpu.SemaphoreType.DMA((NR,)),
             pltpu.SemaphoreType.DMA((NR,)),
-            pltpu.SemaphoreType.DMA((1, Gather.SLOTS)),
-            pltpu.SemaphoreType.DMA((1, Gather.SLOTS)),
+            pltpu.SemaphoreType.DMA((1, 16)),
+            pltpu.SemaphoreType.DMA((1, 16)),
             pltpu.SemaphoreType.DMA((4, GroupGather.SLOTS)),
             pltpu.SemaphoreType.DMA((4, GroupGather.SLOTS)),
             pltpu.SemaphoreType.DMA((NR,)),

time: 213 us -> 190 us (0.89); the launches traced: 210 us -> 190 us
  Pallas kernels: 202 us -> 183 us
    pallas_call x3 -> x1, Pallas kernels: 144 us -> 118 us  [shards(): pl.pallas_call(functools.partial(encoder_kernel, head), name='encoder', o...]
    pallas_call x1, Pallas kernels: 55.4 us -> 62.3 us  [shards(): pl.pallas_call(functools.partial(decode_kernel, genes_all, cells_all, pan...]
    pad x4 -> x0, local copies, waits for them, and re-layouts: 3.9 us -> none  [the longest x2 2.32 us: head_weights(): turned = jnp.pad(turned, ((0, 0), (0, 0), (0, 64 - three // 3), (0, 0)))]
    transpose x0 -> x1, local copies, waits for them, and re-layouts: none -> 3.2 us  [head_weights(): return jnp.transpose(turned_w, (0, 2, 1, 3))]
    reshape x2 -> x0, local copies, waits for them, and re-layouts: 2.74 us -> none  [head_weights(): jnp.transpose(w_qkv, (2, 1, 0)).reshape(3, three // 3, heads, width)]
where the time goes in v3:
time: 190 us
  Pallas kernels  183 us (96%)
  local copies, waits for them, and re-layouts  5.77 us (3%)
    pallas_call x1, Pallas kernels, shards(): pl.pallas_call(functools.partial(encoder_kernel, head), name='encoder', o...  118 us
    pallas_call x1, Pallas kernels, shards(): pl.pallas_call(functools.partial(decode_kernel, genes_all, cells_all, pan...  62.3 us

profile of v3, /device:TPU:1, one launch (start us, length us, event | category | flops | bytes accessed | tf_op | source)
XLA Modules:
  0.0 189.9 jit_solution(11261708667337350398)
XLA Ops:
  0.6 0.0 copy-start
  0.6 0.0 copy-start.1
  0.7 3.2 %copy_bitcast_fusion = (bf16[3,2,50,1600]{3,2,1,0:T(8,128)(2,1)}, bf16[3,2,50,1600]{3,2,1,0:T(8,128)(2,1)}) fusion(bf16[3,50,2,1600]{3,2,1,0:T(2,128)(2,1)} %bitcast.20, bf16[3,50,2,1600]{3,2,1,0:T(2,128)(2,1)} %bitcast.21), kind=kLoop, calls=%fused_computation | loop fusion | bytes 3840000 | tf_op jit(solution)/shard_map/transpose | solution.py:824
  3.8 0.0 copy-done
  3.9 0.8 copy.17.o1_hbm
  4.6 0.0 copy-done.1
  4.6 0.8 copy.18.o2_hbm
  5.4 0.0 copy-start.2
  5.4 118.4 %encoder.1 = (bf16[256,1600]{1,0:T(8,128)(2,1)}, f32[8,256]{1,0:T(8,128)}) custom-call(s32[960,256]{1,0:T(8,128)} %bitcast.17, s32[1,256]{1,0:T(1,128)} %groups.1, bf16[960,6400]{1,0:T(8,128)(2,1)} %w_hbm.1, bf16[3,2,50,1600]{3,2,1,0:T(8,128)(2,1)} %get-tuple-element.20.q1_hbm, bf16[3,2,50,1600]{3,2,1,0:T(8,128)(2,1)} %get-tuple-element.19.q2_hbm, ...), custom_call_target="tpu_custom_call" | custom-call | tf_op jit(solution)/shard_map/encoder/pallas_call | solution.py:836
  123.8 0.0 copy-done.2
  123.8 1.0 copy.19.panel_col
  124.8 62.3 %decode.1 = (f32[1,256]{1,0:T(1,128)}, f32[960,256]{1,0:T(8,128)}, f32[8,64,256]{2,1,0:T(8,128)}) custom-call(s32[960,256]{1,0:T(8,128)} %bitcast.18, s32[1,960]{1,0:T(1,128)} %bitcast.23, s32[960,1]{1,0:T(8,128)} %copy.19.panel_col, f32[8,256]{1,0:T(8,128)} %get-tuple-element.11.library, bf16[256,1600]{1,0:T(8,128)(2,1)} %get-tuple-element.12.hidden, ...), custom_call_target="tpu_custom_call" | custom-call | tf_op jit(solution)/shard_map/decode/pallas_call | solution.py:845
  187.1 2.7 %finish.1 = (f32[1,256]{1,0:T(1,128)}, f32[200,960]{1,0:T(8,128)}, f32[64,1600]{1,0:T(8,128)}) custom-call(f32[960,256]{1,0:T(8,128)} %get-tuple-element.13.gradient, f32[8,64,256]{2,1,0:T(8,128)} %get-tuple-element.14.disp_block, f32[1,256]{1,0:T(1,128)} %get-tuple-element.15.loss), custom_call_target="tpu_custom_call" | custom-call | tf_op jit(solution)/shard_map/finish/pallas_call | solution.py:878
Async XLA Ops:
  0.6 3.2 %copy-start = (bf16[2,50,1600]{2,0,1:T(2,128)(2,1)S(1)}, bf16[2,50,1600]{2,0,1:T(2,128)(2,1)}, u32[]{:S(2)}) copy-start(bf16[2,50,1600]{2,0,1:T(2,128)(2,1)} %param.15) | copy-start | bytes 960004
  0.6 4.0 %copy-start.1 = (bf16[2,50,1600]{2,0,1:T(2,128)(2,1)S(1)}, bf16[2,50,1600]{2,0,1:T(2,128)(2,1)}, u32[]{:S(2)}) copy-start(bf16[2,50,1600]{2,0,1:T(2,128)(2,1)} %param.17) | copy-start | bytes 960004
  5.4 118.4 %copy-start.2 = (s32[960]{0:T(1024)S(1)}, s32[960]{0:T(1024)}, u32[]{:S(2)}) copy-start(s32[960]{0:T(1024)} %param.11) | copy-start | bytes 11524

commit v4 on v3

--- a/solution.py
+++ b/solution.py
@@ -82,16 +82,23 @@
             pltpu.VMEM((NM, ROWS, width), BF16),
             pltpu.VMEM((NM, ROWS, width), BF16),
             pltpu.VMEM((NM, ROWS, width), F32),
+            pltpu.VMEM((2, NX, ROWS, width), BF16),
             pltpu.SemaphoreType.DMA((NM, 7)),
             pltpu.SemaphoreType.DMA((NM, 7)),
         ]
 
     def __init__(self, place, refs):
-        (self.chip, self.from_left, self.from_right, self.relay, self.y_out, self.y_in, self.mine, send, recv) = refs
+        (self.chip, self.from_left, self.from_right, self.relay, self.y_out, self.y_in, self.mine, four, send, recv) = refs
+        self.send, self.recv = send, recv
         p = self.place = place
         ahead, behind, across = p.shift(1), p.shift(3), p.shift(2)
-        self.copies = []
+        self.copies, self.turned = [], {}
         for m in range(NM):
+            if m % 2:
+                self.turned[m] = ScatterY(self, m, four.at[m // 2], 1 if m == 1 else -1)
+                self.copies.append(self.turned[m].c)
+                continue
+
             def go(slot, src, dst, to):
                 return remote(src, dst, send.at[m, slot], recv.at[m, slot], "gene", to)
             self.copies.append([
@@ -105,10 +112,14 @@
             ])
 
     def spread(self, m):
+        if m in self.turned:
+            return self.turned[m].spread()
         for k in (0, 1, 2, 3):
             self.copies[m][k].start()
 
     def forward(self, m):
+        if m in self.turned:
+            return self.turned[m].forward()
         p = self.place
         self.copies[m][0].wait_recv()
         self.relay[m, 0] = (
@@ -122,6 +133,8 @@
         self.copies[m][5].start()
 
     def cross(self, m):
+        if m in self.turned:
+            return self.turned[m].cross()
         p = self.place
         for k in (2, 3, 4, 5):
             self.copies[m][k].wait_recv()
@@ -138,6 +151,8 @@
         )
 
     def take(self, m):
+        if m in self.turned:
+            return self.turned[m].take()
         self.copies[m][6].wait_recv()
         return self.mine[m] + self.y_in[m].astype(F32)
 
@@ -145,6 +160,48 @@
         for row in self.copies:
             for copy in row:
                 copy.wait_send()
+
+
+class ScatterY:
+    def __init__(self, base, m, y_four, way):
+        p = base.place
+        self.base, self.m, self.four = base, m, y_four
+        to, back = (p.right, p.left) if way > 0 else (p.left, p.right)
+        ahead, behind = (p.shift(1), p.shift(3)) if way > 0 else (p.shift(3), p.shift(1))
+        self.order = (p.shift(2), behind, ahead)
+        self.outgoing = (base.relay.at[m, 0], base.relay.at[m, 1], base.y_out.at[m])
+        self.incoming = (base.from_left.at[m, 0], base.from_right.at[m, 0], base.from_left.at[m, 1])
+
+        def go(slot, src, dst, device):
+            return remote(src, dst, base.send.at[m, slot], base.recv.at[m, slot], "gene", device)
+
+        self.c = [go(0, base.chip.at[m, pl.ds((1 - p.y) * NX, NX)], y_four, p.other_y)] + [
+            go(1 + k, self.outgoing[k], self.incoming[k], (to, back, to)[k]) for k in range(3)
+        ]
+
+    def spread(self):
+        self.c[0].start()
+
+    def total(self, x):
+        p = self.base.place
+        return self.base.chip[self.m, p.chip(p.y, x)].astype(F32) + self.four[x].astype(F32)
+
+    def forward(self):
+        self.c[0].wait_recv()
+        for k in (0, 1):
+            self.outgoing[k][...] = self.total(self.order[k]).astype(BF16)
+            self.c[1 + k].start()
+        self.base.mine[self.m] = self.total(self.base.place.x)
+
+    def cross(self):
+        self.c[1].wait_recv()
+        self.outgoing[2][...] = (self.total(self.order[2]) + self.incoming[0][...].astype(F32)).astype(BF16)
+        self.c[3].start()
+
+    def take(self):
+        self.c[2].wait_recv()
+        self.c[3].wait_recv()
+        return self.base.mine[self.m] + self.incoming[1][...].astype(F32) + self.incoming[2][...].astype(F32)
 
 
 def run_pipeline(steps, count=NM):
@@ -196,6 +253,119 @@
     def finish(self):
         for k in (2, 3, 5, 6):
             self.c[k].wait_recv()
+
+    def drain(self):
+        for copy in self.c:
+            copy.wait_send()
+
+
+class GatherX:
+    def __init__(self, place, block, send, recv, index, rightward):
+        p = place
+        ahead, behind, across = p.shift(1), p.shift(3), p.shift(2)
+        y, x = p.y, p.x
+        self.rightward = rightward
+
+        def go(slot, owner, to):
+            ref = block(owner)
+            return remote(ref, ref, send.at[index, slot], recv.at[index, slot], "gene", to)
+
+        self.c = [
+            go(0, p.chip(y, x), p.right),
+            go(1, p.chip(y, x), p.left),
+            go(2, p.chip(y, behind), p.right) if rightward else go(2, p.chip(y, ahead), p.left),
+            go(3, p.chip(y, x), p.other_y),
+            go(4, p.chip(y, behind), p.other_y),
+            go(5, p.chip(y, ahead), p.other_y),
+            go(6, p.chip(y, across), p.other_y),
+        ]
+
+    def start(self):
+        for k in (0, 1, 3):
+            self.c[k].start()
+
+    def second(self):
+        c = self.c
+        for k in (0, 1):
+            c[k].wait_recv()
+            if self.rightward == (k == 0):
+                c[2].start()
+            c[4 + k].start()
+
+    def third(self):
+        self.c[2].wait_recv()
+        self.c[6].start()
+
+    def finish(self):
+        for k in (3, 4, 5, 6):
+            self.c[k].wait_recv()
+
+    def drain(self):
+        for copy in self.c:
+            copy.wait_send()
+
+
+class WideGather:
+    SLOTS = 15
+
+    def __init__(self, place, block, send, recv, index):
+        p = place
+        core, x, y, z = p.core, p.x, p.y, 1 - p.y
+        ahead, behind, across = p.shift(1), p.shift(3), p.shift(2)
+        self.far = Gather(place, lambda q: block(2 * q + core), send, recv, index)
+        held = [p.chip(y, x), p.chip(z, x), p.chip(y, behind), p.chip(y, ahead), p.chip(z, behind), p.chip(z, ahead),
+                p.chip(y, across), p.chip(z, across)]
+        self.near = []
+        for k, q in enumerate(held):
+            ref = block(2 * q + core)
+            self.near.append(remote(ref, ref, send.at[index, 7 + k], recv.at[index, 7 + k], "gene", p.other_core))
+
+    def start(self):
+        self.far.start()
+        self.near[0].start()
+
+    def second(self):
+        self.far.second()
+        self.near[1].start()
+        self.near[2].start()
+
+    def third(self):
+        self.far.third()
+        self.near[5].start()
+
+    def finish(self):
+        self.far.finish()
+        for k in (3, 4, 6, 7):
+            self.near[k].start()
+        for copy in self.near:
+            copy.wait_recv()
+
+    def drain(self):
+        self.far.drain()
+        for copy in self.near:
+            copy.wait_send()
+
+
+class DirectSum:
+    def __init__(self, place, shares, slots, send, recv):
+        p = place
+        self.shares, self.slots = shares, slots
+        self.chip = p.chip(p.y, p.x)
+        self.c = []
+        for k in range(1, NCHIP):
+            to = lax.rem(self.chip + k, NCHIP)
+            self.c.append(remote(shares.at[to], slots.at[k], send.at[k], recv.at[k], "gene", to * 2 + p.core))
+
+    def start(self):
+        for copy in self.c:
+            copy.start()
+
+    def take(self):
+        total = self.shares[self.chip].astype(F32)
+        for k in range(1, NCHIP):
+            self.c[k - 1].wait_recv()
+            total = total + self.slots[k].astype(F32)
+        return total
 
     def drain(self):
         for copy in self.c:
@@ -344,7 +514,14 @@
         + [pltpu.SemaphoreType.DMA((NM, NM))] * 2
         + [pltpu.SemaphoreType.DMA((2 * NM, Gather.SLOTS))] * 2
         + [pltpu.SemaphoreType.DMA((1, 16))] * 2
-        + Scatter.scratch(width) * 3
+        + Scatter.scratch(width) * 2
+        + [
+            pltpu.VMEM((half, width), F32),
+            pltpu.VMEM((NCHIP, ROWS, width), BF16),
+            pltpu.VMEM((NCHIP, ROWS, width), BF16),
+            pltpu.SemaphoreType.DMA((NCHIP,)),
+            pltpu.SemaphoreType.DMA((NCHIP,)),
+        ]
     )
 
 
@@ -352,12 +529,12 @@
     (scaled, w_proj, tile, slots, halves, pair, padded, tokens, resid, kv, queries, spot, load_sem) = refs[:13]
     raws, layers = refs[13:17], refs[17:23]
     (s_send, s_recv, w_send, w_recv, p_send, p_recv, k_send, k_recv, a_send, a_recv, d_send, d_recv) = refs[23:35]
-    sums = refs[35:]
+    sums, (gathered, shares, share_in, z_send, z_recv) = refs[35:-5], refs[-5:]
     place = Place()
     width = resid.shape[-1]
     wide = w_proj.shape[-1]
     core, here = place.core, place.chip(place.y, place.x)
-    scatter = [Scatter(place, sums[9 * k:9 * k + 9]) for k in range(3)]
+    scatter = [Scatter(place, sums[10 * k:10 * k + 10]) for k in range(2)]
     weights, outs, blocks = layers[0::3], layers[1::3], layers[2::3]
 
     greet(everyone(place))
@@ -428,7 +605,12 @@
     run_pipeline([project, join, scatter[0].forward, scatter[0].cross, keep])
 
     gathers = [
-        [Gather(place, lambda q, k=k, m=m: blocks[k].at[m, q], a_send, a_recv, k * NM + m) for m in range(NM)]
+        [
+            GatherX(place, lambda q, k=k, m=m: blocks[k].at[m, q], a_send, a_recv, k * NM + m, m == 1)
+            if m % 2
+            else Gather(place, lambda q, k=k, m=m: blocks[k].at[m, q], a_send, a_recv, k * NM + m)
+            for m in range(NM)
+        ]
         for k in range(2)
     ]
     for s in range(NM):
@@ -490,25 +672,21 @@
         values = jnp.concatenate([kv[m, 0, 1], kv[m, 1, 1]], axis=0)
         mixed = cross_mix(queries[m], keys, values, same, head)
         out = jnp.dot(mixed, outs[1][...], preferred_element_type=F32)
-        scatter[2].chip[m] = out.astype(BF16).reshape(NCHIP, ROWS, width)
-        scatter[2].spread(m)
-
-    def add_cross(m):
-        resid[m] = resid[m] + scatter[2].take(m)
-
-    run_pipeline([
-        lambda m: gathers[1][m].second(), lambda m: gathers[1][m].third(), look, attend,
-        scatter[2].forward, scatter[2].cross, add_cross,
-    ])
-
-    pooled = (resid[0] + resid[1] + resid[2] + resid[3]) * (1.0 / NM)
+        gathered[...] = gathered[...] + out if m else out
+
+    run_pipeline([lambda m: gathers[1][m].second(), lambda m: gathers[1][m].third(), look, attend])
+
+    shares[...] = gathered[...].astype(BF16).reshape(NCHIP, ROWS, width)
+    final = DirectSum(place, shares, share_in, z_send, z_recv)
+    final.start()
+    pooled = (resid[0] + resid[1] + resid[2] + resid[3] + final.take()) * (1.0 / NM)
     hidden[pl.ds(pl.multiple_of(place.g * ROWS, ROWS), ROWS), :] = rms(pooled).astype(BF16)
     last = Direct(
         place, lambda o: hidden.at[pl.ds(pl.multiple_of(o * ROWS, ROWS), ROWS), :], d_send, d_recv, 0
     )
     last.start()
     last.finish()
-    for one in scatter + gathers[0] + gathers[1] + [swap, last]:
+    for one in scatter + gathers[0] + gathers[1] + [swap, final, last]:
         one.drain()
     for copy in share[0] + share[1] + pairs + trade:
         copy.wait_send()
@@ -670,9 +848,9 @@
 
 def decode_kernel(
     genes_all, cells_all, panel_count,
-    counts, panel_row, panel_col, library, hidden, w_mean, w_disp,
+    counts, panel_row, library, hidden, w_mean, w_disp,
     cell_loss, gradient, disp_block,
-    tile, slots, back, piece, columns, field, panel_part, loss,
+    tile, slots, back, piece, columns, field, panel_part, loss, panel_col,
     s_send, s_recv, h_send, h_recv, v_send, v_recv, f_send, f_recv, d_send, d_recv, o_send, o_recv,
 ):
     place = Place()
@@ -685,6 +863,51 @@
     norm_scale = cells_all ** (-0.5)
     greet(everyone(place) + [("grp", lax.rem(r + k, NR)) for k in range(1, NR)])
 
+    panel_col[...] = jnp.broadcast_to(panel_row[...].astype(F32), (128, genes)).T
+    disp = lax.dot_general(w_disp[...], hidden[...], DN_T, preferred_element_type=F32)
+    table = DISP_BASE + (jnp.maximum(disp, 0.0) + jnp.log1p(jnp.exp(-jnp.abs(disp))))
+    high = table.astype(BF16)
+    rest = table - high.astype(F32)
+    middle = rest.astype(BF16)
+    low = (rest - middle.astype(F32)).astype(BF16)
+    tables = jnp.concatenate([high, middle, low], axis=0)
+    rate_scale = library[0:1] / genes_all
+    panel_part[...] = jnp.zeros_like(panel_part)
+    loss[...] = jnp.zeros_like(loss)
+
+    v_gather = WideGather(
+        place, lambda o: columns.at[:, pl.ds(pl.multiple_of(o * ROWS, ROWS), ROWS), :], v_send, v_recv, 0
+    )
+    field_gather = []
+    for p in range(parts):
+        block = lambda o, p=p: field.at[o, pl.ds(p * step, step), :]
+        field_gather.append(
+            GroupGatherZ(r, block, f_send, f_recv, p, True) if p == 1 else GroupGather(r, block, f_send, f_recv, p)
+        )
+    disp_gather = GroupDirect(r, lambda o: field.at[o, pl.ds(genes, panel_count), :], d_send, d_recv)
+    spread = GroupDirect(r, lambda o: disp_block.at[o], o_send, o_recv)
+
+    def decode(p):
+        at = pl.ds(p * step, step)
+        x = counts[at, :].astype(F32)
+        logit = lax.dot_general(w_mean[at, :], hidden[...], DN_T, preferred_element_type=F32)
+        lane = lax.broadcasted_iota(jnp.int32, (step, 3 * panel_count), 1)
+        pick = (panel_col[at, 0:1] == lax.rem(lane, panel_count).astype(F32)).astype(F32).astype(BF16)
+        theta = jnp.dot(pick, tables, preferred_element_type=F32)
+        nll, d_logit, d_theta = terms(x, theta, logit, rate_scale, norm_scale, 12)
+        field[r, at, :] = d_logit.astype(BF16)
+        field_gather[p].start()
+        loss[...] += jnp.sum(nll, axis=0, keepdims=True)
+        row = lax.broadcasted_iota(jnp.int32, (step, 128), 1)
+        wanted = jnp.where(lax.rem(row, 8) < 4, (row // 8) * 4 + lax.rem(row, 8), -1)
+        pick_t = (panel_col[at, :] == wanted.astype(F32)).astype(F32).astype(BF16)
+        upper = d_theta.astype(BF16)
+        lower = (d_theta - upper.astype(F32)).astype(BF16)
+        panel_part[...] += lax.dot_general(pick_t, upper, DN_0, preferred_element_type=F32) + lax.dot_general(
+            pick_t, lower, DN_0, preferred_element_type=F32
+        )
+
+    decode(0)
     own = hidden[pl.ds(pl.multiple_of(place.g * ROWS, ROWS), ROWS), :].astype(F32)
     piece[...] = jnp.zeros_like(piece)
     for k in range(NR):
@@ -699,56 +922,13 @@
         copy.start()
     columns[r, rows] = piece[r]
 
-    disp = lax.dot_general(w_disp[...], hidden[...], DN_T, preferred_element_type=F32)
-    table = DISP_BASE + (jnp.maximum(disp, 0.0) + jnp.log1p(jnp.exp(-jnp.abs(disp))))
-    high = table.astype(BF16)
-    rest = table - high.astype(F32)
-    middle = rest.astype(BF16)
-    low = (rest - middle.astype(F32)).astype(BF16)
-    tables = jnp.concatenate([high, middle, low], axis=0)
-    rate_scale = library[0:1] / genes_all
-    panel_part[...] = jnp.zeros_like(panel_part)
-    loss[...] = jnp.zeros_like(loss)
-
-    v_gather = Direct(
-        place, lambda o: columns.at[:, pl.ds(pl.multiple_of(o * ROWS, ROWS), ROWS), :], v_send, v_recv, 0
-    )
-    field_gather = []
-    for p in range(parts):
-        block = lambda o, p=p: field.at[o, pl.ds(p * step, step), :]
-        field_gather.append(
-            GroupGatherZ(r, block, f_send, f_recv, p, p == 1) if p % 2 else GroupGather(r, block, f_send, f_recv, p)
-        )
-    disp_gather = GroupDirect(r, lambda o: field.at[o, pl.ds(genes, panel_count), :], d_send, d_recv)
-    spread = GroupDirect(r, lambda o: disp_block.at[o], o_send, o_recv)
-
-    def decode(p):
-        at = pl.ds(p * step, step)
-        x = counts[at, :].astype(F32)
-        logit = lax.dot_general(w_mean[at, :], hidden[...], DN_T, preferred_element_type=F32)
-        lane = lax.broadcasted_iota(jnp.int32, (step, 3 * panel_count), 1)
-        pick = (panel_col[at, :] == lax.rem(lane, panel_count)).astype(F32).astype(BF16)
-        theta = jnp.dot(pick, tables, preferred_element_type=F32)
-        nll, d_logit, d_theta = terms(x, theta, logit, rate_scale, norm_scale, 12)
-        field[r, at, :] = d_logit.astype(BF16)
-        field_gather[p].start()
-        loss[...] += jnp.sum(nll, axis=0, keepdims=True)
-        row = lax.broadcasted_iota(jnp.int32, (step, 128), 1)
-        wanted = jnp.where(lax.rem(row, 8) < 4, (row // 8) * 4 + lax.rem(row, 8), -1)
-        pick_t = (panel_col[at, :] == wanted).astype(F32).astype(BF16)
-        upper = d_theta.astype(BF16)
-        lower = (d_theta - upper.astype(F32)).astype(BF16)
-        panel_part[...] += lax.dot_general(pick_t, upper, DN_0, preferred_element_type=F32) + lax.dot_general(
-            pick_t, lower, DN_0, preferred_element_type=F32
-        )
-
-    decode(0)
+    decode(1)
     for copy in into:
         copy.wait_recv()
     v_gather.start()
-    decode(1)
     field_gather[0].second()
     decode(2)
+    v_gather.second()
     field_gather[1].second()
     field_gather[0].third()
     decode(3)
@@ -759,6 +939,7 @@
     first = Swap(place, lambda t: tile.at[t], slots, s_send, s_recv, 0)
     first.start()
     slots[place.g] = tile[place.g]
+    v_gather.third()
     field_gather[2].second()
     field_gather[1].third()
     first.finish()
@@ -767,7 +948,6 @@
     back[place.g] = summed
     second = Swap(place, lambda t: back.at[place.g], back, s_send, s_recv, 1)
     second.start()
-    v_gather.finish()
     field_gather[2].third()
     field_gather[3].second()
     second.finish()
@@ -788,6 +968,7 @@
         field_gather[p].finish()
         gradient[pl.ds(p * step, step), :] = contract(p * step, step)
 
+    v_gather.finish()
     gradient_of(0)
     gradient_of(1)
     disp_gather.finish()
@@ -850,7 +1031,7 @@
             jax.ShapeDtypeStruct((genes, 256), F32),
             jax.ShapeDtypeStruct((NR, panel_count, 256), F32),
         ),
-        in_specs=[whole()] * 7,
+        in_specs=[whole()] * 6,
         out_specs=(whole(), whole(), whole()),
         scratch_shapes=[
             pltpu.VMEM((NG, 8, cells), F32),
@@ -861,11 +1042,12 @@
             pltpu.VMEM((NR, genes + panel_count, cells), BF16),
             pltpu.VMEM((128, cells), F32),
             pltpu.VMEM((1, cells), F32),
+            pltpu.VMEM((genes, 128), F32),
         ] + swap_sems + [
             pltpu.SemaphoreType.DMA((NR,)),
             pltpu.SemaphoreType.DMA((NR,)),
-            pltpu.SemaphoreType.DMA((1, 16)),
-            pltpu.SemaphoreType.DMA((1, 16)),
+            pltpu.SemaphoreType.DMA((1, WideGather.SLOTS)),
+            pltpu.SemaphoreType.DMA((1, WideGather.SLOTS)),
             pltpu.SemaphoreType.DMA((4, GroupGather.SLOTS)),
             pltpu.SemaphoreType.DMA((4, GroupGather.SLOTS)),
             pltpu.SemaphoreType.DMA((NR,)),
@@ -874,7 +1056,7 @@
             pltpu.SemaphoreType.DMA((NR,)),
         ],
         compiler_params=params(3),
-    )(counts_t, panels[None, :], panels[:, None], library, hidden, w_mean.T, w_disp.T)
+    )(counts_t, panels[None, :], library, hidden, w_mean.T, w_disp.T)
     cell_loss, grad_mean, grad_disp = pl.pallas_call(
         finish_kernel,
         name="finish",

time: 190 us -> 178 us (0.937)
  Pallas kernels: 183 us -> 171 us
    pallas_call x1, Pallas kernels: 62.3 us -> 55.3 us  [shards(): pl.pallas_call(functools.partial(decode_kernel, genes_all, cells_all, pan...]
    pallas_call x1, Pallas kernels: 118 us -> 113 us  [shards(): pl.pallas_call(functools.partial(encoder_kernel, head), name='encoder', o...]
    unnamed x8 -> x4, local copies, waits for them, and re-layouts: 1.57 us -> 3.59 us
where the time goes in v4:
time: 178 us
  Pallas kernels  171 us (96%)
  local copies, waits for them, and re-layouts  6.43 us (4%)
    pallas_call x1, Pallas kernels, shards(): pl.pallas_call(functools.partial(encoder_kernel, head), name='encoder', o...  113 us
    pallas_call x1, Pallas kernels, shards(): pl.pallas_call(functools.partial(decode_kernel, genes_all, cells_all, pan...  55.3 us
    unnamed x4, local copies, waits for them, and re-layouts  3.59 us

profile of v4, /device:TPU:1, one launch (start us, length us, event | category | flops | bytes accessed | tf_op | source)
XLA Modules:
  0.0 177.7 jit_solution(15388992814996901823)
XLA Ops:
  0.6 0.0 copy-start
  0.6 1.8 %copy.17.o1_hbm = bf16[2,50,1600]{2,1,0:T(8,128)(2,1)} copy(bf16[2,50,1600]{2,0,1:T(2,128)(2,1)} %param.15) | data formatting | bytes 640000 | tf_op args[5]
  2.5 1.8 copy.18.o2_hbm
  4.2 0.0 copy-done
  4.2 2.8 %copy_bitcast_fusion = (bf16[3,2,50,1600]{3,2,1,0:T(8,128)(2,1)}, bf16[3,2,50,1600]{3,2,1,0:T(8,128)(2,1)}) fusion(bf16[3,50,2,1600]{3,2,1,0:T(2,128)(2,1)S(1)} %bitcast.19, bf16[3,50,2,1600]{3,2,1,0:T(2,128)(2,1)} %bitcast.20), kind=kLoop, calls=%fused_computation | loop fusion | bytes 3840000 | tf_op jit(solution)/shard_map/transpose | solution.py:1005
  7.1 112.6 %encoder.1 = (bf16[256,1600]{1,0:T(8,128)(2,1)}, f32[8,256]{1,0:T(8,128)}) custom-call(s32[960,256]{1,0:T(8,128)} %bitcast.16, s32[1,256]{1,0:T(1,128)} %groups.1, bf16[960,6400]{1,0:T(8,128)(2,1)} %w_hbm.1, bf16[3,2,50,1600]{3,2,1,0:T(8,128)(2,1)} %get-tuple-element.20.q1_hbm, bf16[3,2,50,1600]{3,2,1,0:T(8,128)(2,1)} %get-tuple-element.19.q2_hbm, ...), custom_call_target="tpu_custom_call" | custom-call | tf_op jit(solution)/shard_map/encoder/pallas_call | solution.py:1017
  119.7 55.3 %decode.1 = (f32[1,256]{1,0:T(1,128)}, f32[960,256]{1,0:T(8,128)}, f32[8,64,256]{2,1,0:T(8,128)}) custom-call(s32[960,256]{1,0:T(8,128)} %bitcast.17, s32[1,960]{1,0:T(1,128)} %bitcast.22, f32[8,256]{1,0:T(8,128)} %get-tuple-element.11.library, bf16[256,1600]{1,0:T(8,128)(2,1)} %get-tuple-element.12.hidden, bf16[960,1600]{1,0:T(8,128)(2,1)} %bitcast.18, ...), custom_call_target="tpu_custom_call" | custom-call | tf_op jit(solution)/shard_map/decode/pallas_call | solution.py:1026
  175.0 2.7 %finish.1 = (f32[1,256]{1,0:T(1,128)}, f32[200,960]{1,0:T(8,128)}, f32[64,1600]{1,0:T(8,128)}) custom-call(f32[960,256]{1,0:T(8,128)} %get-tuple-element.13.gradient, f32[8,64,256]{2,1,0:T(8,128)} %get-tuple-element.14.disp_block, f32[1,256]{1,0:T(1,128)} %get-tuple-element.15.loss), custom_call_target="tpu_custom_call" | custom-call | tf_op jit(solution)/shard_map/finish/pallas_call | solution.py:1060
Async XLA Ops:
  0.6 3.6 %copy-start = (bf16[1600,2,150]{0,1,2:T(2,128)(2,1)S(1)}, bf16[1600,2,150]{0,1,2:T(2,128)(2,1)}, u32[]{:S(2)}) copy-start(bf16[1600,2,150]{0,1,2:T(2,128)(2,1)} %param.16) | copy-start | bytes 2880004

commit v5 on v4

--- a/solution.py
+++ b/solution.py
@@ -94,8 +94,8 @@
         ahead, behind, across = p.shift(1), p.shift(3), p.shift(2)
         self.copies, self.turned = [], {}
         for m in range(NM):
-            if m % 2:
-                self.turned[m] = ScatterY(self, m, four.at[m // 2], 1 if m == 1 else -1)
+            if m % 2 == 0:
+                self.turned[m] = ScatterY(self, m, four.at[m // 2], 1 if m == 0 else -1)
                 self.copies.append(self.turned[m].c)
                 continue
 
@@ -175,32 +175,36 @@
         def go(slot, src, dst, device):
             return remote(src, dst, base.send.at[m, slot], base.recv.at[m, slot], "gene", device)
 
-        self.c = [go(0, base.chip.at[m, pl.ds((1 - p.y) * NX, NX)], y_four, p.other_y)] + [
-            go(1 + k, self.outgoing[k], self.incoming[k], (to, back, to)[k]) for k in range(3)
-        ]
+        self.c = [
+            go(k, base.chip.at[m, p.chip(1 - p.y, x)], y_four.at[x], p.other_y)
+            for k, x in enumerate(self.order + (p.x,))
+        ] + [go(4 + k, self.outgoing[k], self.incoming[k], (to, back, to)[k]) for k in range(3)]
 
     def spread(self):
-        self.c[0].start()
-
-    def total(self, x):
+        for k in range(4):
+            self.c[k].start()
+
+    def total(self, k):
         p = self.base.place
+        x = p.x if k == 3 else self.order[k]
+        self.c[k].wait_recv()
         return self.base.chip[self.m, p.chip(p.y, x)].astype(F32) + self.four[x].astype(F32)
 
     def forward(self):
-        self.c[0].wait_recv()
         for k in (0, 1):
-            self.outgoing[k][...] = self.total(self.order[k]).astype(BF16)
-            self.c[1 + k].start()
-        self.base.mine[self.m] = self.total(self.base.place.x)
+            self.outgoing[k][...] = self.total(k).astype(BF16)
+            self.c[4 + k].start()
 
     def cross(self):
-        self.c[1].wait_recv()
-        self.outgoing[2][...] = (self.total(self.order[2]) + self.incoming[0][...].astype(F32)).astype(BF16)
-        self.c[3].start()
+        value = self.total(2)
+        self.c[4].wait_recv()
+        self.outgoing[2][...] = (value + self.incoming[0][...].astype(F32)).astype(BF16)
+        self.c[6].start()
+        self.base.mine[self.m] = self.total(3)
 
     def take(self):
-        self.c[2].wait_recv()
-        self.c[3].wait_recv()
+        self.c[5].wait_recv()
+        self.c[6].wait_recv()
         return self.base.mine[self.m] + self.incoming[1][...].astype(F32) + self.incoming[2][...].astype(F32)
 
 
@@ -484,7 +488,7 @@
 
 def encoder_scratch(width, genes, cells, head):
     half = cells // 2
-    raw = [pltpu.VMEM((3, 2, head, width), BF16), pltpu.VMEM((2, head, width), BF16)]
+    raw = [pltpu.VMEM((3 * head, 2, width), BF16), pltpu.VMEM((head, 2, width), BF16)]
     layer = [
         pltpu.VMEM((3, width, 256), BF16),
         pltpu.VMEM((256, width), BF16),
@@ -499,6 +503,7 @@
             pltpu.VMEM((NM, NCHIP, 2, ROWS, width), BF16),
             pltpu.VMEM((NM, NCHIP, ROWS, width), BF16),
             pltpu.VMEM((128, width), F32),
+            pltpu.VMEM((2, 3 * head, width), F32),
             pltpu.VMEM((NM, ROWS, width), F32),
             pltpu.VMEM((NM, ROWS, width), F32),
             pltpu.VMEM((NM, 2, 2, half, 256), BF16),
@@ -525,11 +530,11 @@
     )
 
 
-def encoder_kernel(head, counts, groups, w_hbm, q1_hbm, q2_hbm, o1_hbm, o2_hbm, hidden, library, *refs):
-    (scaled, w_proj, tile, slots, halves, pair, padded, tokens, resid, kv, queries, spot, load_sem) = refs[:13]
-    raws, layers = refs[13:17], refs[17:23]
-    (s_send, s_recv, w_send, w_recv, p_send, p_recv, k_send, k_recv, a_send, a_recv, d_send, d_recv) = refs[23:35]
-    sums, (gathered, shares, share_in, z_send, z_recv) = refs[35:-5], refs[-5:]
+def encode(head, early, after, counts, groups, w_hbm, q1_hbm, q2_hbm, o1_hbm, o2_hbm, hidden, library, *refs):
+    (scaled, w_proj, tile, slots, halves, pair, padded, split, tokens, resid, kv, queries, spot, load_sem) = refs[:14]
+    raws, layers = refs[14:18], refs[18:24]
+    (s_send, s_recv, w_send, w_recv, p_send, p_recv, k_send, k_recv, a_send, a_recv, d_send, d_recv) = refs[24:36]
+    sums, (gathered, shares, share_in, z_send, z_recv) = refs[36:-5], refs[-5:]
     place = Place()
     width = resid.shape[-1]
     wide = w_proj.shape[-1]
@@ -537,7 +542,6 @@
     scatter = [Scatter(place, sums[10 * k:10 * k + 10]) for k in range(2)]
     weights, outs, blocks = layers[0::3], layers[1::3], layers[2::3]
 
-    greet(everyone(place))
     tile[...] = jnp.broadcast_to(jnp.sum(counts[...].astype(F32), axis=0, keepdims=True), tile.shape)
     swap = Swap(place, lambda t: tile, slots, s_send, s_recv, 0)
     swap.start()
@@ -551,6 +555,7 @@
     ]
     for load in small[:2] + loads + small[2:]:
         load.start()
+    early()
     slots[place.g] = tile[...]
 
     lanes = pl.ds(pl.multiple_of(core * 128, 128), 128)
@@ -564,14 +569,16 @@
     def prepare(k):
         padded[...] = jnp.zeros_like(padded)
         small[2 * k].wait()
+        for h in range(2):
+            split[h] = raws[2 * k][:, h, :].astype(F32)
         for a in range(3):
             for h in range(2):
-                padded[64 * h:64 * h + head, :] = raws[2 * k][a, h].astype(F32)
+                padded[64 * h:64 * h + head, :] = split[h, a * head:(a + 1) * head, :]
             weights[k][a, :, lanes] = padded[...].T.astype(BF16)
         share[k][0].start()
         small[2 * k + 1].wait()
         for h in range(2):
-            padded[64 * h:64 * h + head, :] = raws[2 * k + 1][h].astype(F32)
+            padded[64 * h:64 * h + head, :] = raws[2 * k + 1][:, h, :].astype(F32)
         outs[k][lanes, :] = padded[...].astype(BF16)
         share[k][1].start()
 
@@ -606,8 +613,8 @@
 
     gathers = [
         [
-            GatherX(place, lambda q, k=k, m=m: blocks[k].at[m, q], a_send, a_recv, k * NM + m, m == 1)
-            if m % 2
+            GatherX(place, lambda q, k=k, m=m: blocks[k].at[m, q], a_send, a_recv, k * NM + m, m == 0)
+            if m % 2 == 0
             else Gather(place, lambda q, k=k, m=m: blocks[k].at[m, q], a_send, a_recv, k * NM + m)
             for m in range(NM)
         ]
@@ -685,6 +692,7 @@
         place, lambda o: hidden.at[pl.ds(pl.multiple_of(o * ROWS, ROWS), ROWS), :], d_send, d_recv, 0
     )
     last.start()
+    after()
     last.finish()
     for one in scatter + gathers[0] + gathers[1] + [swap, final, last]:
         one.drain()
@@ -846,13 +854,15 @@
     return nll, d_logit, d_theta
 
 
-def decode_kernel(
-    genes_all, cells_all, panel_count,
-    counts, panel_row, library, hidden, w_mean, w_disp,
-    cell_loss, gradient, disp_block,
-    tile, slots, back, piece, columns, field, panel_part, loss, panel_col,
-    s_send, s_recv, h_send, h_recv, v_send, v_recv, f_send, f_recv, d_send, d_recv, o_send, o_recv,
+def network_kernel(
+    head, genes_all, cells_all, panel_count, encoder_count,
+    counts, groups, w_hbm, q1_hbm, q2_hbm, o1_hbm, o2_hbm, panel_row, w_mean_hbm, w_disp,
+    cell_loss, gradient, disp_block, *refs,
 ):
+    (
+        hidden, library, w_mean, tile, slots, back, piece, columns, field, panel_part, loss, panel_col, mean_sem,
+        s_send, s_recv, h_send, h_recv, v_send, v_recv, f_send, f_recv, d_send, d_recv, o_send, o_recv,
+    ) = refs[encoder_count:]
     place = Place()
     r = lax.axis_index("grp")
     genes, cells = counts.shape
@@ -861,9 +871,34 @@
     parts = 4
     step = genes // parts
     norm_scale = cells_all ** (-0.5)
+    rows = pl.ds(pl.multiple_of(place.g * ROWS, ROWS), ROWS)
+    out, into = [], []
+    for k in range(1, NR):
+        to, frm = lax.rem(r + k, NR), lax.rem(r + NR - k, NR)
+        out.append(remote(piece.at[to], columns.at[r, rows], h_send.at[k], h_recv.at[r], "grp", to))
+        into.append(remote(piece.at[frm], columns.at[frm, rows], h_send.at[k], h_recv.at[frm], "grp", frm))
+    load_mean = pltpu.make_async_copy(w_mean_hbm, w_mean, mean_sem)
+
+    def early():
+        load_mean.start()
+        panel_col[...] = jnp.broadcast_to(panel_row[...].astype(F32), (128, genes)).T
+        piece[...] = jnp.zeros_like(piece)
+        panel_part[...] = jnp.zeros_like(panel_part)
+        loss[...] = jnp.zeros_like(loss)
+
+    def after():
+        own = hidden[rows, :].astype(F32)
+        for k in range(NR):
+            piece[k, :, 0:share] = own[:, k * share:(k + 1) * share].astype(BF16)
+        for copy in out:
+            copy.start()
+        columns[r, rows] = piece[r]
+
     greet(everyone(place) + [("grp", lax.rem(r + k, NR)) for k in range(1, NR)])
-
-    panel_col[...] = jnp.broadcast_to(panel_row[...].astype(F32), (128, genes)).T
+    encode(
+        head, early, after, counts, groups, w_hbm, q1_hbm, q2_hbm, o1_hbm, o2_hbm, hidden, library, *refs[:encoder_count]
+    )
+    load_mean.wait()
     disp = lax.dot_general(w_disp[...], hidden[...], DN_T, preferred_element_type=F32)
     table = DISP_BASE + (jnp.maximum(disp, 0.0) + jnp.log1p(jnp.exp(-jnp.abs(disp))))
     high = table.astype(BF16)
@@ -872,8 +907,6 @@
     low = (rest - middle.astype(F32)).astype(BF16)
     tables = jnp.concatenate([high, middle, low], axis=0)
     rate_scale = library[0:1] / genes_all
-    panel_part[...] = jnp.zeros_like(panel_part)
-    loss[...] = jnp.zeros_like(loss)
 
     v_gather = WideGather(
         place, lambda o: columns.at[:, pl.ds(pl.multiple_of(o * ROWS, ROWS), ROWS), :], v_send, v_recv, 0
@@ -882,7 +915,7 @@
     for p in range(parts):
         block = lambda o, p=p: field.at[o, pl.ds(p * step, step), :]
         field_gather.append(
-            GroupGatherZ(r, block, f_send, f_recv, p, True) if p == 1 else GroupGather(r, block, f_send, f_recv, p)
+            GroupGatherZ(r, block, f_send, f_recv, p, True) if p == 0 else GroupGather(r, block, f_send, f_recv, p)
         )
     disp_gather = GroupDirect(r, lambda o: field.at[o, pl.ds(genes, panel_count), :], d_send, d_recv)
     spread = GroupDirect(r, lambda o: disp_block.at[o], o_send, o_recv)
@@ -907,28 +940,15 @@
             pick_t, lower, DN_0, preferred_element_type=F32
         )
 
-    decode(0)
-    own = hidden[pl.ds(pl.multiple_of(place.g * ROWS, ROWS), ROWS), :].astype(F32)
-    piece[...] = jnp.zeros_like(piece)
-    for k in range(NR):
-        piece[k, :, 0:share] = own[:, k * share:(k + 1) * share].astype(BF16)
-    rows = pl.ds(pl.multiple_of(place.g * ROWS, ROWS), ROWS)
-    out, into = [], []
-    for k in range(1, NR):
-        to, frm = lax.rem(r + k, NR), lax.rem(r + NR - k, NR)
-        out.append(remote(piece.at[to], columns.at[r, rows], h_send.at[k], h_recv.at[r], "grp", to))
-        into.append(remote(piece.at[frm], columns.at[frm, rows], h_send.at[k], h_recv.at[frm], "grp", frm))
-    for copy in out:
-        copy.start()
-    columns[r, rows] = piece[r]
-
-    decode(1)
     for copy in into:
         copy.wait_recv()
     v_gather.start()
+    decode(0)
+    v_gather.second()
+    decode(1)
     field_gather[0].second()
+    v_gather.third()
     decode(2)
-    v_gather.second()
     field_gather[1].second()
     field_gather[0].third()
     decode(3)
@@ -939,7 +959,6 @@
     first = Swap(place, lambda t: tile.at[t], slots, s_send, s_recv, 0)
     first.start()
     slots[place.g] = tile[place.g]
-    v_gather.third()
     field_gather[2].second()
     field_gather[1].third()
     first.finish()
@@ -999,12 +1018,6 @@
     return pltpu.CompilerParams(collective_id=number, has_side_effects=True, vmem_limit_bytes=LIMIT)
 
 
-def head_weights(w_qkv):
-    width, heads, three = w_qkv.shape
-    turned_w = jnp.transpose(w_qkv, (2, 1, 0)).reshape(3, three // 3, heads, width)
-    return jnp.transpose(turned_w, (0, 2, 1, 3))
-
-
 def shards(counts, panels, membership, w_proj, w_qkv_within, w_out_within, w_qkv_cross, w_out_cross, w_mean, w_disp):
     cells, genes = counts.shape
     width = w_qkv_within.shape[0]
@@ -1014,26 +1027,21 @@
     panel_count = w_disp.shape[1]
     counts_t = counts.T
     swap_sems = [pltpu.SemaphoreType.DMA((2, NG))] * 2
-    hidden, library = pl.pallas_call(
-        functools.partial(encoder_kernel, head),
-        name="encoder",
-        out_shape=(jax.ShapeDtypeStruct((cells, width), BF16), jax.ShapeDtypeStruct((8, cells), F32)),
-        in_specs=[whole()] * 2 + [pl.BlockSpec(memory_space=pl.ANY)] * 5,
-        out_specs=(whole(), whole()),
-        scratch_shapes=encoder_scratch(width, genes, cells, head),
-        compiler_params=params(0),
-    )(counts_t, membership, w_proj, head_weights(w_qkv_within), head_weights(w_qkv_cross), w_out_within, w_out_cross)
+    first_part = encoder_scratch(width, genes, cells, head)
     cell_loss, gradient, disp_block = pl.pallas_call(
-        functools.partial(decode_kernel, genes_all, cells_all, panel_count),
-        name="decode",
+        functools.partial(network_kernel, head, genes_all, cells_all, panel_count, len(first_part)),
+        name="network",
         out_shape=(
             jax.ShapeDtypeStruct((1, cells), F32),
             jax.ShapeDtypeStruct((genes, 256), F32),
             jax.ShapeDtypeStruct((NR, panel_count, 256), F32),
         ),
-        in_specs=[whole()] * 6,
+        in_specs=[whole()] * 2 + [pl.BlockSpec(memory_space=pl.ANY)] * 5 + [whole(), pl.BlockSpec(memory_space=pl.ANY), whole()],
         out_specs=(whole(), whole(), whole()),
-        scratch_shapes=[
+        scratch_shapes=first_part + [
+            pltpu.VMEM((cells, width), BF16),
+            pltpu.VMEM((8, cells), F32),
+            pltpu.VMEM((genes, width), BF16),
             pltpu.VMEM((NG, 8, cells), F32),
             pltpu.VMEM((NG, 8, cells), F32),
             pltpu.VMEM((NG, 8, cells), F32),
@@ -1043,6 +1051,7 @@
             pltpu.VMEM((128, cells), F32),
             pltpu.VMEM((1, cells), F32),
             pltpu.VMEM((genes, 128), F32),
+            pltpu.SemaphoreType.DMA,
         ] + swap_sems + [
             pltpu.SemaphoreType.DMA((NR,)),
             pltpu.SemaphoreType.DMA((NR,)),
@@ -1055,8 +1064,12 @@
             pltpu.SemaphoreType.DMA((NR,)),
             pltpu.SemaphoreType.DMA((NR,)),
         ],
-        compiler_params=params(3),
-    )(counts_t, panels[None, :], library, hidden, w_mean.T, w_disp.T)
+        compiler_params=params(0),
+    )(
+        counts_t, membership, w_proj, jnp.transpose(w_qkv_within, (2, 1, 0)), jnp.transpose(w_qkv_cross, (2, 1, 0)),
+        jnp.transpose(w_out_within, (1, 0, 2)), jnp.transpose(w_out_cross, (1, 0, 2)),
+        panels[None, :], w_mean.T, w_disp.T,
+    )
     cell_loss, grad_mean, grad_disp = pl.pallas_call(
         finish_kernel,
         name="finish",

time: 178 us -> 163 us (0.916)
  Pallas kernels: 171 us -> 162 us
  local copies, waits for them, and re-layouts: 6.43 us -> 0 us
    pallas_call x2 -> x1, Pallas kernels: 168 us -> 159 us  [shards(): pl.pallas_call(functools.partial(network_kernel, head, genes_all, cells_a...]
    unnamed x4 -> x0, local copies, waits for them, and re-layouts: 3.59 us -> none
    transpose x1 -> x0, local copies, waits for them, and re-layouts: 2.84 us -> none  [head_weights(): return jnp.transpose(turned_w, (0, 2, 1, 3))]
where the time goes in v5:
time: 163 us
  Pallas kernels  162 us (99%)
    pallas_call x1, Pallas kernels, shards(): pl.pallas_call(functools.partial(network_kernel, head, genes_all, cells_a...  159 us

profile of v5, /device:TPU:1, one launch (start us, length us, event | category | flops | bytes accessed | tf_op | source)
XLA Modules:
  0.0 162.6 jit_solution(7170696930469996734)
XLA Ops:
  0.6 159.2 %network.1 = (f32[1,256]{1,0:T(1,128)}, f32[960,256]{1,0:T(8,128)}, f32[8,64,256]{2,1,0:T(8,128)}) custom-call(s32[960,256]{1,0:T(8,128)} %bitcast.13, s32[1,256]{1,0:T(1,128)} %groups.1, bf16[960,6400]{1,0:T(8,128)(2,1)} %w_hbm.1, bf16[150,2,1600]{2,1,0:T(2,128)(2,1)} %bitcast.11, bf16[150,2,1600]{2,1,0:T(2,128)(2,1)} %bitcast.12, ...), custom_call_target="tpu_custom_call" | custom-call | tf_op jit(solution)/shard_map/network/pallas_call | solution.py:1031
  159.9 2.7 %finish.1 = (f32[1,256]{1,0:T(1,128)}, f32[200,960]{1,0:T(8,128)}, f32[64,1600]{1,0:T(8,128)}) custom-call(f32[960,256]{1,0:T(8,128)} %get-tuple-element.9.gradient, f32[8,64,256]{2,1,0:T(8,128)} %get-tuple-element.10.disp_block, f32[1,256]{1,0:T(1,128)} %get-tuple-element.11.loss), custom_call_target="tpu_custom_call" | custom-call | tf_op jit(solution)/shard_map/finish/pallas_call | solution.py:1073

commit v6 on v5

--- a/solution.py
+++ b/solution.py
@@ -56,10 +56,11 @@
         return y * NX + x
 
 
-def greet(axis_peers):
+def greet(axis_peers, meanwhile):
     barrier = pltpu.get_barrier_semaphore()
     for axis, to in axis_peers:
         pl.semaphore_signal(barrier, inc=1, device_id={axis: to}, device_id_type=MESH)
+    meanwhile()
     pl.semaphore_wait(barrier, len(axis_peers))
 
 
@@ -530,7 +531,7 @@
     )
 
 
-def encode(head, early, after, counts, groups, w_hbm, q1_hbm, q2_hbm, o1_hbm, o2_hbm, hidden, library, *refs):
+def encode(head, meet, after, counts, groups, w_hbm, q1_hbm, q2_hbm, o1_hbm, o2_hbm, hidden, library, *refs):
     (scaled, w_proj, tile, slots, halves, pair, padded, split, tokens, resid, kv, queries, spot, load_sem) = refs[:14]
     raws, layers = refs[14:18], refs[18:24]
     (s_send, s_recv, w_send, w_recv, p_send, p_recv, k_send, k_recv, a_send, a_recv, d_send, d_recv) = refs[24:36]
@@ -542,9 +543,6 @@
     scatter = [Scatter(place, sums[10 * k:10 * k + 10]) for k in range(2)]
     weights, outs, blocks = layers[0::3], layers[1::3], layers[2::3]
 
-    tile[...] = jnp.broadcast_to(jnp.sum(counts[...].astype(F32), axis=0, keepdims=True), tile.shape)
-    swap = Swap(place, lambda t: tile, slots, s_send, s_recv, 0)
-    swap.start()
     small = [
         pltpu.make_async_copy(src, dst, load_sem.at[NM + k])
         for k, (src, dst) in enumerate(zip((q1_hbm, o1_hbm, q2_hbm, o2_hbm), raws))
@@ -553,9 +551,17 @@
         pltpu.make_async_copy(w_hbm.at[:, pl.ds((m * width) // 128 * 128, wide)], w_proj.at[m], load_sem.at[m])
         for m in range(NM)
     ]
-    for load in small[:2] + loads + small[2:]:
-        load.start()
-    early()
+
+    def first():
+        for load in small[:2] + loads + small[2:]:
+            load.start()
+
+    def second():
+        tile[...] = jnp.broadcast_to(jnp.sum(counts[...].astype(F32), axis=0, keepdims=True), tile.shape)
+
+    meet(first, second)
+    swap = Swap(place, lambda t: tile, slots, s_send, s_recv, 0)
+    swap.start()
     slots[place.g] = tile[...]
 
     lanes = pl.ds(pl.multiple_of(core * 128, 128), 128)
@@ -743,55 +749,6 @@
 
     def finish(self):
         for k in (2, 3, 5, 6):
-            self.c[k].wait_recv()
-
-    def drain(self):
-        for copy in self.c:
-            copy.wait_send()
-
-
-class GroupGatherZ:
-    def __init__(self, r, block, send, recv, index, upward):
-        z, h = lax.rem(r, NZ), r // NZ
-        up, down, across = lax.rem(z + 1, NZ), lax.rem(z + 3, NZ), lax.rem(z + 2, NZ)
-        k = 1 - h
-        self.upward = upward
-
-        def at(a, b):
-            return a * NZ + b
-
-        def go(slot, owner, to):
-            ref = block(owner)
-            return remote(ref, ref, send.at[index, slot], recv.at[index, slot], "grp", to)
-
-        self.c = [
-            go(0, at(h, z), at(h, up)),
-            go(1, at(h, z), at(h, down)),
-            go(2, at(h, down), at(h, up)) if upward else go(2, at(h, up), at(h, down)),
-            go(3, at(h, z), at(k, z)),
-            go(4, at(h, down), at(k, z)),
-            go(5, at(h, up), at(k, z)),
-            go(6, at(h, across), at(k, z)),
-        ]
-
-    def start(self):
-        for k in (0, 1, 3):
-            self.c[k].start()
-
-    def second(self):
-        c = self.c
-        for k in (0, 1):
-            c[k].wait_recv()
-            if self.upward == (k == 0):
-                c[2].start()
-            c[4 + k].start()
-
-    def third(self):
-        self.c[2].wait_recv()
-        self.c[6].start()
-
-    def finish(self):
-        for k in (3, 4, 5, 6):
             self.c[k].wait_recv()
 
     def drain(self):
@@ -856,11 +813,11 @@
 
 def network_kernel(
     head, genes_all, cells_all, panel_count, encoder_count,
-    counts, groups, w_hbm, q1_hbm, q2_hbm, o1_hbm, o2_hbm, panel_row, w_mean_hbm, w_disp,
+    counts_hbm, groups, w_hbm, q1_hbm, q2_hbm, o1_hbm, o2_hbm, panel_row, w_mean_hbm, w_disp,
     cell_loss, gradient, disp_block, *refs,
 ):
     (
-        hidden, library, w_mean, tile, slots, back, piece, columns, field, panel_part, loss, panel_col, mean_sem,
+        counts, hidden, library, w_mean, tile, slots, back, piece, columns, field, panel_part, loss, panel_col, mean_sem,
         s_send, s_recv, h_send, h_recv, v_send, v_recv, f_send, f_recv, d_send, d_recv, o_send, o_recv,
     ) = refs[encoder_count:]
     place = Place()
@@ -877,10 +834,10 @@
         to, frm = lax.rem(r + k, NR), lax.rem(r + NR - k, NR)
         out.append(remote(piece.at[to], columns.at[r, rows], h_send.at[k], h_recv.at[r], "grp", to))
         into.append(remote(piece.at[frm], columns.at[frm, rows], h_send.at[k], h_recv.at[frm], "grp", frm))
-    load_mean = pltpu.make_async_copy(w_mean_hbm, w_mean, mean_sem)
+    load_mean = pltpu.make_async_copy(w_mean_hbm, w_mean, mean_sem.at[0])
+    load_counts = pltpu.make_async_copy(counts_hbm, counts, mean_sem.at[1])
 
     def early():
-        load_mean.start()
         panel_col[...] = jnp.broadcast_to(panel_row[...].astype(F32), (128, genes)).T
         piece[...] = jnp.zeros_like(piece)
         panel_part[...] = jnp.zeros_like(panel_part)
@@ -894,9 +851,19 @@
             copy.start()
         columns[r, rows] = piece[r]
 
-    greet(everyone(place) + [("grp", lax.rem(r + k, NR)) for k in range(1, NR)])
+    def meet(start, finish):
+        def meanwhile():
+            load_counts.start()
+            start()
+            load_mean.start()
+            early()
+            load_counts.wait()
+            finish()
+
+        greet(everyone(place) + [("grp", lax.rem(r + k, NR)) for k in range(1, NR)], meanwhile)
+
     encode(
-        head, early, after, counts, groups, w_hbm, q1_hbm, q2_hbm, o1_hbm, o2_hbm, hidden, library, *refs[:encoder_count]
+        head, meet, after, counts, groups, w_hbm, q1_hbm, q2_hbm, o1_hbm, o2_hbm, hidden, library, *refs[:encoder_count]
     )
     load_mean.wait()
     disp = lax.dot_general(w_disp[...], hidden[...], DN_T, preferred_element_type=F32)
@@ -915,7 +882,7 @@
     for p in range(parts):
         block = lambda o, p=p: field.at[o, pl.ds(p * step, step), :]
         field_gather.append(
-            GroupGatherZ(r, block, f_send, f_recv, p, True) if p == 0 else GroupGather(r, block, f_send, f_recv, p)
+            GroupGather(r, block, f_send, f_recv, p)
         )
     disp_gather = GroupDirect(r, lambda o: field.at[o, pl.ds(genes, panel_count), :], d_send, d_recv)
     spread = GroupDirect(r, lambda o: disp_block.at[o], o_send, o_recv)
@@ -929,7 +896,8 @@
         theta = jnp.dot(pick, tables, preferred_element_type=F32)
         nll, d_logit, d_theta = terms(x, theta, logit, rate_scale, norm_scale, 12)
         field[r, at, :] = d_logit.astype(BF16)
-        field_gather[p].start()
+        if p < parts - 1:
+            field_gather[p].start()
         loss[...] += jnp.sum(nll, axis=0, keepdims=True)
         row = lax.broadcasted_iota(jnp.int32, (step, 128), 1)
         wanted = jnp.where(lax.rem(row, 8) < 4, (row // 8) * 4 + lax.rem(row, 8), -1)
@@ -958,24 +926,25 @@
     tile[...] = both.reshape(NG, 8, cells)
     first = Swap(place, lambda t: tile.at[t], slots, s_send, s_recv, 0)
     first.start()
+    field_gather[3].start()
     slots[place.g] = tile[place.g]
     field_gather[2].second()
     field_gather[1].third()
     first.finish()
     summed = total_of(slots)
-    cell_loss[...] = summed[4:5] / genes_all
     back[place.g] = summed
     second = Swap(place, lambda t: back.at[place.g], back, s_send, s_recv, 1)
     second.start()
-    field_gather[2].third()
-    field_gather[3].second()
+    cell_loss[...] = summed[4:5] / genes_all
+    v_gather.finish()
     second.finish()
     d_panel = jnp.concatenate([back[k, 0:4] for k in range(NG)], axis=0)
     tail = jnp.exp(-jnp.abs(disp))
     d_disp = d_panel * (jnp.where(disp >= 0, 1.0, tail) / (1.0 + tail)) * norm_scale
     field[r, pl.ds(genes, panel_count), :] = d_disp.astype(BF16)
     disp_gather.start()
-    field_gather[3].third()
+    field_gather[2].third()
+    field_gather[3].second()
 
     def contract(at, size):
         total = jnp.zeros((size, columns.shape[2]), F32)
@@ -987,12 +956,12 @@
         field_gather[p].finish()
         gradient[pl.ds(p * step, step), :] = contract(p * step, step)
 
-    v_gather.finish()
     gradient_of(0)
     gradient_of(1)
     disp_gather.finish()
     disp_block[r] = contract(genes, panel_count)
     spread.start()
+    field_gather[3].third()
     gradient_of(2)
     gradient_of(3)
     spread.finish()
@@ -1008,6 +977,10 @@
     grad_mean[...] = gradient[...].T[0:share]
     for k in range(NR):
         grad_disp[:, k * share:(k + 1) * share] = disp_block[k, :, 0:share]
+
+
+def hbm():
+    return pl.BlockSpec(memory_space=pl.ANY)
 
 
 def whole():
@@ -1036,9 +1009,10 @@
             jax.ShapeDtypeStruct((genes, 256), F32),
             jax.ShapeDtypeStruct((NR, panel_count, 256), F32),
         ),
-        in_specs=[whole()] * 2 + [pl.BlockSpec(memory_space=pl.ANY)] * 5 + [whole(), pl.BlockSpec(memory_space=pl.ANY), whole()],
+        in_specs=[hbm(), whole()] + [hbm()] * 5 + [whole(), hbm(), whole()],
         out_specs=(whole(), whole(), whole()),
         scratch_shapes=first_part + [
+            pltpu.VMEM((genes, cells), jnp.int32),
             pltpu.VMEM((cells, width), BF16),
             pltpu.VMEM((8, cells), F32),
             pltpu.VMEM((genes, width), BF16),
@@ -1051,7 +1025,7 @@
             pltpu.VMEM((128, cells), F32),
             pltpu.VMEM((1, cells), F32),
             pltpu.VMEM((genes, 128), F32),
-            pltpu.SemaphoreType.DMA,
+            pltpu.SemaphoreType.DMA((2,)),
         ] + swap_sems + [
             pltpu.SemaphoreType.DMA((NR,)),
             pltpu.SemaphoreType.DMA((NR,)),

time: 163 us -> 164 us (level)
  no operation moved by 1% of the time
where the time goes in v6:
time: 164 us
  Pallas kernels  163 us (99%)
    pallas_call x1, Pallas kernels, shards(): pl.pallas_call(functools.partial(network_kernel, head, genes_all, cells_a...  160 us

profile of v6, /device:TPU:1, one launch (start us, length us, event | category | flops | bytes accessed | tf_op | source)
XLA Modules:
  0.0 163.8 jit_solution(3530557598094626455)
XLA Ops:
  0.6 160.4 %network.1 = (f32[1,256]{1,0:T(1,128)}, f32[960,256]{1,0:T(8,128)}, f32[8,64,256]{2,1,0:T(8,128)}) custom-call(s32[960,256]{1,0:T(8,128)} %bitcast.13, s32[1,256]{1,0:T(1,128)} %groups.1, bf16[960,6400]{1,0:T(8,128)(2,1)} %w_hbm.1, bf16[150,2,1600]{2,1,0:T(2,128)(2,1)} %bitcast.11, bf16[150,2,1600]{2,1,0:T(2,128)(2,1)} %bitcast.12, ...), custom_call_target="tpu_custom_call" | custom-call | tf_op jit(solution)/shard_map/network/pallas_call | solution.py:1004
  161.1 2.7 %finish.1 = (f32[1,256]{1,0:T(1,128)}, f32[200,960]{1,0:T(8,128)}, f32[64,1600]{1,0:T(8,128)}) custom-call(f32[960,256]{1,0:T(8,128)} %get-tuple-element.9.gradient, f32[8,64,256]{2,1,0:T(8,128)} %get-tuple-element.10.disp_block, f32[1,256]{1,0:T(1,128)} %get-tuple-element.11.loss), custom_call_target="tpu_custom_call" | custom-call | tf_op jit(solution)/shard_map/finish/pallas_call | solution.py:1047

commit v7 on v6

--- a/solution.py
+++ b/solution.py
@@ -308,6 +308,13 @@
     def drain(self):
         for copy in self.c:
             copy.wait_send()
+
+
+def lead(gathers):
+    for one in gathers:
+        one.second()
+    for one in gathers[:2]:
+        one.third()
 
 
 class WideGather:
@@ -645,8 +652,12 @@
     for copy in share[0]:
         copy.wait_recv()
 
+    lead(gathers[0])
+
     def within(s):
         gathers[0][s].finish()
+        if s + 2 < NM:
+            gathers[0][s + 2].third()
         rows = blocks[0][s].reshape(NCHIP * ROWS, width)
         mixed = within_mix(*heads_of(rows, weights[0], head), head)
         out = jnp.dot(mixed, outs[0][...], preferred_element_type=F32)
@@ -656,10 +667,7 @@
     def add_within(s):
         tokens[s] = tokens[s] + scatter[1].take(s)
 
-    run_pipeline([
-        lambda s: gathers[0][s].second(), lambda s: gathers[0][s].third(), within,
-        scatter[1].forward, scatter[1].cross, add_within,
-    ])
+    run_pipeline([within, scatter[1].forward, scatter[1].cross, add_within])
 
     for m in range(NM):
         for s in range(NM):
@@ -673,7 +681,11 @@
         for m in range(NM)
     ]
 
+    lead(gathers[1])
+
     def look(m):
+        if m + 2 < NM:
+            gathers[1][m + 2].third()
         gathers[1][m].finish()
         rows = blocks[1][m].reshape(NCHIP * ROWS, width)
         queries[m], kv[m, core, 0], kv[m, core, 1] = heads_of(rows, weights[1], head)
@@ -687,7 +699,7 @@
         out = jnp.dot(mixed, outs[1][...], preferred_element_type=F32)
         gathered[...] = gathered[...] + out if m else out
 
-    run_pipeline([lambda m: gathers[1][m].second(), lambda m: gathers[1][m].third(), look, attend])
+    run_pipeline([look, attend])
 
     shares[...] = gathered[...].astype(BF16).reshape(NCHIP, ROWS, width)
     final = DirectSum(place, shares, share_in, z_send, z_recv)
@@ -749,6 +761,55 @@
 
     def finish(self):
         for k in (2, 3, 5, 6):
+            self.c[k].wait_recv()
+
+    def drain(self):
+        for copy in self.c:
+            copy.wait_send()
+
+
+class GroupGatherZ:
+    def __init__(self, r, block, send, recv, index, upward):
+        z, h = lax.rem(r, NZ), r // NZ
+        up, down, across = lax.rem(z + 1, NZ), lax.rem(z + 3, NZ), lax.rem(z + 2, NZ)
+        k = 1 - h
+        self.upward = upward
+
+        def at(a, b):
+            return a * NZ + b
+
+        def go(slot, owner, to):
+            ref = block(owner)
+            return remote(ref, ref, send.at[index, slot], recv.at[index, slot], "grp", to)
+
+        self.c = [
+            go(0, at(h, z), at(h, up)),
+            go(1, at(h, z), at(h, down)),
+            go(2, at(h, down), at(h, up)) if upward else go(2, at(h, up), at(h, down)),
+            go(3, at(h, z), at(k, z)),
+            go(4, at(h, down), at(k, z)),
+            go(5, at(h, up), at(k, z)),
+            go(6, at(h, across), at(k, z)),
+        ]
+
+    def start(self):
+        for k in (0, 1, 3):
+            self.c[k].start()
+
+    def second(self):
+        c = self.c
+        for k in (0, 1):
+            c[k].wait_recv()
+            if self.upward == (k == 0):
+                c[2].start()
+            c[4 + k].start()
+
+    def third(self):
+        self.c[2].wait_recv()
+        self.c[6].start()
+
+    def finish(self):
+        for k in (3, 4, 5, 6):
             self.c[k].wait_recv()
 
     def drain(self):
@@ -817,7 +878,7 @@
     cell_loss, gradient, disp_block, *refs,
 ):
     (
-        counts, hidden, library, w_mean, tile, slots, back, piece, columns, field, panel_part, loss, panel_col, mean_sem,
+        counts, hidden, library, w_mean, tile, slots, back, piece, columns, field, panel_part, loss, panel_col, logits, thetas, mean_sem,
         s_send, s_recv, h_send, h_recv, v_send, v_recv, f_send, f_recv, d_send, d_recv, o_send, o_recv,
     ) = refs[encoder_count:]
     place = Place()
@@ -826,6 +887,7 @@
     width = hidden.shape[1]
     share = width // NR
     parts = 4
+    few = 48
     step = genes // parts
     norm_scale = cells_all ** (-0.5)
     rows = pl.ds(pl.multiple_of(place.g * ROWS, ROWS), ROWS)
@@ -882,23 +944,38 @@
     for p in range(parts):
         block = lambda o, p=p: field.at[o, pl.ds(p * step, step), :]
         field_gather.append(
-            GroupGather(r, block, f_send, f_recv, p)
+            GroupGatherZ(r, block, f_send, f_recv, p, True) if p == 0 else GroupGather(r, block, f_send, f_recv, p)
         )
-    disp_gather = GroupDirect(r, lambda o: field.at[o, pl.ds(genes, panel_count), :], d_send, d_recv)
-    spread = GroupDirect(r, lambda o: disp_block.at[o], o_send, o_recv)
+    half = panel_count // 2
+    mine = pl.ds(pl.multiple_of(place.core * half, half), half)
+    mine_field = pl.ds(pl.multiple_of(genes + place.core * half, half), half)
+    disp_gather = GroupDirect(r, lambda o: field.at[o, mine_field, :], d_send, d_recv)
+    spread = GroupDirect(r, lambda o: disp_block.at[o, mine, :], o_send, o_recv)
+    swap_halves = remote(
+        disp_block.at[:, mine, :], disp_block.at[:, mine, :], o_send.at[0], o_recv.at[0], "gene", place.other_core
+    )
 
     def decode(p):
         at = pl.ds(p * step, step)
-        x = counts[at, :].astype(F32)
-        logit = lax.dot_general(w_mean[at, :], hidden[...], DN_T, preferred_element_type=F32)
+        logits[...] = lax.dot_general(w_mean[at, :], hidden[...], DN_T, preferred_element_type=F32)
         lane = lax.broadcasted_iota(jnp.int32, (step, 3 * panel_count), 1)
         pick = (panel_col[at, 0:1] == lax.rem(lane, panel_count).astype(F32)).astype(F32).astype(BF16)
-        theta = jnp.dot(pick, tables, preferred_element_type=F32)
-        nll, d_logit, d_theta = terms(x, theta, logit, rate_scale, norm_scale, 12)
-        field[r, at, :] = d_logit.astype(BF16)
+        thetas[...] = jnp.dot(pick, tables, preferred_element_type=F32)
+
+        def chunk(i, lost):
+            rows = pl.ds(pl.multiple_of(i * few, few), few)
+            there = pl.ds(pl.multiple_of(p * step + i * few, few), few)
+            nll, d_logit, d_theta = terms(
+                counts[there, :].astype(F32), thetas[rows, :], logits[rows, :], rate_scale, norm_scale, 12
+            )
+            field[r, there, :] = d_logit.astype(BF16)
+            thetas[rows, :] = d_theta
+            return lost + jnp.sum(nll, axis=0, keepdims=True)
+
+        loss[...] += lax.fori_loop(0, step // few, chunk, jnp.zeros_like(loss))
+        d_theta = thetas[...]
         if p < parts - 1:
             field_gather[p].start()
-        loss[...] += jnp.sum(nll, axis=0, keepdims=True)
         row = lax.broadcasted_iota(jnp.int32, (step, 128), 1)
         wanted = jnp.where(lax.rem(row, 8) < 4, (row // 8) * 4 + lax.rem(row, 8), -1)
         pick_t = (panel_col[at, :] == wanted.astype(F32)).astype(F32).astype(BF16)
@@ -949,22 +1026,24 @@
     def contract(at, size):
         total = jnp.zeros((size, columns.shape[2]), F32)
         for k in range(NR):
-            total = total + jnp.dot(field[k, pl.ds(at, size), :], columns[k], preferred_element_type=F32)
+            total = total + jnp.dot(field[k, at, :], columns[k], preferred_element_type=F32)
         return total
 
     def gradient_of(p):
         field_gather[p].finish()
-        gradient[pl.ds(p * step, step), :] = contract(p * step, step)
+        gradient[pl.ds(p * step, step), :] = contract(pl.ds(p * step, step), step)
 
     gradient_of(0)
     gradient_of(1)
+    field_gather[3].third()
     disp_gather.finish()
-    disp_block[r] = contract(genes, panel_count)
+    disp_block[r, mine, :] = contract(mine_field, half)
     spread.start()
-    field_gather[3].third()
     gradient_of(2)
     gradient_of(3)
     spread.finish()
+    swap_halves.start()
+    swap_halves.wait()
     for copy in out:
         copy.wait_send()
     for one in [v_gather, first, second, disp_gather, spread] + field_gather:
@@ -1025,6 +1104,8 @@
             pltpu.VMEM((128, cells), F32),
             pltpu.VMEM((1, cells), F32),
             pltpu.VMEM((genes, 128), F32),
+            pltpu.VMEM((genes // 4, cells), F32),
+            pltpu.VMEM((genes // 4, cells), F32),
             pltpu.SemaphoreType.DMA((2,)),
         ] + swap_sems + [
             pltpu.SemaphoreType.DMA((NR,)),

time: 164 us -> 160 us (0.976)
  Pallas kernels: 163 us -> 160 us
    pallas_call x1, Pallas kernels: 160 us -> 157 us  [shards(): pl.pallas_call(functools.partial(network_kernel, head, genes_all, cells_a...]
where the time goes in v7:
time: 160 us
  Pallas kernels  160 us (100%)
    pallas_call x1, Pallas kernels, shards(): pl.pallas_call(functools.partial(network_kernel, head, genes_all, cells_a...  157 us

profile of v7, /device:TPU:1, one launch (start us, length us, event | category | flops | bytes accessed | tf_op | source)
XLA Modules:
  0.0 160.2 jit_solution(10409331742058395276)
XLA Ops:
  0.6 156.8 %network.1 = (f32[1,256]{1,0:T(1,128)}, f32[960,256]{1,0:T(8,128)}, f32[8,64,256]{2,1,0:T(8,128)}) custom-call(s32[960,256]{1,0:T(8,128)} %bitcast.13, s32[1,256]{1,0:T(1,128)} %groups.1, bf16[960,6400]{1,0:T(8,128)(2,1)} %w_hbm.1, bf16[150,2,1600]{2,1,0:T(2,128)(2,1)} %bitcast.11, bf16[150,2,1600]{2,1,0:T(2,128)(2,1)} %bitcast.12, ...), custom_call_target="tpu_custom_call" | custom-call | tf_op jit(solution)/shard_map/network/pallas_call | solution.py:1083
  157.5 2.7 %finish.1 = (f32[1,256]{1,0:T(1,128)}, f32[200,960]{1,0:T(8,128)}, f32[64,1600]{1,0:T(8,128)}) custom-call(f32[960,256]{1,0:T(8,128)} %get-tuple-element.9.gradient, f32[8,64,256]{2,1,0:T(8,128)} %get-tuple-element.10.disp_block, f32[1,256]{1,0:T(1,128)} %get-tuple-element.11.loss), custom_call_target="tpu_custom_call" | custom-call | tf_op jit(solution)/shard_map/finish/pallas_call | solution.py:1128

commit v8 on v7

--- a/solution.py
+++ b/solution.py
@@ -74,7 +74,7 @@
 
 class Scatter:
     @staticmethod
-    def scratch(width):
+    def scratch(width, sends):
         return [
             pltpu.VMEM((NM, NCHIP, ROWS, width), BF16),
             pltpu.VMEM((NM, 3, ROWS, width), BF16),
@@ -85,11 +85,10 @@
             pltpu.VMEM((NM, ROWS, width), F32),
             pltpu.VMEM((2, NX, ROWS, width), BF16),
             pltpu.SemaphoreType.DMA((NM, 7)),
-            pltpu.SemaphoreType.DMA((NM, 7)),
-        ]
+        ] + [pltpu.SemaphoreType.DMA((NM, 7))] * sends
 
     def __init__(self, place, refs):
-        (self.chip, self.from_left, self.from_right, self.relay, self.y_out, self.y_in, self.mine, four, send, recv) = refs
+        (self.chip, self.from_left, self.from_right, self.relay, self.y_out, self.y_in, self.mine, four, recv, send) = refs
         self.send, self.recv = send, recv
         p = self.place = place
         ahead, behind, across = p.shift(1), p.shift(3), p.shift(2)
@@ -219,14 +218,15 @@
 class Gather:
     SLOTS = 7
 
-    def __init__(self, place, block, send, recv, index):
+    def __init__(self, place, block, send, recv, index, send_index=None):
         p = place
+        send_index = index if send_index is None else send_index
         ahead, behind, across = p.shift(1), p.shift(3), p.shift(2)
         y, z, x = p.y, 1 - p.y, p.x
 
         def go(slot, owner, to):
             ref = block(owner)
-            return remote(ref, ref, send.at[index, slot], recv.at[index, slot], "gene", to)
+            return remote(ref, ref, send.at[send_index, slot], recv.at[index, slot], "gene", to)
 
         own, paired = p.chip(y, x), p.chip(z, x)
         self.c = [
@@ -265,7 +265,7 @@
 
 
 class GatherX:
-    def __init__(self, place, block, send, recv, index, rightward):
+    def __init__(self, place, block, send, recv, index, send_index, rightward):
         p = place
         ahead, behind, across = p.shift(1), p.shift(3), p.shift(2)
         y, x = p.y, p.x
@@ -273,7 +273,7 @@
 
         def go(slot, owner, to):
             ref = block(owner)
-            return remote(ref, ref, send.at[index, slot], recv.at[index, slot], "gene", to)
+            return remote(ref, ref, send.at[send_index, slot], recv.at[index, slot], "gene", to)
 
         self.c = [
             go(0, p.chip(y, x), p.right),
@@ -524,10 +524,11 @@
         + [pltpu.SemaphoreType.DMA((1, NG))] * 2
         + [pltpu.SemaphoreType.DMA((NM,))] * 2
         + [pltpu.SemaphoreType.DMA((NM,))] * 2
-        + [pltpu.SemaphoreType.DMA((NM, NM))] * 2
-        + [pltpu.SemaphoreType.DMA((2 * NM, Gather.SLOTS))] * 2
+        + [pltpu.SemaphoreType.DMA((NM,))] * 2
+        + [pltpu.SemaphoreType.DMA((NM, Gather.SLOTS)), pltpu.SemaphoreType.DMA((2 * NM, Gather.SLOTS))]
         + [pltpu.SemaphoreType.DMA((1, 16))] * 2
-        + Scatter.scratch(width) * 2
+        + Scatter.scratch(width, 1)
+        + Scatter.scratch(width, 0)
         + [
             pltpu.VMEM((half, width), F32),
             pltpu.VMEM((NCHIP, ROWS, width), BF16),
@@ -547,7 +548,7 @@
     width = resid.shape[-1]
     wide = w_proj.shape[-1]
     core, here = place.core, place.chip(place.y, place.x)
-    scatter = [Scatter(place, sums[10 * k:10 * k + 10]) for k in range(2)]
+    scatter = [Scatter(place, sums[0:10]), Scatter(place, sums[10:19] + sums[9:10])]
     weights, outs, blocks = layers[0::3], layers[1::3], layers[2::3]
 
     small = [
@@ -623,12 +624,13 @@
         scatter[0].mine[m] = scatter[0].take(m)
 
     run_pipeline([project, join, scatter[0].forward, scatter[0].cross, keep])
+    scatter[0].drain()
 
     gathers = [
         [
-            GatherX(place, lambda q, k=k, m=m: blocks[k].at[m, q], a_send, a_recv, k * NM + m, m == 0)
+            GatherX(place, lambda q, k=k, m=m: blocks[k].at[m, q], a_send, a_recv, k * NM + m, m, m == 0)
             if m % 2 == 0
-            else Gather(place, lambda q, k=k, m=m: blocks[k].at[m, q], a_send, a_recv, k * NM + m)
+            else Gather(place, lambda q, k=k, m=m: blocks[k].at[m, q], a_send, a_recv, k * NM + m, m)
             for m in range(NM)
         ]
         for k in range(2)
@@ -668,6 +670,8 @@
         tokens[s] = tokens[s] + scatter[1].take(s)
 
     run_pipeline([within, scatter[1].forward, scatter[1].cross, add_within])
+    for one in gathers[0]:
+        one.drain()
 
     for m in range(NM):
         for s in range(NM):
@@ -677,7 +681,7 @@
     for copy in share[1]:
         copy.wait_recv()
     trade = [
-        remote(kv.at[m, core], kv.at[m, core], k_send.at[m, 0], k_recv.at[m, 0], "gene", place.other_core)
+        remote(kv.at[m, core], kv.at[m, core], k_send.at[m], k_recv.at[m], "gene", place.other_core)
         for m in range(NM)
     ]
 
@@ -712,7 +716,7 @@
     last.start()
     after()
     last.finish()
-    for one in scatter + gathers[0] + gathers[1] + [swap, final, last]:
+    for one in scatter[1:] + gathers[1] + [swap, final, last]:
         one.drain()
     for copy in share[0] + share[1] + pairs + trade:
         copy.wait_send()
@@ -879,7 +883,7 @@
 ):
     (
         counts, hidden, library, w_mean, tile, slots, back, piece, columns, field, panel_part, loss, panel_col, logits, thetas, mean_sem,
-        s_send, s_recv, h_send, h_recv, v_send, v_recv, f_send, f_recv, d_send, d_recv, o_send, o_recv,
+        s_send, s_recv, h_send, h_recv, v_send, v_recv, f_send, f_recv, d_recv, o_recv,
     ) = refs[encoder_count:]
     place = Place()
     r = lax.axis_index("grp")
@@ -949,10 +953,10 @@
     half = panel_count // 2
     mine = pl.ds(pl.multiple_of(place.core * half, half), half)
     mine_field = pl.ds(pl.multiple_of(genes + place.core * half, half), half)
-    disp_gather = GroupDirect(r, lambda o: field.at[o, mine_field, :], d_send, d_recv)
-    spread = GroupDirect(r, lambda o: disp_block.at[o, mine, :], o_send, o_recv)
+    disp_gather = GroupDirect(r, lambda o: field.at[o, mine_field, :], h_send, d_recv)
+    spread = GroupDirect(r, lambda o: disp_block.at[o, mine, :], h_send, o_recv)
     swap_halves = remote(
-        disp_block.at[:, mine, :], disp_block.at[:, mine, :], o_send.at[0], o_recv.at[0], "gene", place.other_core
+        disp_block.at[:, mine, :], disp_block.at[:, mine, :], h_send.at[0], o_recv.at[0], "gene", place.other_core
     )
 
     def decode(p):
@@ -1013,15 +1017,17 @@
     second = Swap(place, lambda t: back.at[place.g], back, s_send, s_recv, 1)
     second.start()
     cell_loss[...] = summed[4:5] / genes_all
+    field_gather[3].second()
+    field_gather[2].third()
     v_gather.finish()
     second.finish()
     d_panel = jnp.concatenate([back[k, 0:4] for k in range(NG)], axis=0)
     tail = jnp.exp(-jnp.abs(disp))
     d_disp = d_panel * (jnp.where(disp >= 0, 1.0, tail) / (1.0 + tail)) * norm_scale
     field[r, pl.ds(genes, panel_count), :] = d_disp.astype(BF16)
+    for copy in out:
+        copy.wait_send()
     disp_gather.start()
-    field_gather[2].third()
-    field_gather[3].second()
 
     def contract(at, size):
         total = jnp.zeros((size, columns.shape[2]), F32)
@@ -1038,15 +1044,14 @@
     field_gather[3].third()
     disp_gather.finish()
     disp_block[r, mine, :] = contract(mine_field, half)
+    disp_gather.drain()
     spread.start()
     gradient_of(2)
     gradient_of(3)
     spread.finish()
     swap_halves.start()
     swap_halves.wait()
-    for copy in out:
-        copy.wait_send()
-    for one in [v_gather, first, second, disp_gather, spread] + field_gather:
+    for one in [v_gather, first, second, spread] + field_gather:
         one.drain()
 
 
@@ -1116,8 +1121,6 @@
             pltpu.SemaphoreType.DMA((4, GroupGather.SLOTS)),
             pltpu.SemaphoreType.DMA((NR,)),
             pltpu.SemaphoreType.DMA((NR,)),
-            pltpu.SemaphoreType.DMA((NR,)),
-            pltpu.SemaphoreType.DMA((NR,)),
         ],
         compiler_params=params(0),
     )(

time: 160 us -> 159 us (level)
  Pallas kernels: 160 us -> 158 us
where the time goes in v8:
time: 159 us
  Pallas kernels  158 us (99%)
    pallas_call x1, Pallas kernels, shards(): pl.pallas_call(functools.partial(network_kernel, head, genes_all, cells_a...  155 us

profile of v8, /device:TPU:1, one launch (start us, length us, event | category | flops | bytes accessed | tf_op | source)
XLA Modules:
  0.0 158.6 jit_solution(5759278551776259390)
XLA Ops:
  0.6 155.2 %network.1 = (f32[1,256]{1,0:T(1,128)}, f32[960,256]{1,0:T(8,128)}, f32[8,64,256]{2,1,0:T(8,128)}) custom-call(s32[960,256]{1,0:T(8,128)} %bitcast.13, s32[1,256]{1,0:T(1,128)} %groups.1, bf16[960,6400]{1,0:T(8,128)(2,1)} %w_hbm.1, bf16[150,2,1600]{2,1,0:T(2,128)(2,1)} %bitcast.11, bf16[150,2,1600]{2,1,0:T(2,128)(2,1)} %bitcast.12, ...), custom_call_target="tpu_custom_call" | custom-call | tf_op jit(solution)/shard_map/network/pallas_call | solution.py:1088
  155.9 2.7 %finish.1 = (f32[1,256]{1,0:T(1,128)}, f32[200,960]{1,0:T(8,128)}, f32[64,1600]{1,0:T(8,128)}) custom-call(f32[960,256]{1,0:T(8,128)} %get-tuple-element.9.gradient, f32[8,64,256]{2,1,0:T(8,128)} %get-tuple-element.10.disp_block, f32[1,256]{1,0:T(1,128)} %get-tuple-element.11.loss), custom_call_target="tpu_custom_call" | custom-call | tf_op jit(solution)/shard_map/finish/pallas_call | solution.py:1131

commit v9 on v8

--- a/solution.py
+++ b/solution.py
@@ -892,7 +892,8 @@
     share = width // NR
     parts = 4
     few = 48
-    step = genes // parts
+    sizes = [genes * k // 20 for k in (6, 6, 5, 3)]
+    starts = [sum(sizes[:k]) for k in range(parts)]
     norm_scale = cells_all ** (-0.5)
     rows = pl.ds(pl.multiple_of(place.g * ROWS, ROWS), ROWS)
     out, into = [], []
@@ -946,7 +947,7 @@
     )
     field_gather = []
     for p in range(parts):
-        block = lambda o, p=p: field.at[o, pl.ds(p * step, step), :]
+        block = lambda o, p=p: field.at[o, pl.ds(starts[p], sizes[p]), :]
         field_gather.append(
             GroupGatherZ(r, block, f_send, f_recv, p, True) if p == 0 else GroupGather(r, block, f_send, f_recv, p)
         )
@@ -960,15 +961,16 @@
     )
 
     def decode(p):
-        at = pl.ds(p * step, step)
-        logits[...] = lax.dot_general(w_mean[at, :], hidden[...], DN_T, preferred_element_type=F32)
+        step = sizes[p]
+        at = pl.ds(starts[p], step)
+        logits[0:step, :] = lax.dot_general(w_mean[at, :], hidden[...], DN_T, preferred_element_type=F32)
         lane = lax.broadcasted_iota(jnp.int32, (step, 3 * panel_count), 1)
         pick = (panel_col[at, 0:1] == lax.rem(lane, panel_count).astype(F32)).astype(F32).astype(BF16)
-        thetas[...] = jnp.dot(pick, tables, preferred_element_type=F32)
+        thetas[0:step, :] = jnp.dot(pick, tables, preferred_element_type=F32)
 
         def chunk(i, lost):
             rows = pl.ds(pl.multiple_of(i * few, few), few)
-            there = pl.ds(pl.multiple_of(p * step + i * few, few), few)
+            there = pl.ds(pl.multiple_of(starts[p] + i * few, few), few)
             nll, d_logit, d_theta = terms(
                 counts[there, :].astype(F32), thetas[rows, :], logits[rows, :], rate_scale, norm_scale, 12
             )
@@ -977,7 +979,7 @@
             return lost + jnp.sum(nll, axis=0, keepdims=True)
 
         loss[...] += lax.fori_loop(0, step // few, chunk, jnp.zeros_like(loss))
-        d_theta = thetas[...]
+        d_theta = thetas[0:step, :]
         if p < parts - 1:
             field_gather[p].start()
         row = lax.broadcasted_iota(jnp.int32, (step, 128), 1)
@@ -1037,7 +1039,7 @@
 
     def gradient_of(p):
         field_gather[p].finish()
-        gradient[pl.ds(p * step, step), :] = contract(pl.ds(p * step, step), step)
+        gradient[pl.ds(starts[p], sizes[p]), :] = contract(pl.ds(starts[p], sizes[p]), sizes[p])
 
     gradient_of(0)
     gradient_of(1)
@@ -1109,8 +1111,8 @@
             pltpu.VMEM((128, cells), F32),
             pltpu.VMEM((1, cells), F32),
             pltpu.VMEM((genes, 128), F32),
-            pltpu.VMEM((genes // 4, cells), F32),
-            pltpu.VMEM((genes // 4, cells), F32),
+            pltpu.VMEM((genes * 6 // 20, cells), F32),
+            pltpu.VMEM((genes * 6 // 20, cells), F32),
             pltpu.SemaphoreType.DMA((2,)),
         ] + swap_sems + [
             pltpu.SemaphoreType.DMA((NR,)),

time: 159 us -> 159 us (level)
  no operation moved by 1% of the time
where the time goes in v9:
time: 159 us
  Pallas kernels  158 us (99%)
    pallas_call x1, Pallas kernels, shards(): pl.pallas_call(functools.partial(network_kernel, head, genes_all, cells_a...  155 us

profile of v9, /device:TPU:1, one launch (start us, length us, event | category | flops | bytes accessed | tf_op | source)
XLA Modules:
  0.0 158.7 jit_solution(14759292574683403828)
XLA Ops:
  0.6 155.3 %network.1 = (f32[1,256]{1,0:T(1,128)}, f32[960,256]{1,0:T(8,128)}, f32[8,64,256]{2,1,0:T(8,128)}) custom-call(s32[960,256]{1,0:T(8,128)} %bitcast.13, s32[1,256]{1,0:T(1,128)} %groups.1, bf16[960,6400]{1,0:T(8,128)(2,1)} %w_hbm.1, bf16[150,2,1600]{2,1,0:T(2,128)(2,1)} %bitcast.11, bf16[150,2,1600]{2,1,0:T(2,128)(2,1)} %bitcast.12, ...), custom_call_target="tpu_custom_call" | custom-call | tf_op jit(solution)/shard_map/network/pallas_call | solution.py:1090
  156.0 2.7 %finish.1 = (f32[1,256]{1,0:T(1,128)}, f32[200,960]{1,0:T(8,128)}, f32[64,1600]{1,0:T(8,128)}) custom-call(f32[960,256]{1,0:T(8,128)} %get-tuple-element.9.gradient, f32[8,64,256]{2,1,0:T(8,128)} %get-tuple-element.10.disp_block, f32[1,256]{1,0:T(1,128)} %get-tuple-element.11.loss), custom_call_target="tpu_custom_call" | custom-call | tf_op jit(solution)/shard_map/finish/pallas_call | solution.py:1133
